TPU v7x, 256 devices: a whole 4x4x8 slice. The times are simulated.
256 devices in a mesh: section: 2 (over core), blk: 128 (over z, x, y).
Axes of the slice: x: 4, y: 4, z: 8, core: 2. Of those that a mesh axis runs over, the one named last changes fastest.
Arguments:
- hidden: bfloat16 [2, 384, 3072], P(None, 'blk'), may hold values from -4 to 4
- qkv_weight: bfloat16 [2, 3072, 9216], P('section', None, 'blk'), may hold values from -0.109375 to 0.109375
- out_weight: bfloat16 [2, 3072, 3072], P('section', None, 'blk'), may hold values from -0.109375 to 0.109375
- modulation: float32 [2, 50, 3, 3072], P('section'), may hold values from -3 to 3
- timestep: int32 [1], replicated, may hold values from 0 to 49
- fresh: int32 [2, 2, 128], P('section'), may hold values 0 or 1
- live: int32 [2, 128], replicated, may hold values from 0 to 1, as said below
- k_stale: bfloat16 [2, 2, 384, 3072], P('section', None, 'blk'), may hold values from -6 to 6
- v_stale: bfloat16 [2, 2, 384, 3072], P('section', None, 'blk'), may hold values from -16 to 16
Outputs:
- layer_outputs: bfloat16 [2, 2, 384, 3072], P('section', None, 'blk')
Inputs may be any that keep to these rules, and one draw needn't show every extreme that they name: Block 0 of every request is live.
All inputs are finite; a program needn't handle non-finite values. No bound on the sum of `fresh` on one device may be relied on, other than what follows from the above.
Results may differ from a plain program's by a relative error of at most 0.017.
Values may be sent and summed in bfloat16 or wider, within the bound.
A program may use at most 64 MiB of HBM per device.

v0:
```python
import jax
import jax.numpy as jnp
from jax import lax
from jax.sharding import PartitionSpec as P


def from_behind(shard, axis, by):
    count = lax.axis_size(axis)
    pairs = [(i, i + by) for i in range(count) if 0 <= i + by < count]
    return lax.ppermute(shard, axis, pairs)


def attend(layer_in, qkv_cols, out_cols, modulate, fresh_own, old_keys, old_values, live):
    stream = layer_in.astype(jnp.float32)
    center = jnp.mean(stream, axis=-1, keepdims=True)
    variance = jnp.mean((stream - center) ** 2, axis=-1, keepdims=True)
    normed = (stream - center) / jnp.sqrt(variance + 1e-06) * (1.0 + modulate[0]) + modulate[1]
    normed_b = normed.astype(jnp.bfloat16)
    columns = jnp.einsum(
        "rnd,dc->rnc",
        lax.all_gather(normed_b, "blk", axis=1, tiled=True),
        qkv_cols,
        preferred_element_type=jnp.float32,
    ).astype(jnp.bfloat16)
    projected = lax.all_to_all(columns, "blk", split_axis=1, concat_axis=2, tiled=True)
    num_req, num_rows, width = layer_in.shape
    queries = projected[:, :, :width]
    new_keys = projected[:, :, width : 2 * width]
    new_values = projected[:, :, 2 * width :]
    use_fresh = (fresh_own == 1)[:, None, None]
    keys = jnp.where(use_fresh, new_keys, old_keys)
    values = jnp.where(use_fresh, new_values, old_values)
    num_heads = width // 64
    num_blocks = live.shape[1]
    q_heads = queries.reshape(num_req, num_rows, num_heads, 64)
    live_float = live.astype(jnp.float32)
    run_max = jnp.full((num_req, num_heads, num_rows), -1e30, jnp.float32)
    key_piece = lax.all_gather(keys, "blk", axis=1, tiled=True)
    value_piece = lax.all_gather(values, "blk", axis=1, tiled=True)
    piece_rows = key_piece.shape[1]
    key_heads = key_piece.reshape(num_req, piece_rows, num_heads, 64)
    value_heads = value_piece.reshape(num_req, piece_rows, num_heads, 64)
    scores = (
        jnp.einsum("qrhd,qnhd->qhrn", q_heads, key_heads, preferred_element_type=jnp.float32)
        * 0.125
    )
    block_ids = jnp.arange(piece_rows) // num_rows
    one_hot = (block_ids[:, None] == jnp.arange(num_blocks)[None, :]).astype(jnp.float32)
    usable = jnp.einsum("qb,nb->qn", live_float, one_hot) > 0.5
    usable = usable[:, None, None, :]
    scores = jnp.where(usable, scores, -1e30)
    new_max = jnp.maximum(run_max, jnp.max(scores, axis=-1))
    weights = jnp.where(usable, jnp.exp(scores - new_max[..., None]), 0.0)
    new_sum = jnp.sum(weights, axis=-1)
    new_acc = jnp.einsum(
        "qhrn,qnhd->qhrd", weights, value_heads.astype(jnp.float32), precision=lax.Precision.HIGHEST
    )
    attn = new_acc / new_sum[..., None]
    attn = jnp.transpose(attn, (0, 2, 1, 3)).reshape(num_req, num_rows, width).astype(jnp.bfloat16)
    out_part = jnp.einsum(
        "rnd,dc->rnc",
        lax.all_gather(attn, "blk", axis=1, tiled=True),
        out_cols,
        preferred_element_type=jnp.float32,
    ).astype(jnp.bfloat16)
    mixed_back = lax.all_to_all(out_part, "blk", split_axis=1, concat_axis=2, tiled=True)
    return (stream + modulate[2] * mixed_back.astype(jnp.float32)).astype(jnp.bfloat16)


def pick_request(array, req_idx):
    return lax.dynamic_index_in_dim(array, req_idx, 0, keepdims=True)


def per_device(hidden, qkv_weight, out_weight, modulation, timestep, fresh, live, k_stale, v_stale):
    section_idx = lax.axis_index("section")
    block_idx = lax.axis_index("blk")
    steps_all = modulation.shape[1]
    pick_row = (jnp.arange(steps_all) == timestep[0]).astype(jnp.float32)
    modulate = jnp.einsum("t,tcd->cd", pick_row, modulation[0], precision=lax.Precision.HIGHEST)
    num_blocks = fresh.shape[2]
    own_column = (jnp.arange(num_blocks) == block_idx).astype(jnp.int32)
    fresh_own = jnp.sum(fresh[0] * own_column[None, :], axis=1)
    qkv_cols = qkv_weight[0]
    out_cols = out_weight[0]
    old_keys = k_stale[0]
    old_values = v_stale[0]
    num_req = hidden.shape[0]
    received = jnp.zeros_like(hidden[0:1])
    first_out = []
    second_out = []
    for tick_idx in range(num_req + 1):
        if tick_idx < num_req:
            own_input = hidden[tick_idx : tick_idx + 1]
        else:
            own_input = jnp.zeros_like(hidden[0:1])
        layer_in = jnp.where(section_idx == 0, own_input, received)
        req_idx = jnp.clip(tick_idx - section_idx, 0, num_req - 1)
        layer_out = attend(
            layer_in,
            qkv_cols,
            out_cols,
            modulate,
            pick_request(fresh_own, req_idx),
            pick_request(old_keys, req_idx),
            pick_request(old_values, req_idx),
            pick_request(live, req_idx),
        )
        if tick_idx < num_req:
            first_out.append(layer_out)
            received = from_behind(layer_out, "section", 1)
        if tick_idx >= 1:
            second_out.append(layer_out)
    result = jnp.where(
        section_idx == 0, jnp.concatenate(first_out, axis=0), jnp.concatenate(second_out, axis=0)
    )
    return result[None]


def solution(mesh):
    return jax.shard_map(
        per_device,
        mesh=mesh,
        in_specs=(
            P(None, "blk", None),
            P("section", None, "blk"),
            P("section", None, "blk"),
            P("section", None, None, None),
            P(),
            P("section", None, None),
            P(),
            P("section", None, "blk", None),
            P("section", None, "blk", None),
        ),
        out_specs=P("section", None, "blk", None),
        check_vma=False,
    )
```

profile of v0, /device:TPU:1, one launch (start us, length us, event | category | flops | bytes accessed | tf_op | source)
XLA Modules:
  0.0 1594.2 jit_solution(17317601868942555664)
XLA Ops:
  12.8 117.6 %all-gather.13.cloned.1.call-done = bf16[1,384,3072]{2,0,1:T(2,128)(2,1)} async-done(((bf16[1,3,3072]{2,0,1:T(2,128)(2,1)}), bf16[1,384,3072]{2,0,1:T(2,128)(2,1)}) %all-gather.13.cloned.1.call-update) | async-done | bytes 2359312 | tf_op jit(solution)/shard_map/all_gather | solution.py:21
  145.2 10.5 all-to-all-done
  158.5 110.3 %all-gather.15.cloned.1.call-done = bf16[1,384,3072]{2,0,1:T(2,128)(2,1)} async-done(((bf16[1,3,3072]{2,0,1:T(2,128)(2,1)}), bf16[1,384,3072]{2,0,1:T(2,128)(2,1)}) %all-gather.15.cloned.1.call-update) | async-done | bytes 2359312 | tf_op jit(solution)/shard_map/all_gather | solution.py:38
  268.8 10.0 copy.113
  279.7 107.0 %all-gather.17.cloned.1.call-done = bf16[1,384,3072]{2,0,1:T(2,128)(2,1)} async-done(((bf16[1,3,3072]{2,0,1:T(2,128)(2,1)}), bf16[1,384,3072]{2,0,1:T(2,128)(2,1)}) %all-gather.17.cloned.1.call-update) | async-done | bytes 2359312 | tf_op jit(solution)/shard_map/all_gather | solution.py:39
  386.6 10.0 copy.116
  400.0 114.2 %all-gather.19.cloned.1.call-done = bf16[1,384,3072]{2,0,1:T(2,128)(2,1)} async-done(((bf16[1,3,3072]{2,0,1:T(2,128)(2,1)}), bf16[1,384,3072]{2,0,1:T(2,128)(2,1)}) %all-gather.19.cloned.1.call-update) | async-done | bytes 2359312 | tf_op jit(solution)/shard_map/all_gather | solution.py:62
  517.5 21.0 %all_to_all.81 = bf16[1,384,24]{2,0,1:T(2,128)(2,1)S(1)} all-to-all(bf16[1,384,24]{2,0,1:T(2,128)(2,1)S(1)} %copy.119), channel_id=1, replica_groups=mesh['section'=2,'blk'=128] {'blk'}, dimensions={1} | all-to-all | bytes 36864 | tf_op jit(solution)/shard_map/all_to_all | solution.py:66
  547.5 106.3 %all-gather.21.cloned.1.call-done = bf16[1,384,3072]{2,0,1:T(2,128)(2,1)} async-done(((bf16[1,3,3072]{2,0,1:T(2,128)(2,1)}), bf16[1,384,3072]{2,0,1:T(2,128)(2,1)}) %all-gather.21.cloned.1.call-update) | async-done | bytes 2359312 | tf_op jit(solution)/shard_map/all_gather | solution.py:21
  667.8 11.3 all-to-all-done.2
  681.9 110.3 %all-gather.23.cloned.1.call-done = bf16[1,384,3072]{2,0,1:T(2,128)(2,1)} async-done(((bf16[1,3,3072]{2,0,1:T(2,128)(2,1)}), bf16[1,384,3072]{2,0,1:T(2,128)(2,1)}) %all-gather.23.cloned.1.call-update) | async-done | bytes 2359312 | tf_op jit(solution)/shard_map/all_gather | solution.py:38
  792.2 10.0 copy.124
  803.1 106.9 %all-gather.25.cloned.1.call-done = bf16[1,384,3072]{2,0,1:T(2,128)(2,1)} async-done(((bf16[1,3,3072]{2,0,1:T(2,128)(2,1)}), bf16[1,384,3072]{2,0,1:T(2,128)(2,1)}) %all-gather.25.cloned.1.call-update) | async-done | bytes 2359312 | tf_op jit(solution)/shard_map/all_gather | solution.py:39
  910.0 10.0 copy.127
  923.4 114.2 %all-gather.27.cloned.1.call-done = bf16[1,384,3072]{2,0,1:T(2,128)(2,1)} async-done(((bf16[1,3,3072]{2,0,1:T(2,128)(2,1)}), bf16[1,384,3072]{2,0,1:T(2,128)(2,1)}) %all-gather.27.cloned.1.call-update) | async-done | bytes 2359312 | tf_op jit(solution)/shard_map/all_gather | solution.py:62
  1040.9 21.0 %all_to_all.82 = bf16[1,384,24]{2,0,1:T(2,128)(2,1)S(1)} all-to-all(bf16[1,384,24]{2,0,1:T(2,128)(2,1)S(1)} %copy.130), channel_id=1, replica_groups=mesh['section'=2,'blk'=128] {'blk'}, dimensions={1} | all-to-all | bytes 36864 | tf_op jit(solution)/shard_map/all_to_all | solution.py:66
  1070.8 106.3 %all-gather.29.cloned.1.call-done = bf16[1,384,3072]{2,0,1:T(2,128)(2,1)} async-done(((bf16[1,3,3072]{2,0,1:T(2,128)(2,1)}), bf16[1,384,3072]{2,0,1:T(2,128)(2,1)}) %all-gather.29.cloned.1.call-update) | async-done | bytes 2359312 | tf_op jit(solution)/shard_map/all_gather | solution.py:21
  1191.2 11.3 all-to-all-done.4
  1205.2 110.3 %all-gather.31.cloned.1.call-done = bf16[1,384,3072]{2,0,1:T(2,128)(2,1)} async-done(((bf16[1,3,3072]{2,0,1:T(2,128)(2,1)}), bf16[1,384,3072]{2,0,1:T(2,128)(2,1)}) %all-gather.31.cloned.1.call-update) | async-done | bytes 2359312 | tf_op jit(solution)/shard_map/all_gather | solution.py:38
  1315.6 10.0 copy.135
  1326.4 107.0 %all-gather.33.cloned.1.call-done = bf16[1,384,3072]{2,0,1:T(2,128)(2,1)} async-done(((bf16[1,3,3072]{2,0,1:T(2,128)(2,1)}), bf16[1,384,3072]{2,0,1:T(2,128)(2,1)}) %all-gather.33.cloned.1.call-update) | async-done | bytes 2359312 | tf_op jit(solution)/shard_map/all_gather | solution.py:39
  1433.4 10.0 copy.138
  1446.7 114.2 %all-gather.35.cloned.1.call-done = bf16[1,384,3072]{2,0,1:T(2,128)(2,1)} async-done(((bf16[1,3,3072]{2,0,1:T(2,128)(2,1)}), bf16[1,384,3072]{2,0,1:T(2,128)(2,1)}) %all-gather.35.cloned.1.call-update) | async-done | bytes 2359312 | tf_op jit(solution)/shard_map/all_gather | solution.py:62
  1574.2 11.9 all-to-all-done.5
  (146 shorter events, 106.2 us)
Async XLA Ops:
  6.5 123.9 %copy-start = (bf16[1,3072,72]{1,2,0:T(8,128)(2,1)S(1)}, bf16[1,3072,72]{1,2,0:T(8,128)(2,1)}, u32[]{:S(2)}) copy-start(bf16[1,3072,72]{1,2,0:T(8,128)(2,1)} %param.10) | copy-start | bytes 1327108
  6.5 6.0 copy-start.3
  6.5 6.0 copy-start.2
  6.5 123.9 %all-gather.13.cloned.1.call-start = ((), (), s32[]{:S(2)}) async-start(), calls=%async_computation.6 | async-start | bytes 4755456 | tf_op jit(solution)/shard_map/all_gather | solution.py:21
  12.5 131.4 %copy-start.4 = (s32[1,2,128]{2,1,0:T(2,128)S(1)}, s32[1,2,128]{2,1,0:T(2,128)}, u32[]{:S(2)}) copy-start(s32[1,2,128]{2,1,0:T(2,128)} %param.14) | copy-start | bytes 3076
  12.8 145.4 %copy-start.6 = (s32[2,128]{1,0:T(2,128)S(1)}, s32[2,128]{1,0:T(2,128)}, u32[]{:S(2)}) copy-start(s32[2,128]{1,0:T(2,128)} %param.15) | copy-start | bytes 3076
  134.5 21.2 %all-to-all-start = ((bf16[1,384,72]{2,0,1:T(2,128)(2,1)}), bf16[1,384,72]{2,0,1:T(2,128)(2,1)S(1)}, u32[]{:S(2)}, u32[]{:S(2)}) async-start(bf16[1,384,72]{2,0,1:T(2,128)(2,1)} %copy.110), calls=%async_computation | async-start | bytes 393216 | tf_op jit(solution)/shard_map/all_to_all | solution.py:25
  143.8 125.0 %all-gather.15.cloned.1.call-start = ((), (), s32[]{:S(2)}) async-start(), calls=%async_computation.7 | async-start | bytes 4755456 | tf_op jit(solution)/shard_map/all_gather | solution.py:38
  157.3 229.3 %all-gather.17.cloned.1.call-start = ((), (), s32[]{:S(2)}) async-start(), calls=%async_computation.8 | async-start | bytes 4755456 | tf_op jit(solution)/shard_map/all_gather | solution.py:39
  158.1 356.1 %all-gather.19.cloned.1.call-start = ((), (), s32[]{:S(2)}) async-start(), calls=%async_computation.9 | async-start | bytes 4755456 | tf_op jit(solution)/shard_map/all_gather | solution.py:62
  396.6 117.6 %copy-start.5 = (bf16[1,3072,24]{1,2,0:T(8,128)(2,1)S(1)}, bf16[1,3072,24]{1,2,0:T(8,128)(2,1)}, u32[]{:S(2)}) copy-start(bf16[1,3072,24]{1,2,0:T(8,128)(2,1)} %param.11) | copy-start | bytes 442372
  400.0 253.9 %all-gather.21.cloned.1.call-start = ((), (), s32[]{:S(2)}) async-start(), calls=%async_computation.10 | async-start | bytes 4755456 | tf_op jit(solution)/shard_map/all_gather | solution.py:21
  539.0 7.4 collective-permute-start
  657.9 21.2 %all-to-all-start.2 = ((bf16[1,384,72]{2,0,1:T(2,128)(2,1)}), bf16[1,384,72]{2,0,1:T(2,128)(2,1)S(1)}, u32[]{:S(2)}, u32[]{:S(2)}) async-start(bf16[1,384,72]{2,0,1:T(2,128)(2,1)} %copy.121), calls=%async_computation.2 | async-start | bytes 393216 | tf_op jit(solution)/shard_map/all_to_all | solution.py:25
  667.2 125.0 %all-gather.23.cloned.1.call-start = ((), (), s32[]{:S(2)}) async-start(), calls=%async_computation.11 | async-start | bytes 4755456 | tf_op jit(solution)/shard_map/all_gather | solution.py:38
  680.7 229.3 %all-gather.25.cloned.1.call-start = ((), (), s32[]{:S(2)}) async-start(), calls=%async_computation.12 | async-start | bytes 4755456 | tf_op jit(solution)/shard_map/all_gather | solution.py:39
  681.5 356.1 %all-gather.27.cloned.1.call-start = ((), (), s32[]{:S(2)}) async-start(), calls=%async_computation.13 | async-start | bytes 4755456 | tf_op jit(solution)/shard_map/all_gather | solution.py:62
  923.3 253.8 %all-gather.29.cloned.1.call-start = ((), (), s32[]{:S(2)}) async-start(), calls=%async_computation.14 | async-start | bytes 4755456 | tf_op jit(solution)/shard_map/all_gather | solution.py:21
  1062.3 7.3 collective-permute-start.1
  1181.2 21.2 %all-to-all-start.4 = ((bf16[1,384,72]{2,0,1:T(2,128)(2,1)}), bf16[1,384,72]{2,0,1:T(2,128)(2,1)S(1)}, u32[]{:S(2)}, u32[]{:S(2)}) async-start(bf16[1,384,72]{2,0,1:T(2,128)(2,1)} %copy.132), calls=%async_computation.4 | async-start | bytes 393216 | tf_op jit(solution)/shard_map/all_to_all | solution.py:25
  1190.5 125.0 %all-gather.31.cloned.1.call-start = ((), (), s32[]{:S(2)}) async-start(), calls=%async_computation.15 | async-start | bytes 4755456 | tf_op jit(solution)/shard_map/all_gather | solution.py:38
  1204.1 229.3 %all-gather.33.cloned.1.call-start = ((), (), s32[]{:S(2)}) async-start(), calls=%async_computation.16 | async-start | bytes 4755456 | tf_op jit(solution)/shard_map/all_gather | solution.py:39
  1204.8 356.1 %all-gather.35.cloned.1.call-start = ((), (), s32[]{:S(2)}) async-start(), calls=%async_computation.17 | async-start | bytes 4755456 | tf_op jit(solution)/shard_map/all_gather | solution.py:62
  1564.9 21.2 %all-to-all-start.5 = ((bf16[1,384,24]{2,0,1:T(2,128)(2,1)}), bf16[1,384,24]{2,0,1:T(2,128)(2,1)S(1)}, u32[]{:S(2)}, u32[]{:S(2)}) async-start(bf16[1,384,24]{2,0,1:T(2,128)(2,1)} %copy.141), calls=%async_computation.5 | async-start | bytes 393216 | tf_op jit(solution)/shard_map/all_to_all | solution.py:66
  (1 other events, 5.1 us)
Sparse Core Ops, SparseCore 0:
  12.6 117.7 all-gather.12
  157.5 111.3 all-gather.14
  272.5 114.0 all-gather.16
  400.1 114.0 all-gather.18
  547.7 106.1 all-gather.20
  680.9 111.3 all-gather.22
  795.9 114.0 all-gather.24
  923.5 114.0 all-gather.26
  1070.9 106.1 all-gather.28
  1204.2 111.3 all-gather.30
  1319.2 114.0 all-gather.32
  1446.8 114.0 all-gather.34
where the time goes:
time: 1600 us; the launch traced here: 1590 us
  waiting for transfers between devices  1380 us (86%)
  local copies, waits for them, and re-layouts  72.8 us (5%)
  blocking collectives  42 us (3%)
  starting transfers between devices  40.5 us (3%)
  matrix products  31.8 us (2%)
  between operations  16.6 us (1%)
    all_gather x3, waiting for transfers between devices, attend(): lax.all_gather(attn, 'blk', axis=1, tiled=True)  343 us
    all_gather x3, waiting for transfers between devices, attend(): key_piece = lax.all_gather(keys, 'blk', axis=1, tiled=True)  331 us
    all_gather x3, waiting for transfers between devices, attend(): lax.all_gather(normed_b, 'blk', axis=1, tiled=True)  330 us
    all_gather x3, waiting for transfers between devices, attend(): value_piece = lax.all_gather(values, 'blk', axis=1, tiled=True)  321 us
    all_to_all x2, blocking collectives, attend(): lax.all_to_all(out_part, 'blk', split_axis=1, concat_axis=2, tiled=True)  42 us
    all_to_all x3, waiting for transfers between devices, attend(): lax.all_to_all(columns, 'blk', split_axis=1, concat_axis=2, tiled=True)  33.1 us
  transfers between devices with their start and end apart: 18, of which 18 were waited for; matrix products, arithmetic and copies ran while one was open for 2% of the time, Pallas kernels for 0%

commit v1 on v0

--- a/solution.py
+++ b/solution.py
@@ -1,7 +1,83 @@
+import functools
+
 import jax
 import jax.numpy as jnp
 from jax import lax
+from jax.experimental import pallas as pl
+from jax.experimental.pallas import tpu as pltpu
 from jax.sharding import PartitionSpec as P
+
+MESH = pl.DeviceIdType.MESH
+
+
+def gather_kernel(n, x_ref, o_ref, send_sem, recv_sem, local_sem):
+    me = lax.axis_index("blk")
+    sec = lax.axis_index("section")
+    barrier = pltpu.get_barrier_semaphore()
+
+    def greet(i, carry):
+        peer = lax.rem(me + 1 + i, n)
+        pl.semaphore_signal(barrier, inc=1, device_id=(sec, peer), device_id_type=MESH)
+        return carry
+
+    lax.fori_loop(0, n - 1, greet, 0)
+    pl.semaphore_wait(barrier, n - 1)
+    local = pltpu.make_async_copy(x_ref, o_ref.at[me], local_sem)
+    local.start()
+
+    def remote(i):
+        peer = lax.rem(me + 1 + i, n)
+        return pltpu.make_async_remote_copy(
+            src_ref=x_ref,
+            dst_ref=o_ref.at[me],
+            send_sem=send_sem.at[i],
+            recv_sem=recv_sem.at[me],
+            device_id=(sec, peer),
+            device_id_type=MESH,
+        )
+
+    def send(i, carry):
+        remote(i).start()
+        return carry
+
+    lax.fori_loop(0, n - 1, send, 0)
+
+    def finish(i, carry):
+        remote(i).wait_send()
+        src = lax.rem(me + n - 1 - i, n)
+        pltpu.make_async_remote_copy(
+            src_ref=x_ref,
+            dst_ref=o_ref.at[src],
+            send_sem=send_sem.at[i],
+            recv_sem=recv_sem.at[src],
+            device_id=(sec, src),
+            device_id_type=MESH,
+        ).wait_recv()
+        return carry
+
+    lax.fori_loop(0, n - 1, finish, 0)
+    local.wait()
+
+
+def gather_blk(x, n, cid):
+    return pl.pallas_call(
+        functools.partial(gather_kernel, n),
+        out_shape=jax.ShapeDtypeStruct((n,) + x.shape, x.dtype),
+        in_specs=[pl.BlockSpec(memory_space=pl.ANY)],
+        out_specs=pl.BlockSpec(memory_space=pl.ANY),
+        scratch_shapes=[
+            pltpu.SemaphoreType.DMA((n,)),
+            pltpu.SemaphoreType.DMA((n,)),
+            pltpu.SemaphoreType.DMA,
+        ],
+        compiler_params=pltpu.CompilerParams(collective_id=cid, has_side_effects=True),
+    )(x)
+
+
+def gather_rows(x, cid):
+    n = lax.axis_size("blk")
+    _, rows, width = x.shape
+    return gather_blk(x[0], n, cid).reshape(1, n * rows, width)
 
 
 def from_behind(shard, axis, by):
@@ -18,7 +94,7 @@
     normed_b = normed.astype(jnp.bfloat16)
     columns = jnp.einsum(
         "rnd,dc->rnc",
-        lax.all_gather(normed_b, "blk", axis=1, tiled=True),
+        gather_rows(normed_b, 0),
         qkv_cols,
         preferred_element_type=jnp.float32,
     ).astype(jnp.bfloat16)
@@ -35,8 +111,9 @@
     q_heads = queries.reshape(num_req, num_rows, num_heads, 64)
     live_float = live.astype(jnp.float32)
     run_max = jnp.full((num_req, num_heads, num_rows), -1e30, jnp.float32)
-    key_piece = lax.all_gather(keys, "blk", axis=1, tiled=True)
-    value_piece = lax.all_gather(values, "blk", axis=1, tiled=True)
+    kv_piece = gather_rows(jnp.concatenate([keys, values], axis=2), 1)
+    key_piece = kv_piece[:, :, :width]
+    value_piece = kv_piece[:, :, width:]
     piece_rows = key_piece.shape[1]
     key_heads = key_piece.reshape(num_req, piece_rows, num_heads, 64)
     value_heads = value_piece.reshape(num_req, piece_rows, num_heads, 64)
@@ -59,7 +136,7 @@
     attn = jnp.transpose(attn, (0, 2, 1, 3)).reshape(num_req, num_rows, width).astype(jnp.bfloat16)
     out_part = jnp.einsum(
         "rnd,dc->rnc",
-        lax.all_gather(attn, "blk", axis=1, tiled=True),
+        gather_rows(attn, 0),
         out_cols,
         preferred_element_type=jnp.float32,
     ).astype(jnp.bfloat16)

time: 1600 us -> 1320 us (0.82)
  waiting for transfers between devices: 1380 us -> 39.6 us
  Pallas kernels: 0 us -> 988 us
  blocking collectives: 42 us -> 81.2 us
  local copies, waits for them, and re-layouts: 72.8 us -> 111 us
  starting transfers between devices: 40.5 us -> 59.4 us
    all_gather x12 -> x0, waiting for transfers between devices: 1320 us -> none  [the longest x3 343 us: attend(): lax.all_gather(attn, 'blk', axis=1, tiled=True)]
    pallas_call x0 -> x9, Pallas kernels: none -> 988 us  [gather_blk(): pl.pallas_call(functools.partial(gather_kernel, n), out_shape=jax.ShapeDt...]
    all_gather x6 -> x0, local copies, waits for them, and re-layouts: 59.8 us -> none  [the longest x3 29.9 us: attend(): key_piece = lax.all_gather(keys, 'blk', axis=1, tiled=True)]
    all_to_all x2 -> x3, blocking collectives: 42 us -> 81.2 us  [attend(): lax.all_to_all(out_part, 'blk', split_axis=1, concat_axis=2, tiled=True)]
    reshape x0 -> x3, local copies, waits for them, and re-layouts: none -> 37.2 us  [gather_rows(): return gather_blk(x[0], n, cid).reshape(1, n * rows, width)]
    slice x0 -> x10, local copies, waits for them, and re-layouts: none -> 33.4 us  [the longest x6 23.4 us: attend(): key_piece = kv_piece[:, :, :width]]
    another operation x3 -> x9, local copies, waits for them, and re-layouts: 0.29 us -> 32.3 us
    all_to_all x3, starting transfers between devices: 27.9 us -> 56.6 us  [attend(): lax.all_to_all(columns, 'blk', split_axis=1, concat_axis=2, tiled=True)]
  transfers between devices with their start and end apart: 18 -> 5, of which waited for: 18 -> 5; matrix products, arithmetic and copies ran while one was open for 2% -> 0% of each run, Pallas kernels for 0% -> 0%
where the time goes in v1:
time: 1320 us; the launch traced here: 1310 us
  Pallas kernels  988 us (75%)
  local copies, waits for them, and re-layouts  111 us (8%)
  blocking collectives  81.2 us (6%)
  starting transfers between devices  59.4 us (4%)
  waiting for transfers between devices  39.6 us (3%)
  matrix products  17.5 us (1%)
    pallas_call x9, Pallas kernels, gather_blk(): pl.pallas_call(functools.partial(gather_kernel, n), out_shape=jax.ShapeDt...  988 us
    all_to_all x3, blocking collectives, attend(): lax.all_to_all(out_part, 'blk', split_axis=1, concat_axis=2, tiled=True)  81.2 us
    all_to_all x3, starting transfers between devices, attend(): lax.all_to_all(columns, 'blk', split_axis=1, concat_axis=2, tiled=True)  56.6 us
    reshape x3, local copies, waits for them, and re-layouts, gather_rows(): return gather_blk(x[0], n, cid).reshape(1, n * rows, width)  37.2 us
    all_to_all x3, waiting for transfers between devices, attend(): lax.all_to_all(columns, 'blk', split_axis=1, concat_axis=2, tiled=True)  32.8 us
    another operation x9, local copies, waits for them, and re-layouts  32.3 us
  transfers between devices with their start and end apart: 5, of which 5 were waited for; matrix products, arithmetic and copies ran while one was open for 0% of the time, Pallas kernels for 0%

profile of v1, /device:TPU:1, one launch (start us, length us, event | category | flops | bytes accessed | tf_op | source)
XLA Modules:
  0.0 1308.3 jit_solution(12684976163807597393)
XLA Ops:
  5.1 87.8 %shard_map.91 = bf16[128,3,3072]{2,1,0:T(4,128)(2,1)} custom-call(bf16[3,3072]{1,0:T(4,128)(2,1)} %fusion.66.x_ref), custom_call_target="tpu_custom_call" | custom-call | tf_op jit(solution)/shard_map/pallas_call | solution.py:63
  92.9 5.3 reshape.518
  100.0 14.4 %all-to-all-start = ((bf16[1,384,72]{2,0,1:T(2,128)(2,1)}), bf16[1,384,72]{2,0,1:T(2,128)(2,1)S(1)}, u32[]{:S(2)}, u32[]{:S(2)}) async-start(bf16[1,384,72]{2,0,1:T(2,128)(2,1)} %copy.92), calls=%async_computation | async-start | bytes 393216 | tf_op jit(solution)/shard_map/all_to_all | solution.py:101
  116.4 10.0 all-to-all-done
  127.9 149.7 %shard_map.92 = bf16[128,3,6144]{2,1,0:T(4,128)(2,1)} custom-call(bf16[3,6144]{1,0:T(4,128)(2,1)} %maximum_bitcast_fusion.x_ref), custom_call_target="tpu_custom_call" | custom-call | tf_op jit(solution)/shard_map/pallas_call | solution.py:63
  277.7 12.4 reshape.520
  305.2 99.9 %shard_map.93 = bf16[128,3,3072]{2,1,0:T(4,128)(2,1)} custom-call(bf16[3,3072]{1,0:T(4,128)(2,1)} %convert_element_type.200.x_ref), custom_call_target="tpu_custom_call" | custom-call | tf_op jit(solution)/shard_map/pallas_call | solution.py:63
  405.1 5.4 reshape.523
  411.4 27.2 %all_to_all.81 = bf16[1,384,24]{2,0,1:T(2,128)(2,1)S(1)} all-to-all(bf16[1,384,24]{2,0,1:T(2,128)(2,1)S(1)} %copy.98), channel_id=1, replica_groups=mesh['section'=2,'blk'=128] {'blk'}, dimensions={1} | all-to-all | bytes 36864 | tf_op jit(solution)/shard_map/all_to_all | solution.py:143
  445.2 75.9 %shard_map.94 = bf16[128,3,3072]{2,1,0:T(4,128)(2,1)} custom-call(bf16[3,3072]{1,0:T(4,128)(2,1)} %fusion.65.x_ref), custom_call_target="tpu_custom_call" | custom-call | tf_op jit(solution)/shard_map/pallas_call | solution.py:63
  521.2 5.3 reshape.525
  528.2 22.7 %all-to-all-start.2 = ((bf16[1,384,72]{2,0,1:T(2,128)(2,1)}), bf16[1,384,72]{2,0,1:T(2,128)(2,1)S(1)}, u32[]{:S(2)}, u32[]{:S(2)}) async-start(bf16[1,384,72]{2,0,1:T(2,128)(2,1)} %copy.102), calls=%async_computation.2 | async-start | bytes 393216 | tf_op jit(solution)/shard_map/all_to_all | solution.py:101
  551.5 11.5 all-to-all-done.2
  564.6 147.8 %shard_map.95 = bf16[128,3,6144]{2,1,0:T(4,128)(2,1)} custom-call(bf16[3,6144]{1,0:T(4,128)(2,1)} %maximum_bitcast_fusion.1.x_ref), custom_call_target="tpu_custom_call" | custom-call | tf_op jit(solution)/shard_map/pallas_call | solution.py:63
  712.4 12.4 reshape.527
  739.9 101.0 %shard_map.96 = bf16[128,3,3072]{2,1,0:T(4,128)(2,1)} custom-call(bf16[3,3072]{1,0:T(4,128)(2,1)} %convert_element_type.216.x_ref), custom_call_target="tpu_custom_call" | custom-call | tf_op jit(solution)/shard_map/pallas_call | solution.py:63
  847.1 27.0 %all_to_all.82 = bf16[1,384,24]{2,0,1:T(2,128)(2,1)S(1)} all-to-all(bf16[1,384,24]{2,0,1:T(2,128)(2,1)S(1)} %copy.108), channel_id=1, replica_groups=mesh['section'=2,'blk'=128] {'blk'}, dimensions={1} | all-to-all | bytes 36864 | tf_op jit(solution)/shard_map/all_to_all | solution.py:143
  880.6 75.9 %shard_map.97 = bf16[128,3,3072]{2,1,0:T(4,128)(2,1)} custom-call(bf16[3,3072]{1,0:T(4,128)(2,1)} %fusion.64.x_ref), custom_call_target="tpu_custom_call" | custom-call | tf_op jit(solution)/shard_map/pallas_call | solution.py:63
  963.5 19.6 %all-to-all-start.4 = ((bf16[1,384,72]{2,0,1:T(2,128)(2,1)}), bf16[1,384,72]{2,0,1:T(2,128)(2,1)S(1)}, u32[]{:S(2)}, u32[]{:S(2)}) async-start(bf16[1,384,72]{2,0,1:T(2,128)(2,1)} %copy.111), calls=%async_computation.4 | async-start | bytes 393216 | tf_op jit(solution)/shard_map/all_to_all | solution.py:101
  983.6 11.3 all-to-all-done.4
  996.5 147.7 %shard_map.98 = bf16[128,3,6144]{2,1,0:T(4,128)(2,1)} custom-call(bf16[3,6144]{1,0:T(4,128)(2,1)} %maximum_bitcast_fusion.2.x_ref), custom_call_target="tpu_custom_call" | custom-call | tf_op jit(solution)/shard_map/pallas_call | solution.py:63
  1144.2 12.4 reshape.534
  1171.7 102.0 %shard_map.99 = bf16[128,3,3072]{2,1,0:T(4,128)(2,1)} custom-call(bf16[3,3072]{1,0:T(4,128)(2,1)} %convert_element_type.232.x_ref), custom_call_target="tpu_custom_call" | custom-call | tf_op jit(solution)/shard_map/pallas_call | solution.py:63
  1279.9 27.0 %all_to_all.83 = bf16[1,384,24]{2,0,1:T(2,128)(2,1)S(1)} all-to-all(bf16[1,384,24]{2,0,1:T(2,128)(2,1)S(1)} %copy.117), channel_id=1, replica_groups=mesh['section'=2,'blk'=128] {'blk'}, dimensions={1} | all-to-all | bytes 36864 | tf_op jit(solution)/shard_map/all_to_all | solution.py:143
  (123 shorter events, 93.6 us)
Async XLA Ops:
  0.0 98.3 %copy-start = (bf16[1,3072,72]{1,2,0:T(8,128)(2,1)S(1)}, bf16[1,3072,72]{1,2,0:T(8,128)(2,1)}, u32[]{:S(2)}) copy-start(bf16[1,3072,72]{1,2,0:T(8,128)(2,1)} %param.10) | copy-start | bytes 1327108
  98.3 16.2 %copy-start.5 = (s32[2,128]{1,0:T(2,128)S(1)}, s32[2,128]{1,0:T(2,128)}, u32[]{:S(2)}) copy-start(s32[2,128]{1,0:T(2,128)} %param.15) | copy-start | bytes 3076
  98.3 16.4 %copy-start.2 = (bf16[1,2,3,3072]{3,1,2,0:T(2,128)(2,1)S(1)}, bf16[1,2,3,3072]{3,1,2,0:T(2,128)(2,1)}, u32[]{:S(2)}) copy-start(bf16[1,2,3,3072]{3,1,2,0:T(2,128)(2,1)} %param.17) | copy-start | bytes 110596
  98.3 16.4 %copy-start.3 = (bf16[1,2,3,3072]{3,1,2,0:T(2,128)(2,1)S(1)}, bf16[1,2,3,3072]{3,1,2,0:T(2,128)(2,1)}, u32[]{:S(2)}) copy-start(bf16[1,2,3,3072]{3,1,2,0:T(2,128)(2,1)} %param.16) | copy-start | bytes 110596
  98.3 16.7 %copy-start.4 = (s32[1,2,128]{2,1,0:T(2,128)S(1)}, s32[1,2,128]{2,1,0:T(2,128)}, u32[]{:S(2)}) copy-start(s32[1,2,128]{2,1,0:T(2,128)} %param.14) | copy-start | bytes 3076
  100.0 26.4 %all-to-all-start = ((bf16[1,384,72]{2,0,1:T(2,128)(2,1)}), bf16[1,384,72]{2,0,1:T(2,128)(2,1)S(1)}, u32[]{:S(2)}, u32[]{:S(2)}) async-start(bf16[1,384,72]{2,0,1:T(2,128)(2,1)} %copy.92), calls=%async_computation | async-start | bytes 393216 | tf_op jit(solution)/shard_map/all_to_all | solution.py:101
  405.1 5.4 copy-start.1
  439.0 5.2 collective-permute-start
  528.2 34.8 %all-to-all-start.2 = ((bf16[1,384,72]{2,0,1:T(2,128)(2,1)}), bf16[1,384,72]{2,0,1:T(2,128)(2,1)S(1)}, u32[]{:S(2)}, u32[]{:S(2)}) async-start(bf16[1,384,72]{2,0,1:T(2,128)(2,1)} %copy.102), calls=%async_computation.2 | async-start | bytes 393216 | tf_op jit(solution)/shard_map/all_to_all | solution.py:101
  874.6 4.9 collective-permute-start.1
  963.5 31.4 %all-to-all-start.4 = ((bf16[1,384,72]{2,0,1:T(2,128)(2,1)}), bf16[1,384,72]{2,0,1:T(2,128)(2,1)S(1)}, u32[]{:S(2)}, u32[]{:S(2)}) async-start(bf16[1,384,72]{2,0,1:T(2,128)(2,1)} %copy.111), calls=%async_computation.4 | async-start | bytes 393216 | tf_op jit(solution)/shard_map/all_to_all | solution.py:101

commit v2 on v1

--- a/solution.py
+++ b/solution.py
@@ -77,7 +77,12 @@
 def gather_rows(x, cid):
     n = lax.axis_size("blk")
     _, rows, width = x.shape
-    return gather_blk(x[0], n, cid).reshape(1, n * rows, width)
+    size = rows * width
+    tile = 16 * 128
+    padded = -(-size // tile) * tile
+    flat = jnp.pad(x.reshape(size), (0, padded - size)).reshape(padded // 128, 128)
+    out = gather_blk(flat, n, cid).reshape(n, padded)[:, :size]
+    return out.reshape(1, n * rows, width)
 
 
 def from_behind(shard, axis, by):

time: 1320 us -> 1090 us (0.83)
  Pallas kernels: 988 us -> 774 us
  blocking collectives: 81.2 us -> 52.7 us
    pallas_call x9, Pallas kernels: 988 us -> 774 us  [gather_blk(): pl.pallas_call(functools.partial(gather_kernel, n), out_shape=jax.ShapeDt...]
    reshape x3 -> x12, local copies, waits for them, and re-layouts: 37.2 us -> 5.77 us  [the longest x9 5.69 us: gather_rows(): jnp.pad(x.reshape(size), (0, padded - size)).reshape(padded // 128, 128)]
    all_to_all x3 -> x2, blocking collectives: 81.2 us -> 52.7 us  [attend(): lax.all_to_all(out_part, 'blk', split_axis=1, concat_axis=2, tiled=True)]
    all_to_all x0 -> x1, starting transfers between devices: none -> 17.1 us  [attend(): lax.all_to_all(out_part, 'blk', split_axis=1, concat_axis=2, tiled=True)]
    unnamed x12 -> x23, local copies, waits for them, and re-layouts: 0.04 us -> 14.6 us
    another operation x9 -> x12, local copies, waits for them, and re-layouts: 32.3 us -> 41.1 us  [the longest x3 23 us: gather_rows(): return out.reshape(1, n * rows, width)]
  transfers between devices with their start and end apart: 5 -> 6, of which waited for: 5 -> 6; matrix products, arithmetic and copies ran while one was open for 0% -> 0% of each run, Pallas kernels for 0% -> 0%
where the time goes in v2:
time: 1090 us; the launch traced here: 1080 us
  Pallas kernels  774 us (71%)
  local copies, waits for them, and re-layouts  106 us (10%)
  starting transfers between devices  66.5 us (6%)
  blocking collectives  52.7 us (5%)
  waiting for transfers between devices  50.4 us (5%)
  matrix products  22.4 us (2%)
    pallas_call x9, Pallas kernels, gather_blk(): pl.pallas_call(functools.partial(gather_kernel, n), out_shape=jax.ShapeDt...  774 us
    all_to_all x2, blocking collectives, attend(): lax.all_to_all(out_part, 'blk', split_axis=1, concat_axis=2, tiled=True)  52.7 us
    all_to_all x3, starting transfers between devices, attend(): lax.all_to_all(columns, 'blk', split_axis=1, concat_axis=2, tiled=True)  46.5 us
    all_to_all x3, waiting for transfers between devices, attend(): lax.all_to_all(columns, 'blk', split_axis=1, concat_axis=2, tiled=True)  32.1 us
    slice x6, local copies, waits for them, and re-layouts, attend(): key_piece = kv_piece[:, :, :width]  23.6 us
    another operation x3, local copies, waits for them, and re-layouts, gather_rows(): return out.reshape(1, n * rows, width)  23 us
  transfers between devices with their start and end apart: 6, of which 6 were waited for; matrix products, arithmetic and copies ran while one was open for 0% of the time, Pallas kernels for 0%

profile of v2, /device:TPU:1, one launch (start us, length us, event | category | flops | bytes accessed | tf_op | source)
XLA Modules:
  0.0 1083.6 jit_solution(9095012333226612808)
XLA Ops:
  6.0 76.5 %shard_map.91 = bf16[128,80,128]{2,1,0:T(8,128)(2,1)} custom-call(bf16[80,128]{1,0:T(8,128)(2,1)} %pad_bitcast_fusion.5.x_ref), custom_call_target="tpu_custom_call" | custom-call | tf_op jit(solution)/shard_map/pallas_call | solution.py:63
  91.5 13.2 %all-to-all-start = ((bf16[1,384,72]{2,0,1:T(2,128)(2,1)}), bf16[1,384,72]{2,0,1:T(2,128)(2,1)S(1)}, u32[]{:S(2)}, u32[]{:S(2)}) async-start(bf16[1,384,72]{2,0,1:T(2,128)(2,1)} %copy.79), calls=%async_computation | async-start | bytes 393216 | tf_op jit(solution)/shard_map/all_to_all | solution.py:106
  106.7 9.9 all-to-all-done
  118.3 114.7 %shard_map.92 = bf16[128,144,128]{2,1,0:T(8,128)(2,1)} custom-call(bf16[144,128]{1,0:T(8,128)(2,1)} %reshape.577.x_ref), custom_call_target="tpu_custom_call" | custom-call | tf_op jit(solution)/shard_map/pallas_call | solution.py:63
  233.0 7.7 reshape_reshape.9
  240.6 4.9 fusion.71
  255.8 74.3 %shard_map.93 = bf16[128,80,128]{2,1,0:T(8,128)(2,1)} custom-call(bf16[80,128]{1,0:T(8,128)(2,1)} %pad_bitcast_fusion.4.x_ref), custom_call_target="tpu_custom_call" | custom-call | tf_op jit(solution)/shard_map/pallas_call | solution.py:63
  338.0 26.4 %all_to_all.81 = bf16[1,384,24]{2,0,1:T(2,128)(2,1)S(1)} all-to-all(bf16[1,384,24]{2,0,1:T(2,128)(2,1)S(1)} %copy.85), channel_id=1, replica_groups=mesh['section'=2,'blk'=128] {'blk'}, dimensions={1} | all-to-all | bytes 36864 | tf_op jit(solution)/shard_map/all_to_all | solution.py:148
  371.1 64.6 %shard_map.94 = bf16[128,80,128]{2,1,0:T(8,128)(2,1)} custom-call(bf16[80,128]{1,0:T(8,128)(2,1)} %pad_bitcast_fusion.3.x_ref), custom_call_target="tpu_custom_call" | custom-call | tf_op jit(solution)/shard_map/pallas_call | solution.py:63
  444.7 16.7 %all-to-all-start.2 = ((bf16[1,384,72]{2,0,1:T(2,128)(2,1)}), bf16[1,384,72]{2,0,1:T(2,128)(2,1)S(1)}, u32[]{:S(2)}, u32[]{:S(2)}) async-start(bf16[1,384,72]{2,0,1:T(2,128)(2,1)} %copy.87), calls=%async_computation.2 | async-start | bytes 393216 | tf_op jit(solution)/shard_map/all_to_all | solution.py:106
  462.1 11.0 %all-to-all-done.2 = bf16[1,384,72]{2,0,1:T(2,128)(2,1)S(1)} async-done(((bf16[1,384,72]{2,0,1:T(2,128)(2,1)}), bf16[1,384,72]{2,0,1:T(2,128)(2,1)S(1)}, u32[]{:S(2)}, u32[]{:S(2)}) %all-to-all-start.2) | async-done | bytes 55328 | tf_op jit(solution)/shard_map/all_to_all | solution.py:106
  474.7 111.7 %shard_map.95 = bf16[128,144,128]{2,1,0:T(8,128)(2,1)} custom-call(bf16[144,128]{1,0:T(8,128)(2,1)} %reshape.589.x_ref), custom_call_target="tpu_custom_call" | custom-call | tf_op jit(solution)/shard_map/pallas_call | solution.py:63
  586.5 7.7 reshape_reshape.10
  594.1 4.9 fusion.70
  609.3 77.8 %shard_map.96 = bf16[128,80,128]{2,1,0:T(8,128)(2,1)} custom-call(bf16[80,128]{1,0:T(8,128)(2,1)} %pad_bitcast_fusion.2.x_ref), custom_call_target="tpu_custom_call" | custom-call | tf_op jit(solution)/shard_map/pallas_call | solution.py:63
  695.0 26.2 %all_to_all.82 = bf16[1,384,24]{2,0,1:T(2,128)(2,1)S(1)} all-to-all(bf16[1,384,24]{2,0,1:T(2,128)(2,1)S(1)} %copy.93), channel_id=1, replica_groups=mesh['section'=2,'blk'=128] {'blk'}, dimensions={1} | all-to-all | bytes 36864 | tf_op jit(solution)/shard_map/all_to_all | solution.py:148
  727.9 64.6 %shard_map.97 = bf16[128,80,128]{2,1,0:T(8,128)(2,1)} custom-call(bf16[80,128]{1,0:T(8,128)(2,1)} %pad_bitcast_fusion.1.x_ref), custom_call_target="tpu_custom_call" | custom-call | tf_op jit(solution)/shard_map/pallas_call | solution.py:63
  801.4 16.6 %all-to-all-start.4 = ((bf16[1,384,72]{2,0,1:T(2,128)(2,1)}), bf16[1,384,72]{2,0,1:T(2,128)(2,1)S(1)}, u32[]{:S(2)}, u32[]{:S(2)}) async-start(bf16[1,384,72]{2,0,1:T(2,128)(2,1)} %copy.95), calls=%async_computation.4 | async-start | bytes 393216 | tf_op jit(solution)/shard_map/all_to_all | solution.py:106
  818.7 11.2 %all-to-all-done.4 = bf16[1,384,72]{2,0,1:T(2,128)(2,1)S(1)} async-done(((bf16[1,384,72]{2,0,1:T(2,128)(2,1)}), bf16[1,384,72]{2,0,1:T(2,128)(2,1)S(1)}, u32[]{:S(2)}, u32[]{:S(2)}) %all-to-all-start.4) | async-done | bytes 55328 | tf_op jit(solution)/shard_map/all_to_all | solution.py:106
  831.5 113.8 %shard_map.98 = bf16[128,144,128]{2,1,0:T(8,128)(2,1)} custom-call(bf16[144,128]{1,0:T(8,128)(2,1)} %reshape.601.x_ref), custom_call_target="tpu_custom_call" | custom-call | tf_op jit(solution)/shard_map/pallas_call | solution.py:63
  945.4 7.7 reshape_reshape.11
  968.2 76.3 %shard_map.99 = bf16[128,80,128]{2,1,0:T(8,128)(2,1)} custom-call(bf16[80,128]{1,0:T(8,128)(2,1)} %pad_bitcast_fusion.x_ref), custom_call_target="tpu_custom_call" | custom-call | tf_op jit(solution)/shard_map/pallas_call | solution.py:63
  1053.0 17.1 %all-to-all-start.5 = ((bf16[1,384,24]{2,0,1:T(2,128)(2,1)}), bf16[1,384,24]{2,0,1:T(2,128)(2,1)S(1)}, u32[]{:S(2)}, u32[]{:S(2)}) async-start(bf16[1,384,24]{2,0,1:T(2,128)(2,1)} %copy.101), calls=%async_computation.5 | async-start | bytes 393216 | tf_op jit(solution)/shard_map/all_to_all | solution.py:148
  1070.2 11.9 %all-to-all-done.5 = bf16[1,384,24]{2,0,1:T(2,128)(2,1)S(1)} async-done(((bf16[1,384,24]{2,0,1:T(2,128)(2,1)}), bf16[1,384,24]{2,0,1:T(2,128)(2,1)S(1)}, u32[]{:S(2)}, u32[]{:S(2)}) %all-to-all-start.5) | async-done | bytes 18464 | tf_op jit(solution)/shard_map/all_to_all | solution.py:148
  (152 shorter events, 112.6 us)
Async XLA Ops:
  0.0 89.8 %copy-start = (bf16[1,3072,72]{1,2,0:T(8,128)(2,1)S(1)}, bf16[1,3072,72]{1,2,0:T(8,128)(2,1)}, u32[]{:S(2)}) copy-start(bf16[1,3072,72]{1,2,0:T(8,128)(2,1)} %param.10) | copy-start | bytes 1327108
  0.0 5.1 copy-start.2
  89.8 14.9 %copy-start.6 = (s32[2,128]{1,0:T(2,128)S(1)}, s32[2,128]{1,0:T(2,128)}, u32[]{:S(2)}) copy-start(s32[2,128]{1,0:T(2,128)} %param.15) | copy-start | bytes 3076
  89.8 15.2 %copy-start.3 = (bf16[1,2,3,3072]{3,1,2,0:T(2,128)(2,1)S(1)}, bf16[1,2,3,3072]{3,1,2,0:T(2,128)(2,1)}, u32[]{:S(2)}) copy-start(bf16[1,2,3,3072]{3,1,2,0:T(2,128)(2,1)} %param.17) | copy-start | bytes 110596
  89.8 15.2 %copy-start.4 = (bf16[1,2,3,3072]{3,1,2,0:T(2,128)(2,1)S(1)}, bf16[1,2,3,3072]{3,1,2,0:T(2,128)(2,1)}, u32[]{:S(2)}) copy-start(bf16[1,2,3,3072]{3,1,2,0:T(2,128)(2,1)} %param.16) | copy-start | bytes 110596
  89.8 15.4 %copy-start.5 = (s32[1,2,128]{2,1,0:T(2,128)S(1)}, s32[1,2,128]{2,1,0:T(2,128)}, u32[]{:S(2)}) copy-start(s32[1,2,128]{2,1,0:T(2,128)} %param.14) | copy-start | bytes 3076
  91.5 25.1 %all-to-all-start = ((bf16[1,384,72]{2,0,1:T(2,128)(2,1)}), bf16[1,384,72]{2,0,1:T(2,128)(2,1)S(1)}, u32[]{:S(2)}, u32[]{:S(2)}) async-start(bf16[1,384,72]{2,0,1:T(2,128)(2,1)} %copy.79), calls=%async_computation | async-start | bytes 393216 | tf_op jit(solution)/shard_map/all_to_all | solution.py:106
  332.7 2.7 copy-start.1
  365.0 4.9 collective-permute-start
  444.7 28.4 %all-to-all-start.2 = ((bf16[1,384,72]{2,0,1:T(2,128)(2,1)}), bf16[1,384,72]{2,0,1:T(2,128)(2,1)S(1)}, u32[]{:S(2)}, u32[]{:S(2)}) async-start(bf16[1,384,72]{2,0,1:T(2,128)(2,1)} %copy.87), calls=%async_computation.2 | async-start | bytes 393216 | tf_op jit(solution)/shard_map/all_to_all | solution.py:106
  721.6 5.0 collective-permute-start.1
  801.4 28.4 %all-to-all-start.4 = ((bf16[1,384,72]{2,0,1:T(2,128)(2,1)}), bf16[1,384,72]{2,0,1:T(2,128)(2,1)S(1)}, u32[]{:S(2)}, u32[]{:S(2)}) async-start(bf16[1,384,72]{2,0,1:T(2,128)(2,1)} %copy.95), calls=%async_computation.4 | async-start | bytes 393216 | tf_op jit(solution)/shard_map/all_to_all | solution.py:106
  1053.0 29.0 %all-to-all-start.5 = ((bf16[1,384,24]{2,0,1:T(2,128)(2,1)}), bf16[1,384,24]{2,0,1:T(2,128)(2,1)S(1)}, u32[]{:S(2)}, u32[]{:S(2)}) async-start(bf16[1,384,24]{2,0,1:T(2,128)(2,1)} %copy.101), calls=%async_computation.5 | async-start | bytes 393216 | tf_op jit(solution)/shard_map/all_to_all | solution.py:148

commit v3 on v2

--- a/solution.py
+++ b/solution.py
@@ -10,9 +10,18 @@
 MESH = pl.DeviceIdType.MESH
 
 
-def gather_kernel(n, x_ref, o_ref, send_sem, recv_sem, local_sem):
+def gather_kernel(n, active, x_ref, o_ref, send_sem, recv_sem, local_sem):
+    sec = lax.axis_index("section")
+    if active is None:
+        gather_body(n, sec, x_ref, o_ref, send_sem, recv_sem, local_sem)
+    else:
+        pl.when(sec == active)(
+            lambda: gather_body(n, sec, x_ref, o_ref, send_sem, recv_sem, local_sem)
+        )
+
+
+def gather_body(n, sec, x_ref, o_ref, send_sem, recv_sem, local_sem):
     me = lax.axis_index("blk")
-    sec = lax.axis_index("section")
     barrier = pltpu.get_barrier_semaphore()
 
     def greet(i, carry):
@@ -59,9 +68,9 @@
     local.wait()
 
 
-def gather_blk(x, n, cid):
+def gather_blk(x, n, cid, active):
     return pl.pallas_call(
-        functools.partial(gather_kernel, n),
+        functools.partial(gather_kernel, n, active),
         out_shape=jax.ShapeDtypeStruct((n,) + x.shape, x.dtype),
         in_specs=[pl.BlockSpec(memory_space=pl.ANY)],
         out_specs=pl.BlockSpec(memory_space=pl.ANY),
@@ -74,14 +83,14 @@
     )(x)
 
 
-def gather_rows(x, cid):
+def gather_rows(x, cid, active):
     n = lax.axis_size("blk")
     _, rows, width = x.shape
     size = rows * width
     tile = 16 * 128
     padded = -(-size // tile) * tile
     flat = jnp.pad(x.reshape(size), (0, padded - size)).reshape(padded // 128, 128)
-    out = gather_blk(flat, n, cid).reshape(n, padded)[:, :size]
+    out = gather_blk(flat, n, cid + (0 if active is None else 2 + active) * 2, active).reshape(n, padded)[:, :size]
     return out.reshape(1, n * rows, width)
 
 
@@ -91,7 +100,7 @@
     return lax.ppermute(shard, axis, pairs)
 
 
-def attend(layer_in, qkv_cols, out_cols, modulate, fresh_own, old_keys, old_values, live):
+def attend(layer_in, qkv_cols, out_cols, modulate, fresh_own, old_keys, old_values, live, active):
     stream = layer_in.astype(jnp.float32)
     center = jnp.mean(stream, axis=-1, keepdims=True)
     variance = jnp.mean((stream - center) ** 2, axis=-1, keepdims=True)
@@ -99,7 +108,7 @@
     normed_b = normed.astype(jnp.bfloat16)
     columns = jnp.einsum(
         "rnd,dc->rnc",
-        gather_rows(normed_b, 0),
+        gather_rows(normed_b, 0, active),
         qkv_cols,
         preferred_element_type=jnp.float32,
     ).astype(jnp.bfloat16)
@@ -116,7 +125,7 @@
     q_heads = queries.reshape(num_req, num_rows, num_heads, 64)
     live_float = live.astype(jnp.float32)
     run_max = jnp.full((num_req, num_heads, num_rows), -1e30, jnp.float32)
-    kv_piece = gather_rows(jnp.concatenate([keys, values], axis=2), 1)
+    kv_piece = gather_rows(jnp.concatenate([keys, values], axis=2), 1, active)
     key_piece = kv_piece[:, :, :width]
     value_piece = kv_piece[:, :, width:]
     piece_rows = key_piece.shape[1]
@@ -141,7 +150,7 @@
     attn = jnp.transpose(attn, (0, 2, 1, 3)).reshape(num_req, num_rows, width).astype(jnp.bfloat16)
     out_part = jnp.einsum(
         "rnd,dc->rnc",
-        gather_rows(attn, 0),
+        gather_rows(attn, 0, active),
         out_cols,
         preferred_element_type=jnp.float32,
     ).astype(jnp.bfloat16)
@@ -186,6 +195,7 @@
             pick_request(old_keys, req_idx),
             pick_request(old_values, req_idx),
             pick_request(live, req_idx),
+            0 if tick_idx == 0 else (1 if tick_idx == num_req else None),
         )
         if tick_idx < num_req:
             first_out.append(layer_out)

time: 1090 us -> 875 us (0.80)
  Pallas kernels: 774 us -> 411 us
  waiting for transfers between devices: 50.4 us -> 207 us
    pallas_call x9, Pallas kernels: 774 us -> 411 us  [gather_blk(): pl.pallas_call(functools.partial(gather_kernel, n, active), out_shape=jax...]
    ppermute x2, waiting for transfers between devices: 6.43 us -> 157 us  [from_behind(): return lax.ppermute(shard, axis, pairs)]
where the time goes in v3:
time: 875 us; the launch traced here: 868 us
  Pallas kernels  411 us (47%)
  waiting for transfers between devices  207 us (24%)
  local copies, waits for them, and re-layouts  106 us (12%)
  starting transfers between devices  63.1 us (7%)
  blocking collectives  47.9 us (5%)
  matrix products  22.4 us (3%)
    pallas_call x9, Pallas kernels, gather_blk(): pl.pallas_call(functools.partial(gather_kernel, n, active), out_shape=jax...  411 us
    ppermute x2, waiting for transfers between devices, from_behind(): return lax.ppermute(shard, axis, pairs)  157 us
    all_to_all x2, blocking collectives, attend(): lax.all_to_all(out_part, 'blk', split_axis=1, concat_axis=2, tiled=True)  47.9 us
    all_to_all x3, starting transfers between devices, attend(): lax.all_to_all(columns, 'blk', split_axis=1, concat_axis=2, tiled=True)  46.1 us
    all_to_all x3, waiting for transfers between devices, attend(): lax.all_to_all(columns, 'blk', split_axis=1, concat_axis=2, tiled=True)  37.8 us
    slice x6, local copies, waits for them, and re-layouts, attend(): key_piece = kv_piece[:, :, :width]  23.6 us
    another operation x3, local copies, waits for them, and re-layouts, gather_rows(): return out.reshape(1, n * rows, width)  23 us
    another operation x9, local copies, waits for them, and re-layouts  18.1 us
  transfers between devices with their start and end apart: 6, of which 6 were waited for; matrix products, arithmetic and copies ran while one was open for 0% of the time, Pallas kernels for 0%

profile of v3, /device:TPU:1, one launch (start us, length us, event | category | flops | bytes accessed | tf_op | source)
XLA Modules:
  0.0 867.8 jit_solution(10306076198671102542)
XLA Ops:
  17.3 16.3 %all-to-all-start = ((bf16[1,384,72]{2,0,1:T(2,128)(2,1)}), bf16[1,384,72]{2,0,1:T(2,128)(2,1)S(1)}, u32[]{:S(2)}, u32[]{:S(2)}) async-start(bf16[1,384,72]{2,0,1:T(2,128)(2,1)} %copy.79), calls=%async_computation | async-start | bytes 393216 | tf_op jit(solution)/shard_map/all_to_all | solution.py:115
  35.6 15.5 %all-to-all-done = bf16[1,384,72]{2,0,1:T(2,128)(2,1)S(1)} async-done(((bf16[1,384,72]{2,0,1:T(2,128)(2,1)}), bf16[1,384,72]{2,0,1:T(2,128)(2,1)S(1)}, u32[]{:S(2)}, u32[]{:S(2)}) %all-to-all-start) | async-done | bytes 55328 | tf_op jit(solution)/shard_map/all_to_all | solution.py:115
  55.2 7.7 reshape_reshape.9
  62.9 4.9 fusion.71
  88.2 21.7 %all_to_all.81 = bf16[1,384,24]{2,0,1:T(2,128)(2,1)S(1)} all-to-all(bf16[1,384,24]{2,0,1:T(2,128)(2,1)S(1)} %copy.85), channel_id=1, replica_groups=mesh['section'=2,'blk'=128] {'blk'}, dimensions={1} | all-to-all | bytes 36864 | tf_op jit(solution)/shard_map/all_to_all | solution.py:157
  111.9 153.5 %collective-permute-done = bf16[1,3,3072]{2,0,1:T(2,128)(2,1)S(1)} collective-permute-done((bf16[1,3,3072]{2,0,1:T(2,128)(2,1)S(1)}, bf16[1,3,3072]{2,0,1:T(2,128)(2,1)S(1)}, u32[]{:S(2)}, u32[]{:S(2)}) %collective-permute-start) | collective-permute-done | bytes 18464 | tf_op jit(solution)/shard_map/ppermute | solution.py:100
  266.7 64.4 %shard_map.94 = bf16[128,80,128]{2,1,0:T(8,128)(2,1)} custom-call(bf16[80,128]{1,0:T(8,128)(2,1)} %pad_bitcast_fusion.3.x_ref), custom_call_target="tpu_custom_call" | custom-call | tf_op jit(solution)/shard_map/pallas_call | solution.py:72
  340.0 17.4 %all-to-all-start.2 = ((bf16[1,384,72]{2,0,1:T(2,128)(2,1)}), bf16[1,384,72]{2,0,1:T(2,128)(2,1)S(1)}, u32[]{:S(2)}, u32[]{:S(2)}) async-start(bf16[1,384,72]{2,0,1:T(2,128)(2,1)} %copy.87), calls=%async_computation.2 | async-start | bytes 393216 | tf_op jit(solution)/shard_map/all_to_all | solution.py:115
  358.1 11.1 %all-to-all-done.2 = bf16[1,384,72]{2,0,1:T(2,128)(2,1)S(1)} async-done(((bf16[1,384,72]{2,0,1:T(2,128)(2,1)}), bf16[1,384,72]{2,0,1:T(2,128)(2,1)S(1)}, u32[]{:S(2)}, u32[]{:S(2)}) %all-to-all-start.2) | async-done | bytes 55328 | tf_op jit(solution)/shard_map/all_to_all | solution.py:115
  370.8 112.5 %shard_map.95 = bf16[128,144,128]{2,1,0:T(8,128)(2,1)} custom-call(bf16[144,128]{1,0:T(8,128)(2,1)} %reshape.589.x_ref), custom_call_target="tpu_custom_call" | custom-call | tf_op jit(solution)/shard_map/pallas_call | solution.py:72
  483.3 7.7 reshape_reshape.10
  491.0 4.9 fusion.70
  506.2 76.0 %shard_map.96 = bf16[128,80,128]{2,1,0:T(8,128)(2,1)} custom-call(bf16[80,128]{1,0:T(8,128)(2,1)} %pad_bitcast_fusion.2.x_ref), custom_call_target="tpu_custom_call" | custom-call | tf_op jit(solution)/shard_map/pallas_call | solution.py:72
  590.1 26.2 %all_to_all.82 = bf16[1,384,24]{2,0,1:T(2,128)(2,1)S(1)} all-to-all(bf16[1,384,24]{2,0,1:T(2,128)(2,1)S(1)} %copy.93), channel_id=1, replica_groups=mesh['section'=2,'blk'=128] {'blk'}, dimensions={1} | all-to-all | bytes 36864 | tf_op jit(solution)/shard_map/all_to_all | solution.py:157
  618.3 3.7 collective-permute-done.1
  623.3 41.3 %shard_map.97 = bf16[128,80,128]{2,1,0:T(8,128)(2,1)} custom-call(bf16[80,128]{1,0:T(8,128)(2,1)} %pad_bitcast_fusion.1.x_ref), custom_call_target="tpu_custom_call" | custom-call | tf_op jit(solution)/shard_map/pallas_call | solution.py:72
  673.6 12.4 %all-to-all-start.4 = ((bf16[1,384,72]{2,0,1:T(2,128)(2,1)}), bf16[1,384,72]{2,0,1:T(2,128)(2,1)S(1)}, u32[]{:S(2)}, u32[]{:S(2)}) async-start(bf16[1,384,72]{2,0,1:T(2,128)(2,1)} %copy.95), calls=%async_computation.4 | async-start | bytes 393216 | tf_op jit(solution)/shard_map/all_to_all | solution.py:115
  686.6 11.3 %all-to-all-done.4 = bf16[1,384,72]{2,0,1:T(2,128)(2,1)S(1)} async-done(((bf16[1,384,72]{2,0,1:T(2,128)(2,1)}), bf16[1,384,72]{2,0,1:T(2,128)(2,1)S(1)}, u32[]{:S(2)}, u32[]{:S(2)}) %all-to-all-start.4) | async-done | bytes 55328 | tf_op jit(solution)/shard_map/all_to_all | solution.py:115
  699.5 59.3 %shard_map.98 = bf16[128,144,128]{2,1,0:T(8,128)(2,1)} custom-call(bf16[144,128]{1,0:T(8,128)(2,1)} %reshape.601.x_ref), custom_call_target="tpu_custom_call" | custom-call | tf_op jit(solution)/shard_map/pallas_call | solution.py:72
  758.8 7.7 reshape_reshape.11
  766.4 4.9 fusion.69
  781.6 49.9 %shard_map.99 = bf16[128,80,128]{2,1,0:T(8,128)(2,1)} custom-call(bf16[80,128]{1,0:T(8,128)(2,1)} %pad_bitcast_fusion.x_ref), custom_call_target="tpu_custom_call" | custom-call | tf_op jit(solution)/shard_map/pallas_call | solution.py:72
  840.1 14.4 %all-to-all-start.5 = ((bf16[1,384,24]{2,0,1:T(2,128)(2,1)}), bf16[1,384,24]{2,0,1:T(2,128)(2,1)S(1)}, u32[]{:S(2)}, u32[]{:S(2)}) async-start(bf16[1,384,24]{2,0,1:T(2,128)(2,1)} %copy.101), calls=%async_computation.5 | async-start | bytes 393216 | tf_op jit(solution)/shard_map/all_to_all | solution.py:157
  854.5 11.9 %all-to-all-done.5 = bf16[1,384,24]{2,0,1:T(2,128)(2,1)S(1)} async-done(((bf16[1,384,24]{2,0,1:T(2,128)(2,1)}), bf16[1,384,24]{2,0,1:T(2,128)(2,1)S(1)}, u32[]{:S(2)}, u32[]{:S(2)}) %all-to-all-start.5) | async-done | bytes 18464 | tf_op jit(solution)/shard_map/all_to_all | solution.py:157
  (152 shorter events, 108.0 us)
Async XLA Ops:
  0.0 15.5 %copy-start = (bf16[1,3072,72]{1,2,0:T(8,128)(2,1)S(1)}, bf16[1,3072,72]{1,2,0:T(8,128)(2,1)}, u32[]{:S(2)}) copy-start(bf16[1,3072,72]{1,2,0:T(8,128)(2,1)} %param.10) | copy-start | bytes 1327108
  0.0 5.1 copy-start.2
  15.5 18.1 %copy-start.6 = (s32[2,128]{1,0:T(2,128)S(1)}, s32[2,128]{1,0:T(2,128)}, u32[]{:S(2)}) copy-start(s32[2,128]{1,0:T(2,128)} %param.15) | copy-start | bytes 3076
  15.6 18.4 %copy-start.3 = (bf16[1,2,3,3072]{3,1,2,0:T(2,128)(2,1)S(1)}, bf16[1,2,3,3072]{3,1,2,0:T(2,128)(2,1)}, u32[]{:S(2)}) copy-start(bf16[1,2,3,3072]{3,1,2,0:T(2,128)(2,1)} %param.17) | copy-start | bytes 110596
  15.6 18.4 %copy-start.4 = (bf16[1,2,3,3072]{3,1,2,0:T(2,128)(2,1)S(1)}, bf16[1,2,3,3072]{3,1,2,0:T(2,128)(2,1)}, u32[]{:S(2)}) copy-start(bf16[1,2,3,3072]{3,1,2,0:T(2,128)(2,1)} %param.16) | copy-start | bytes 110596
  15.6 18.6 %copy-start.5 = (s32[1,2,128]{2,1,0:T(2,128)S(1)}, s32[1,2,128]{2,1,0:T(2,128)}, u32[]{:S(2)}) copy-start(s32[1,2,128]{2,1,0:T(2,128)} %param.14) | copy-start | bytes 3076
  17.3 33.8 %all-to-all-start = ((bf16[1,384,72]{2,0,1:T(2,128)(2,1)}), bf16[1,384,72]{2,0,1:T(2,128)(2,1)S(1)}, u32[]{:S(2)}, u32[]{:S(2)}) async-start(bf16[1,384,72]{2,0,1:T(2,128)(2,1)} %copy.79), calls=%async_computation | async-start | bytes 393216 | tf_op jit(solution)/shard_map/all_to_all | solution.py:115
  82.9 2.7 copy-start.1
  110.4 155.1 %collective-permute-start = (bf16[1,3,3072]{2,0,1:T(2,128)(2,1)S(1)}, bf16[1,3,3072]{2,0,1:T(2,128)(2,1)S(1)}, u32[]{:S(2)}, u32[]{:S(2)}) collective-permute-start(bf16[1,3,3072]{2,0,1:T(2,128)(2,1)S(1)} %add_convert_fusion.2), channel_id=1, source_target_pairs={{0,128},{1,129},{2,130},{3,131},{4,132},{5,133},{6,134},{7,135},{8... | collective-permute-start | bytes 55304 | tf_op jit(solution)/shard_map/ppermute | solution.py:100
  340.0 29.1 %all-to-all-start.2 = ((bf16[1,384,72]{2,0,1:T(2,128)(2,1)}), bf16[1,384,72]{2,0,1:T(2,128)(2,1)S(1)}, u32[]{:S(2)}, u32[]{:S(2)}) async-start(bf16[1,384,72]{2,0,1:T(2,128)(2,1)} %copy.87), calls=%async_computation.2 | async-start | bytes 393216 | tf_op jit(solution)/shard_map/all_to_all | solution.py:115
  616.8 5.3 collective-permute-start.1
  673.6 24.3 %all-to-all-start.4 = ((bf16[1,384,72]{2,0,1:T(2,128)(2,1)}), bf16[1,384,72]{2,0,1:T(2,128)(2,1)S(1)}, u32[]{:S(2)}, u32[]{:S(2)}) async-start(bf16[1,384,72]{2,0,1:T(2,128)(2,1)} %copy.95), calls=%async_computation.4 | async-start | bytes 393216 | tf_op jit(solution)/shard_map/all_to_all | solution.py:115
  840.1 26.3 %all-to-all-start.5 = ((bf16[1,384,24]{2,0,1:T(2,128)(2,1)}), bf16[1,384,24]{2,0,1:T(2,128)(2,1)S(1)}, u32[]{:S(2)}, u32[]{:S(2)}) async-start(bf16[1,384,24]{2,0,1:T(2,128)(2,1)} %copy.101), calls=%async_computation.5 | async-start | bytes 393216 | tf_op jit(solution)/shard_map/all_to_all | solution.py:157

commit v4 on v3

--- a/solution.py
+++ b/solution.py
@@ -10,77 +10,111 @@
 MESH = pl.DeviceIdType.MESH
 
 
-def gather_kernel(n, active, x_ref, o_ref, send_sem, recv_sem, local_sem):
+PLANE = 16
+
+
+def gather_kernel(n, active, x_ref, o_ref, send1, recv1, send2, recv2, local_sem):
     sec = lax.axis_index("section")
+    args = (n, sec, x_ref, o_ref, send1, recv1, send2, recv2, local_sem)
     if active is None:
-        gather_body(n, sec, x_ref, o_ref, send_sem, recv_sem, local_sem)
+        gather_body(*args)
     else:
-        pl.when(sec == active)(
-            lambda: gather_body(n, sec, x_ref, o_ref, send_sem, recv_sem, local_sem)
-        )
-
-
-def gather_body(n, sec, x_ref, o_ref, send_sem, recv_sem, local_sem):
+        pl.when(sec == active)(lambda: gather_body(*args))
+
+
+def gather_body(n, sec, x_ref, o_ref, send1, recv1, send2, recv2, local_sem):
+    nz = n // PLANE
     me = lax.axis_index("blk")
+    zme = me // PLANE
+    xy = me % PLANE
     barrier = pltpu.get_barrier_semaphore()
 
-    def greet(i, carry):
-        peer = lax.rem(me + 1 + i, n)
-        pl.semaphore_signal(barrier, inc=1, device_id=(sec, peer), device_id_type=MESH)
-        return carry
-
-    lax.fori_loop(0, n - 1, greet, 0)
-    pl.semaphore_wait(barrier, n - 1)
-    local = pltpu.make_async_copy(x_ref, o_ref.at[me], local_sem)
+    def z_peer(i):
+        return lax.rem(zme + 1 + i, nz)
+
+    def xy_peer(i):
+        return lax.rem(xy + 1 + i, PLANE)
+
+    def greet_z(i, carry):
+        pl.semaphore_signal(barrier, inc=1, device_id=(sec, z_peer(i) * PLANE + xy), device_id_type=MESH)
+        return carry
+
+    def greet_xy(i, carry):
+        pl.semaphore_signal(barrier, inc=1, device_id=(sec, zme * PLANE + xy_peer(i)), device_id_type=MESH)
+        return carry
+
+    lax.fori_loop(0, nz - 1, greet_z, 0)
+    lax.fori_loop(0, PLANE - 1, greet_xy, 0)
+    pl.semaphore_wait(barrier, nz - 1 + PLANE - 1)
+
+    local = pltpu.make_async_copy(x_ref, o_ref.at[xy, zme], local_sem)
     local.start()
 
-    def remote(i):
-        peer = lax.rem(me + 1 + i, n)
+    def copy1(i, src_z):
         return pltpu.make_async_remote_copy(
             src_ref=x_ref,
-            dst_ref=o_ref.at[me],
-            send_sem=send_sem.at[i],
-            recv_sem=recv_sem.at[me],
-            device_id=(sec, peer),
+            dst_ref=o_ref.at[xy, src_z],
+            send_sem=send1.at[i],
+            recv_sem=recv1.at[src_z],
+            device_id=(sec, z_peer(i) * PLANE + xy),
             device_id_type=MESH,
         )
 
-    def send(i, carry):
-        remote(i).start()
-        return carry
-
-    lax.fori_loop(0, n - 1, send, 0)
-
-    def finish(i, carry):
-        remote(i).wait_send()
-        src = lax.rem(me + n - 1 - i, n)
-        pltpu.make_async_remote_copy(
-            src_ref=x_ref,
-            dst_ref=o_ref.at[src],
-            send_sem=send_sem.at[i],
-            recv_sem=recv_sem.at[src],
-            device_id=(sec, src),
+    def send1_step(i, carry):
+        copy1(i, zme).start()
+        return carry
+
+    lax.fori_loop(0, nz - 1, send1_step, 0)
+
+    def finish1(i, carry):
+        copy1(i, zme).wait_send()
+        copy1(i, lax.rem(zme + nz - 1 - i, nz)).wait_recv()
+        return carry
+
+    lax.fori_loop(0, nz - 1, finish1, 0)
+    local.wait()
+
+    def copy2(i, src_xy):
+        return pltpu.make_async_remote_copy(
+            src_ref=o_ref.at[src_xy],
+            dst_ref=o_ref.at[src_xy],
+            send_sem=send2.at[i],
+            recv_sem=recv2.at[src_xy],
+            device_id=(sec, zme * PLANE + xy_peer(i)),
             device_id_type=MESH,
-        ).wait_recv()
-        return carry
-
-    lax.fori_loop(0, n - 1, finish, 0)
-    local.wait()
+        )
+
+    def send2_step(i, carry):
+        copy2(i, xy).start()
+        return carry
+
+    lax.fori_loop(0, PLANE - 1, send2_step, 0)
+
+    def finish2(i, carry):
+        copy2(i, xy).wait_send()
+        copy2(i, lax.rem(xy + PLANE - 1 - i, PLANE)).wait_recv()
+        return carry
+
+    lax.fori_loop(0, PLANE - 1, finish2, 0)
 
 
 def gather_blk(x, n, cid, active):
-    return pl.pallas_call(
+    nz = n // PLANE
+    out = pl.pallas_call(
         functools.partial(gather_kernel, n, active),
-        out_shape=jax.ShapeDtypeStruct((n,) + x.shape, x.dtype),
+        out_shape=jax.ShapeDtypeStruct((PLANE, nz) + x.shape, x.dtype),
         in_specs=[pl.BlockSpec(memory_space=pl.ANY)],
         out_specs=pl.BlockSpec(memory_space=pl.ANY),
         scratch_shapes=[
-            pltpu.SemaphoreType.DMA((n,)),
-            pltpu.SemaphoreType.DMA((n,)),
+            pltpu.SemaphoreType.DMA((nz,)),
+            pltpu.SemaphoreType.DMA((nz,)),
+            pltpu.SemaphoreType.DMA((PLANE,)),
+            pltpu.SemaphoreType.DMA((PLANE,)),
             pltpu.SemaphoreType.DMA,
         ],
         compiler_params=pltpu.CompilerParams(collective_id=cid, has_side_effects=True),
     )(x)
+    return jnp.swapaxes(out, 0, 1).reshape((n,) + x.shape)
 
 
 def gather_rows(x, cid, active):

time: 875 us -> 795 us (0.909)
  Pallas kernels: 411 us -> 325 us
  waiting for transfers between devices: 207 us -> 186 us
  local copies, waits for them, and re-layouts: 106 us -> 122 us
    pallas_call x9, Pallas kernels: 411 us -> 325 us  [gather_blk(): pl.pallas_call(functools.partial(gather_kernel, n, active), out_shape=jax...]
    transpose x0 -> x9, local copies, waits for them, and re-layouts: none -> 25.9 us  [gather_blk(): return jnp.swapaxes(out, 0, 1).reshape((n,) + x.shape)]
    ppermute x2, waiting for transfers between devices: 157 us -> 142 us  [from_behind(): return lax.ppermute(shard, axis, pairs)]
    unnamed x23, local copies, waits for them, and re-layouts: 14.6 us -> 4.15 us
    all_to_all x3, starting transfers between devices: 46.1 us -> 56.1 us  [attend(): lax.all_to_all(columns, 'blk', split_axis=1, concat_axis=2, tiled=True)]
where the time goes in v4:
time: 795 us; the launch traced here: 788 us
  Pallas kernels  325 us (41%)
  waiting for transfers between devices  186 us (23%)
  local copies, waits for them, and re-layouts  122 us (15%)
  starting transfers between devices  68.9 us (9%)
  blocking collectives  53.1 us (7%)
  matrix products  22.4 us (3%)
    pallas_call x9, Pallas kernels, gather_blk(): pl.pallas_call(functools.partial(gather_kernel, n, active), out_shape=jax...  325 us
    ppermute x2, waiting for transfers between devices, from_behind(): return lax.ppermute(shard, axis, pairs)  142 us
    all_to_all x3, starting transfers between devices, attend(): lax.all_to_all(columns, 'blk', split_axis=1, concat_axis=2, tiled=True)  56.1 us
    all_to_all x2, blocking collectives, attend(): lax.all_to_all(out_part, 'blk', split_axis=1, concat_axis=2, tiled=True)  53.1 us
    all_to_all x3, waiting for transfers between devices, attend(): lax.all_to_all(columns, 'blk', split_axis=1, concat_axis=2, tiled=True)  32.3 us
    transpose x9, local copies, waits for them, and re-layouts, gather_blk(): return jnp.swapaxes(out, 0, 1).reshape((n,) + x.shape)  25.9 us
    slice x6, local copies, waits for them, and re-layouts, attend(): key_piece = kv_piece[:, :, :width]  23.6 us
    another operation x3, local copies, waits for them, and re-layouts, gather_rows(): return out.reshape(1, n * rows, width)  23 us
  transfers between devices with their start and end apart: 6, of which 6 were waited for; matrix products, arithmetic and copies ran while one was open for 0% of the time, Pallas kernels for 0%

profile of v4, /device:TPU:1, one launch (start us, length us, event | category | flops | bytes accessed | tf_op | source)
XLA Modules:
  0.0 787.8 jit_solution(11459254146640542376)
XLA Ops:
  15.6 16.3 %all-to-all-start = ((bf16[1,384,72]{2,0,1:T(2,128)(2,1)}), bf16[1,384,72]{2,0,1:T(2,128)(2,1)S(1)}, u32[]{:S(2)}, u32[]{:S(2)}) async-start(bf16[1,384,72]{2,0,1:T(2,128)(2,1)} %copy.92), calls=%async_computation | async-start | bytes 393216 | tf_op jit(solution)/shard_map/all_to_all | solution.py:149
  34.0 9.9 %all-to-all-done = bf16[1,384,72]{2,0,1:T(2,128)(2,1)S(1)} async-done(((bf16[1,384,72]{2,0,1:T(2,128)(2,1)}), bf16[1,384,72]{2,0,1:T(2,128)(2,1)S(1)}, u32[]{:S(2)}, u32[]{:S(2)}) %all-to-all-start) | async-done | bytes 55328 | tf_op jit(solution)/shard_map/all_to_all | solution.py:149
  46.4 4.8 copy.94
  51.3 7.7 reshape_reshape_reshape.9
  58.9 4.9 fusion.71
  82.6 21.4 %all_to_all.81 = bf16[1,384,24]{2,0,1:T(2,128)(2,1)S(1)} all-to-all(bf16[1,384,24]{2,0,1:T(2,128)(2,1)S(1)} %copy.100), channel_id=1, replica_groups=mesh['section'=2,'blk'=128] {'blk'}, dimensions={1} | all-to-all | bytes 36864 | tf_op jit(solution)/shard_map/all_to_all | solution.py:191
  106.1 138.0 %collective-permute-done = bf16[1,3,3072]{2,0,1:T(2,128)(2,1)S(1)} collective-permute-done((bf16[1,3,3072]{2,0,1:T(2,128)(2,1)S(1)}, bf16[1,3,3072]{2,0,1:T(2,128)(2,1)S(1)}, u32[]{:S(2)}, u32[]{:S(2)}) %collective-permute-start) | collective-permute-done | bytes 18464 | tf_op jit(solution)/shard_map/ppermute | solution.py:134
  245.4 45.0 %shard_map.94 = bf16[16,8,80,128]{3,2,1,0:T(8,128)(2,1)} custom-call(bf16[80,128]{1,0:T(8,128)(2,1)} %pad_bitcast_fusion.3.x_ref), custom_call_target="tpu_custom_call" | custom-call | tf_op jit(solution)/shard_map/pallas_call | solution.py:103
  299.5 26.4 %all-to-all-start.2 = ((bf16[1,384,72]{2,0,1:T(2,128)(2,1)}), bf16[1,384,72]{2,0,1:T(2,128)(2,1)S(1)}, u32[]{:S(2)}, u32[]{:S(2)}) async-start(bf16[1,384,72]{2,0,1:T(2,128)(2,1)} %copy.103), calls=%async_computation.2 | async-start | bytes 393216 | tf_op jit(solution)/shard_map/all_to_all | solution.py:149
  326.6 11.2 %all-to-all-done.2 = bf16[1,384,72]{2,0,1:T(2,128)(2,1)S(1)} async-done(((bf16[1,384,72]{2,0,1:T(2,128)(2,1)}), bf16[1,384,72]{2,0,1:T(2,128)(2,1)S(1)}, u32[]{:S(2)}, u32[]{:S(2)}) %all-to-all-start.2) | async-done | bytes 55328 | tf_op jit(solution)/shard_map/all_to_all | solution.py:149
  339.4 71.4 %shard_map.95 = bf16[16,8,144,128]{3,2,1,0:T(8,128)(2,1)} custom-call(bf16[144,128]{1,0:T(8,128)(2,1)} %reshape.568.x_ref), custom_call_target="tpu_custom_call" | custom-call | tf_op jit(solution)/shard_map/pallas_call | solution.py:103
  415.7 7.7 reshape_reshape_reshape.10
  423.3 4.9 fusion.70
  438.5 84.7 %shard_map.96 = bf16[16,8,80,128]{3,2,1,0:T(8,128)(2,1)} custom-call(bf16[80,128]{1,0:T(8,128)(2,1)} %pad_bitcast_fusion.2.x_ref), custom_call_target="tpu_custom_call" | custom-call | tf_op jit(solution)/shard_map/pallas_call | solution.py:103
  531.3 31.6 %all_to_all.82 = bf16[1,384,24]{2,0,1:T(2,128)(2,1)S(1)} all-to-all(bf16[1,384,24]{2,0,1:T(2,128)(2,1)S(1)} %copy.111), channel_id=1, replica_groups=mesh['section'=2,'blk'=128] {'blk'}, dimensions={1} | all-to-all | bytes 36864 | tf_op jit(solution)/shard_map/all_to_all | solution.py:191
  569.9 28.4 %shard_map.97 = bf16[16,8,80,128]{3,2,1,0:T(8,128)(2,1)} custom-call(bf16[80,128]{1,0:T(8,128)(2,1)} %pad_bitcast_fusion.1.x_ref), custom_call_target="tpu_custom_call" | custom-call | tf_op jit(solution)/shard_map/pallas_call | solution.py:103
  607.4 13.3 %all-to-all-start.4 = ((bf16[1,384,72]{2,0,1:T(2,128)(2,1)}), bf16[1,384,72]{2,0,1:T(2,128)(2,1)S(1)}, u32[]{:S(2)}, u32[]{:S(2)}) async-start(bf16[1,384,72]{2,0,1:T(2,128)(2,1)} %copy.114), calls=%async_computation.4 | async-start | bytes 393216 | tf_op jit(solution)/shard_map/all_to_all | solution.py:149
  621.3 11.3 %all-to-all-done.4 = bf16[1,384,72]{2,0,1:T(2,128)(2,1)S(1)} async-done(((bf16[1,384,72]{2,0,1:T(2,128)(2,1)}), bf16[1,384,72]{2,0,1:T(2,128)(2,1)S(1)}, u32[]{:S(2)}, u32[]{:S(2)}) %all-to-all-start.4) | async-done | bytes 55328 | tf_op jit(solution)/shard_map/all_to_all | solution.py:149
  634.2 53.4 %shard_map.98 = bf16[16,8,144,128]{3,2,1,0:T(8,128)(2,1)} custom-call(bf16[144,128]{1,0:T(8,128)(2,1)} %reshape.578.x_ref), custom_call_target="tpu_custom_call" | custom-call | tf_op jit(solution)/shard_map/pallas_call | solution.py:103
  692.4 7.7 reshape_reshape_reshape.11
  700.1 4.9 fusion.69
  715.2 40.2 %shard_map.99 = bf16[16,8,80,128]{3,2,1,0:T(8,128)(2,1)} custom-call(bf16[80,128]{1,0:T(8,128)(2,1)} %pad_bitcast_fusion.x_ref), custom_call_target="tpu_custom_call" | custom-call | tf_op jit(solution)/shard_map/pallas_call | solution.py:103
  764.2 10.2 %all-to-all-start.5 = ((bf16[1,384,24]{2,0,1:T(2,128)(2,1)}), bf16[1,384,24]{2,0,1:T(2,128)(2,1)S(1)}, u32[]{:S(2)}, u32[]{:S(2)}) async-start(bf16[1,384,24]{2,0,1:T(2,128)(2,1)} %copy.122), calls=%async_computation.5 | async-start | bytes 393216 | tf_op jit(solution)/shard_map/all_to_all | solution.py:191
  774.5 11.9 %all-to-all-done.5 = bf16[1,384,24]{2,0,1:T(2,128)(2,1)S(1)} async-done(((bf16[1,384,24]{2,0,1:T(2,128)(2,1)}), bf16[1,384,24]{2,0,1:T(2,128)(2,1)S(1)}, u32[]{:S(2)}, u32[]{:S(2)}) %all-to-all-start.5) | async-done | bytes 18464 | tf_op jit(solution)/shard_map/all_to_all | solution.py:191
  (161 shorter events, 117.2 us)
Async XLA Ops:
  0.0 13.9 %copy-start = (bf16[1,3072,72]{1,2,0:T(8,128)(2,1)S(1)}, bf16[1,3072,72]{1,2,0:T(8,128)(2,1)}, u32[]{:S(2)}) copy-start(bf16[1,3072,72]{1,2,0:T(8,128)(2,1)} %param.10) | copy-start | bytes 1327108
  0.0 5.1 copy-start.2
  13.9 18.1 %copy-start.6 = (s32[2,128]{1,0:T(2,128)S(1)}, s32[2,128]{1,0:T(2,128)}, u32[]{:S(2)}) copy-start(s32[2,128]{1,0:T(2,128)} %param.15) | copy-start | bytes 3076
  13.9 18.4 %copy-start.3 = (bf16[1,2,3,3072]{3,1,2,0:T(2,128)(2,1)S(1)}, bf16[1,2,3,3072]{3,1,2,0:T(2,128)(2,1)}, u32[]{:S(2)}) copy-start(bf16[1,2,3,3072]{3,1,2,0:T(2,128)(2,1)} %param.17) | copy-start | bytes 110596
  13.9 18.4 %copy-start.4 = (bf16[1,2,3,3072]{3,1,2,0:T(2,128)(2,1)S(1)}, bf16[1,2,3,3072]{3,1,2,0:T(2,128)(2,1)}, u32[]{:S(2)}) copy-start(bf16[1,2,3,3072]{3,1,2,0:T(2,128)(2,1)} %param.16) | copy-start | bytes 110596
  13.9 18.6 %copy-start.5 = (s32[1,2,128]{2,1,0:T(2,128)S(1)}, s32[1,2,128]{2,1,0:T(2,128)}, u32[]{:S(2)}) copy-start(s32[1,2,128]{2,1,0:T(2,128)} %param.14) | copy-start | bytes 3076
  15.6 28.3 %all-to-all-start = ((bf16[1,384,72]{2,0,1:T(2,128)(2,1)}), bf16[1,384,72]{2,0,1:T(2,128)(2,1)S(1)}, u32[]{:S(2)}, u32[]{:S(2)}) async-start(bf16[1,384,72]{2,0,1:T(2,128)(2,1)} %copy.92), calls=%async_computation | async-start | bytes 393216 | tf_op jit(solution)/shard_map/all_to_all | solution.py:149
  77.3 2.7 copy-start.1
  104.5 139.6 %collective-permute-start = (bf16[1,3,3072]{2,0,1:T(2,128)(2,1)S(1)}, bf16[1,3,3072]{2,0,1:T(2,128)(2,1)S(1)}, u32[]{:S(2)}, u32[]{:S(2)}) collective-permute-start(bf16[1,3,3072]{2,0,1:T(2,128)(2,1)S(1)} %add_convert_fusion.2), channel_id=1, source_target_pairs={{0,128},{1,129},{2,130},{3,131},{4,132},{5,133},{6,134},{7,135},{8... | collective-permute-start | bytes 55304 | tf_op jit(solution)/shard_map/ppermute | solution.py:134
  299.5 38.3 %all-to-all-start.2 = ((bf16[1,384,72]{2,0,1:T(2,128)(2,1)}), bf16[1,384,72]{2,0,1:T(2,128)(2,1)S(1)}, u32[]{:S(2)}, u32[]{:S(2)}) async-start(bf16[1,384,72]{2,0,1:T(2,128)(2,1)} %copy.103), calls=%async_computation.2 | async-start | bytes 393216 | tf_op jit(solution)/shard_map/all_to_all | solution.py:149
  563.4 5.3 collective-permute-start.1
  607.4 25.2 %all-to-all-start.4 = ((bf16[1,384,72]{2,0,1:T(2,128)(2,1)}), bf16[1,384,72]{2,0,1:T(2,128)(2,1)S(1)}, u32[]{:S(2)}, u32[]{:S(2)}) async-start(bf16[1,384,72]{2,0,1:T(2,128)(2,1)} %copy.114), calls=%async_computation.4 | async-start | bytes 393216 | tf_op jit(solution)/shard_map/all_to_all | solution.py:149
  764.2 22.1 %all-to-all-start.5 = ((bf16[1,384,24]{2,0,1:T(2,128)(2,1)}), bf16[1,384,24]{2,0,1:T(2,128)(2,1)S(1)}, u32[]{:S(2)}, u32[]{:S(2)}) async-start(bf16[1,384,24]{2,0,1:T(2,128)(2,1)} %copy.122), calls=%async_computation.5 | async-start | bytes 393216 | tf_op jit(solution)/shard_map/all_to_all | solution.py:191

commit v5 on v4

--- a/solution.py
+++ b/solution.py
@@ -192,52 +192,58 @@
     return (stream + modulate[2] * mixed_back.astype(jnp.float32)).astype(jnp.bfloat16)
 
 
-def pick_request(array, req_idx):
-    return lax.dynamic_index_in_dim(array, req_idx, 0, keepdims=True)
+def swap_sections(x):
+    return lax.ppermute(x, "section", [(0, 1), (1, 0)])
 
 
 def per_device(hidden, qkv_weight, out_weight, modulation, timestep, fresh, live, k_stale, v_stale):
-    section_idx = lax.axis_index("section")
+    sec = lax.axis_index("section")
     block_idx = lax.axis_index("blk")
     steps_all = modulation.shape[1]
     pick_row = (jnp.arange(steps_all) == timestep[0]).astype(jnp.float32)
-    modulate = jnp.einsum("t,tcd->cd", pick_row, modulation[0], precision=lax.Precision.HIGHEST)
+    modulate_own = jnp.einsum("t,tcd->cd", pick_row, modulation[0], precision=lax.Precision.HIGHEST)
     num_blocks = fresh.shape[2]
     own_column = (jnp.arange(num_blocks) == block_idx).astype(jnp.int32)
     fresh_own = jnp.sum(fresh[0] * own_column[None, :], axis=1)
-    qkv_cols = qkv_weight[0]
-    out_cols = out_weight[0]
-    old_keys = k_stale[0]
-    old_values = v_stale[0]
-    num_req = hidden.shape[0]
-    received = jnp.zeros_like(hidden[0:1])
-    first_out = []
-    second_out = []
-    for tick_idx in range(num_req + 1):
-        if tick_idx < num_req:
-            own_input = hidden[tick_idx : tick_idx + 1]
-        else:
-            own_input = jnp.zeros_like(hidden[0:1])
-        layer_in = jnp.where(section_idx == 0, own_input, received)
-        req_idx = jnp.clip(tick_idx - section_idx, 0, num_req - 1)
-        layer_out = attend(
+    qkv_own = qkv_weight[0]
+    out_own = out_weight[0]
+    stale_own = jnp.concatenate([k_stale[0], v_stale[0]], axis=2)
+
+    qkv_other = swap_sections(qkv_own)
+    out_other = swap_sections(out_own)
+    modulate_other = swap_sections(modulate_own)
+    fresh_other = swap_sections(fresh_own)
+    stale_other = swap_sections(lax.dynamic_index_in_dim(stale_own, 1 - sec, 0, keepdims=True))
+
+    stale_mine = lax.dynamic_index_in_dim(stale_own, sec, 0, keepdims=True)
+    fresh_mine = lax.dynamic_index_in_dim(fresh_own, sec, 0, keepdims=True)
+    fresh_theirs = lax.dynamic_index_in_dim(fresh_other, sec, 0, keepdims=True)
+    live_mine = lax.dynamic_index_in_dim(live, sec, 0, keepdims=True)
+    width = hidden.shape[2]
+
+    layer_in = lax.dynamic_index_in_dim(hidden, sec, 0, keepdims=True)
+    outs = []
+    for layer in range(2):
+        own = sec == layer
+        stale = jnp.where(own, stale_mine, stale_other)
+        layer_in = attend(
             layer_in,
-            qkv_cols,
-            out_cols,
-            modulate,
-            pick_request(fresh_own, req_idx),
-            pick_request(old_keys, req_idx),
-            pick_request(old_values, req_idx),
-            pick_request(live, req_idx),
-            0 if tick_idx == 0 else (1 if tick_idx == num_req else None),
+            jnp.where(own, qkv_own, qkv_other),
+            jnp.where(own, out_own, out_other),
+            jnp.where(own, modulate_own, modulate_other),
+            jnp.where(own, fresh_mine, fresh_theirs),
+            stale[:, :, :width],
+            stale[:, :, width:],
+            live_mine,
+            None,
         )
-        if tick_idx < num_req:
-            first_out.append(layer_out)
-            received = from_behind(layer_out, "section", 1)
-        if tick_idx >= 1:
-            second_out.append(layer_out)
+        outs.append(layer_in)
+    first_req1 = lax.ppermute(outs[0], "section", [(1, 0)])
+    second_req0 = lax.ppermute(outs[1], "section", [(0, 1)])
     result = jnp.where(
-        section_idx == 0, jnp.concatenate(first_out, axis=0), jnp.concatenate(second_out, axis=0)
+        sec == 0,
+        jnp.concatenate([outs[0], first_req1], axis=0),
+        jnp.concatenate([second_req0, outs[1]], axis=0),
     )
     return result[None]
 

time: 795 us -> 640 us (0.81)
  waiting for transfers between devices: 186 us -> 33.3 us
  Pallas kernels: 325 us -> 391 us
  local copies, waits for them, and re-layouts: 122 us -> 87.7 us
  blocking collectives: 53.1 us -> 34.1 us
    ppermute x2 -> x7, waiting for transfers between devices: 142 us -> 4.16 us  [the longest x1 4.15 us: per_device(): second_req0 = lax.ppermute(outs[1], 'section', [(0, 1)])]
    pallas_call x9 -> x6, Pallas kernels: 325 us -> 391 us  [gather_blk(): pl.pallas_call(functools.partial(gather_kernel, n, active), out_shape=jax...]
    all_to_all x3 -> x2, starting transfers between devices: 56.1 us -> 34.1 us  [attend(): lax.all_to_all(columns, 'blk', split_axis=1, concat_axis=2, tiled=True)]
    all_to_all x2 -> x1, blocking collectives: 53.1 us -> 34.1 us  [attend(): lax.all_to_all(out_part, 'blk', split_axis=1, concat_axis=2, tiled=True)]
    all_to_all x1, starting transfers between devices: 10.2 us -> 22.1 us  [attend(): lax.all_to_all(out_part, 'blk', split_axis=1, concat_axis=2, tiled=True)]
    all_to_all x3 -> x2, waiting for transfers between devices: 32.3 us -> 21.6 us  [attend(): lax.all_to_all(columns, 'blk', split_axis=1, concat_axis=2, tiled=True)]
    transpose x9 -> x6, local copies, waits for them, and re-layouts: 25.9 us -> 17.3 us  [gather_blk(): return jnp.swapaxes(out, 0, 1).reshape((n,) + x.shape)]
    slice x6 -> x4, local copies, waits for them, and re-layouts: 23.6 us -> 15.7 us  [attend(): key_piece = kv_piece[:, :, :width]]
  transfers between devices with their start and end apart: 6 -> 10, of which waited for: 6 -> 4; matrix products, arithmetic and copies ran while one was open for 0% -> 9% of each run, Pallas kernels for 0% -> 32%
where the time goes in v5:
time: 640 us; the launch traced here: 638 us
  Pallas kernels  391 us (61%)
  local copies, waits for them, and re-layouts  87.7 us (14%)
  starting transfers between devices  66.4 us (10%)
  blocking collectives  34.1 us (5%)
  waiting for transfers between devices  33.3 us (5%)
  matrix products  15.6 us (2%)
  other arithmetic  6.43 us (1%)
    pallas_call x6, Pallas kernels, gather_blk(): pl.pallas_call(functools.partial(gather_kernel, n, active), out_shape=jax...  391 us
    all_to_all x2, starting transfers between devices, attend(): lax.all_to_all(columns, 'blk', split_axis=1, concat_axis=2, tiled=True)  34.1 us
    all_to_all x1, blocking collectives, attend(): lax.all_to_all(out_part, 'blk', split_axis=1, concat_axis=2, tiled=True)  34.1 us
    all_to_all x1, starting transfers between devices, attend(): lax.all_to_all(out_part, 'blk', split_axis=1, concat_axis=2, tiled=True)  22.1 us
    all_to_all x2, waiting for transfers between devices, attend(): lax.all_to_all(columns, 'blk', split_axis=1, concat_axis=2, tiled=True)  21.6 us
    transpose x6, local copies, waits for them, and re-layouts, gather_blk(): return jnp.swapaxes(out, 0, 1).reshape((n,) + x.shape)  17.3 us
    slice x4, local copies, waits for them, and re-layouts, attend(): key_piece = kv_piece[:, :, :width]  15.7 us
    another operation x2, local copies, waits for them, and re-layouts, gather_rows(): return out.reshape(1, n * rows, width)  15.3 us
  transfers between devices with their start and end apart: 10, of which 4 were waited for; matrix products, arithmetic and copies ran while one was open for 9% of the time, Pallas kernels for 32%

profile of v5, /device:TPU:1, one launch (start us, length us, event | category | flops | bytes accessed | tf_op | source)
XLA Modules:
  0.0 638.4 jit_solution(12461491864295482948)
XLA Ops:
  3.1 3.3 collective-permute-start
  13.2 53.9 %shard_map.91 = bf16[16,8,80,128]{3,2,1,0:T(8,128)(2,1)} custom-call(bf16[80,128]{1,0:T(8,128)(2,1)} %pad_bitcast_fusion.3.x_ref), custom_call_target="tpu_custom_call" | custom-call | tf_op jit(solution)/shard_map/pallas_call | solution.py:103
  71.4 3.3 reshape.405
  76.4 15.3 %all-to-all-start = ((bf16[1,384,72]{2,0,1:T(2,128)(2,1)}), bf16[1,384,72]{2,0,1:T(2,128)(2,1)S(1)}, u32[]{:S(2)}, u32[]{:S(2)}) async-start(bf16[1,384,72]{2,0,1:T(2,128)(2,1)} %copy.98), calls=%async_computation | async-start | bytes 393216 | tf_op jit(solution)/shard_map/all_to_all | solution.py:149
  92.3 11.1 %all-to-all-done = bf16[1,384,72]{2,0,1:T(2,128)(2,1)S(1)} async-done(((bf16[1,384,72]{2,0,1:T(2,128)(2,1)}), bf16[1,384,72]{2,0,1:T(2,128)(2,1)S(1)}, u32[]{:S(2)}, u32[]{:S(2)}) %all-to-all-start) | async-done | bytes 55328 | tf_op jit(solution)/shard_map/all_to_all | solution.py:149
  105.0 76.6 %shard_map.92 = bf16[16,8,144,128]{3,2,1,0:T(8,128)(2,1)} custom-call(bf16[144,128]{1,0:T(8,128)(2,1)} %reshape.407.x_ref), custom_call_target="tpu_custom_call" | custom-call | tf_op jit(solution)/shard_map/pallas_call | solution.py:103
  181.6 4.8 copy.102
  186.5 7.7 %reshape_reshape_reshape.6 = bf16[1,384,6144]{2,1,0:T(8,128)(2,1)} reshape(bf16[8,16,144,128]{3,2,1,0:T(8,128)(2,1)} %copy.102) | data formatting | bytes 9437184 | tf_op jit(solution)/shard_map/reshape;reshape;reshape | solution.py:128
  194.1 4.9 fusion.52
  208.7 3.3 fusion.10
  212.7 73.5 %shard_map.93 = bf16[16,8,80,128]{3,2,1,0:T(8,128)(2,1)} custom-call(bf16[80,128]{1,0:T(8,128)(2,1)} %pad_bitcast_fusion.2.x_ref), custom_call_target="tpu_custom_call" | custom-call | tf_op jit(solution)/shard_map/pallas_call | solution.py:103
  295.6 34.1 %all_to_all.54 = bf16[1,384,24]{2,0,1:T(2,128)(2,1)S(1)} all-to-all(bf16[1,384,24]{2,0,1:T(2,128)(2,1)S(1)} %copy.108), channel_id=1, replica_groups=mesh['section'=2,'blk'=128] {'blk'}, dimensions={1} | all-to-all | bytes 36864 | tf_op jit(solution)/shard_map/all_to_all | solution.py:191
  331.4 38.8 %shard_map.94 = bf16[16,8,80,128]{3,2,1,0:T(8,128)(2,1)} custom-call(bf16[80,128]{1,0:T(8,128)(2,1)} %pad_bitcast_fusion.1.x_ref), custom_call_target="tpu_custom_call" | custom-call | tf_op jit(solution)/shard_map/pallas_call | solution.py:103
  379.3 18.9 %all-to-all-start.2 = ((bf16[1,384,72]{2,0,1:T(2,128)(2,1)}), bf16[1,384,72]{2,0,1:T(2,128)(2,1)S(1)}, u32[]{:S(2)}, u32[]{:S(2)}) async-start(bf16[1,384,72]{2,0,1:T(2,128)(2,1)} %copy.111), calls=%async_computation.2 | async-start | bytes 393216 | tf_op jit(solution)/shard_map/all_to_all | solution.py:149
  399.4 10.5 %all-to-all-done.2 = bf16[1,384,72]{2,0,1:T(2,128)(2,1)S(1)} async-done(((bf16[1,384,72]{2,0,1:T(2,128)(2,1)}), bf16[1,384,72]{2,0,1:T(2,128)(2,1)S(1)}, u32[]{:S(2)}, u32[]{:S(2)}) %all-to-all-start.2) | async-done | bytes 55328 | tf_op jit(solution)/shard_map/all_to_all | solution.py:149
  411.5 73.0 %shard_map.95 = bf16[16,8,144,128]{3,2,1,0:T(8,128)(2,1)} custom-call(bf16[144,128]{1,0:T(8,128)(2,1)} %reshape.416.x_ref), custom_call_target="tpu_custom_call" | custom-call | tf_op jit(solution)/shard_map/pallas_call | solution.py:103
  484.6 4.8 copy.113
  489.4 7.7 %reshape_reshape_reshape.7 = bf16[1,384,6144]{2,1,0:T(8,128)(2,1)} reshape(bf16[8,16,144,128]{3,2,1,0:T(8,128)(2,1)} %copy.113) | data formatting | bytes 9437184 | tf_op jit(solution)/shard_map/reshape;reshape;reshape | solution.py:128
  497.1 4.9 fusion.51
  512.2 75.4 %shard_map.96 = bf16[16,8,80,128]{3,2,1,0:T(8,128)(2,1)} custom-call(bf16[80,128]{1,0:T(8,128)(2,1)} %pad_bitcast_fusion.x_ref), custom_call_target="tpu_custom_call" | custom-call | tf_op jit(solution)/shard_map/pallas_call | solution.py:103
  597.6 22.1 %all-to-all-start.3 = ((bf16[1,384,24]{2,0,1:T(2,128)(2,1)}), bf16[1,384,24]{2,0,1:T(2,128)(2,1)S(1)}, u32[]{:S(2)}, u32[]{:S(2)}) async-start(bf16[1,384,24]{2,0,1:T(2,128)(2,1)} %copy.119), calls=%async_computation.3 | async-start | bytes 393216 | tf_op jit(solution)/shard_map/all_to_all | solution.py:191
  619.8 4.3 collective-permute-start.5
  624.1 7.6 %all-to-all-done.3 = bf16[1,384,24]{2,0,1:T(2,128)(2,1)S(1)} async-done(((bf16[1,384,24]{2,0,1:T(2,128)(2,1)}), bf16[1,384,24]{2,0,1:T(2,128)(2,1)S(1)}, u32[]{:S(2)}, u32[]{:S(2)}) %all-to-all-start.3) | async-done | bytes 18464 | tf_op jit(solution)/shard_map/all_to_all | solution.py:191
  633.5 4.1 collective-permute-done.6
  (126 shorter events, 70.9 us)
Async XLA Ops:
  0.0 7.9 %copy-start.7 = (s32[1,2,128]{2,1,0:T(2,128)S(1)}, s32[1,2,128]{2,1,0:T(2,128)}, u32[]{:S(2)}) copy-start(s32[1,2,128]{2,1,0:T(2,128)} %param.14) | copy-start | bytes 3076
  0.0 8.6 %copy-start.1 = (bf16[2,3,3072]{2,0,1:T(2,128)(2,1)S(1)}, bf16[2,3,3072]{2,0,1:T(2,128)(2,1)}, u32[]{:S(2)}) copy-start(bf16[2,3,3072]{2,0,1:T(2,128)(2,1)} %param.9) | copy-start | bytes 110596
  0.0 9.0 %copy-start.8 = (s32[2,128]{1,0:T(2,128)S(1)}, s32[2,128]{1,0:T(2,128)}, u32[]{:S(2)}) copy-start(s32[2,128]{1,0:T(2,128)} %param.15) | copy-start | bytes 3076
  3.1 8.5 %collective-permute-start = (f32[3,3072]{1,0:T(4,128)S(1)}, f32[3,3072]{1,0:T(4,128)S(1)}, u32[]{:S(2)}, u32[]{:S(2)}) collective-permute-start(f32[3,3072]{1,0:T(4,128)S(1)} %bitcast.186), channel_id=1, source_target_pairs={{0,128},{128,0},{1,129},{129,1},{2,130},{130,2},{3,131},{131,3},{4... | collective-permute-start | bytes 110600 | tf_op jit(solution)/shard_map/ppermute | solution.py:196
  6.4 68.2 %collective-permute-start.1 = (bf16[3072,72]{0,1:T(8,128)(2,1)}, bf16[3072,72]{0,1:T(8,128)(2,1)S(1)}, u32[]{:S(2)}, u32[]{:S(2)}) collective-permute-start(bf16[3072,72]{0,1:T(8,128)(2,1)} %bitcast.177), channel_id=1, source_target_pairs={{0,128},{128,0},{1,129},{129,1},{2,130},{130,2},{3,131},{131,3},{4... | collective-permute-start | bytes 1327112 | tf_op jit(solution)/shard_map/ppermute | solution.py:196
  7.4 84.2 %collective-permute-start.3 = (bf16[1,3,6144]{2,1,0:T(4,128)(2,1)S(1)}, bf16[1,3,6144]{2,1,0:T(4,128)(2,1)S(1)}, u32[]{:S(2)}, u32[]{:S(2)}) collective-permute-start(bf16[1,3,6144]{2,1,0:T(4,128)(2,1)S(1)} %fusion.30), channel_id=1, source_target_pairs={{0,128},{128,0},{1,129},{129,1},{2,130},{130,2},{3,131},{131,3},{4... | collective-permute-start | bytes 110600 | tf_op jit(solution)/shard_map/ppermute | solution.py:196
  8.0 1.9 collective-permute-start.2
  8.2 285.5 %collective-permute-start.4 = (bf16[3072,24]{0,1:T(8,128)(2,1)}, bf16[3072,24]{0,1:T(8,128)(2,1)}, u32[]{:S(2)}, u32[]{:S(2)}) collective-permute-start(bf16[3072,24]{0,1:T(8,128)(2,1)} %bitcast.26), channel_id=1, source_target_pairs={{0,128},{128,0},{1,129},{129,1},{2,130},{130,2},{3,131},{131,3},{4... | collective-permute-start | bytes 442376 | tf_op jit(solution)/shard_map/ppermute | solution.py:196
  71.4 3.3 copy-start
  76.4 27.0 %all-to-all-start = ((bf16[1,384,72]{2,0,1:T(2,128)(2,1)}), bf16[1,384,72]{2,0,1:T(2,128)(2,1)S(1)}, u32[]{:S(2)}, u32[]{:S(2)}) async-start(bf16[1,384,72]{2,0,1:T(2,128)(2,1)} %copy.98), calls=%async_computation | async-start | bytes 393216 | tf_op jit(solution)/shard_map/all_to_all | solution.py:149
  293.7 36.4 %copy-start.2 = (bf16[2,3,3072]{2,0,1:T(2,128)(2,1)S(1)}, bf16[2,3,3072]{2,0,1:T(2,128)(2,1)}, u32[]{:S(2)}) copy-start(bf16[2,3,3072]{2,0,1:T(2,128)(2,1)} %param.9) | copy-start | bytes 110596
  293.7 36.4 %copy-start.6 = (f32[1,3072]{1,0:T(1,128)S(1)}, f32[1,3072]{1,0:T(1,128)}, u32[]{:S(2)}) copy-start(f32[1,3072]{1,0:T(1,128)} %get-tuple-element.35) | copy-start | bytes 36868
  293.7 36.8 %copy-start.4 = (f32[1,3072]{1,0:T(1,128)S(1)}, f32[1,3072]{1,0:T(1,128)}, u32[]{:S(2)}) copy-start(f32[1,3072]{1,0:T(1,128)} %get-tuple-element.23) | copy-start | bytes 36868
  377.6 33.2 %copy-start.3 = (bf16[1,3,6144]{2,1,0:T(4,128)(2,1)S(1)}, bf16[1,3,6144]{2,1,0:T(4,128)(2,1)}, u32[]{:S(2)}) copy-start(bf16[1,3,6144]{2,1,0:T(4,128)(2,1)} %get-tuple-element.11) | copy-start | bytes 110596
  379.3 30.6 %all-to-all-start.2 = ((bf16[1,384,72]{2,0,1:T(2,128)(2,1)}), bf16[1,384,72]{2,0,1:T(2,128)(2,1)S(1)}, u32[]{:S(2)}, u32[]{:S(2)}) async-start(bf16[1,384,72]{2,0,1:T(2,128)(2,1)} %copy.111), calls=%async_computation.2 | async-start | bytes 393216 | tf_op jit(solution)/shard_map/all_to_all | solution.py:149
  595.1 37.0 %copy-start.5 = (f32[1,3072]{1,0:T(1,128)S(1)}, f32[1,3072]{1,0:T(1,128)}, u32[]{:S(2)}) copy-start(f32[1,3072]{1,0:T(1,128)} %get-tuple-element.21) | copy-start | bytes 36868
  597.6 34.1 %all-to-all-start.3 = ((bf16[1,384,24]{2,0,1:T(2,128)(2,1)}), bf16[1,384,24]{2,0,1:T(2,128)(2,1)S(1)}, u32[]{:S(2)}, u32[]{:S(2)}) async-start(bf16[1,384,24]{2,0,1:T(2,128)(2,1)} %copy.119), calls=%async_computation.3 | async-start | bytes 393216 | tf_op jit(solution)/shard_map/all_to_all | solution.py:191
  619.8 13.7 %collective-permute-start.5 = (bf16[1,3,3072]{2,0,1:T(2,128)(2,1)S(1)}, bf16[1,3,3072]{2,0,1:T(2,128)(2,1)S(1)}, u32[]{:S(2)}, u32[]{:S(2)}) collective-permute-start(bf16[1,3,3072]{2,0,1:T(2,128)(2,1)S(1)} %get-tuple-element.6), channel_id=1, source_target_pairs={{128,0},{129,1},{130,2},{131,3},{132,4},{133,5},{134,6},{135,7},{1... | collective-permute-start | bytes 55304 | tf_op jit(solution)/shard_map/ppermute | solution.py:241
  632.2 5.5 collective-permute-start.6

commit v6 on v5

--- a/solution.py
+++ b/solution.py
@@ -117,6 +117,75 @@
     return jnp.swapaxes(out, 0, 1).reshape((n,) + x.shape)
 
 
+def exchange_kernel(n, x_ref, o_ref, send_sem, recv_sem, local_sem):
+    sec = lax.axis_index("section")
+    me = lax.axis_index("blk")
+    barrier = pltpu.get_barrier_semaphore()
+
+    def greet(i, carry):
+        peer = lax.rem(me + 1 + i, n)
+        pl.semaphore_signal(barrier, inc=1, device_id=(sec, peer), device_id_type=MESH)
+        return carry
+
+    lax.fori_loop(0, n - 1, greet, 0)
+    pl.semaphore_wait(barrier, n - 1)
+    local = pltpu.make_async_copy(x_ref.at[me], o_ref.at[me], local_sem)
+    local.start()
+
+    def remote(i, dst_slot):
+        peer = lax.rem(me + 1 + i, n)
+        return pltpu.make_async_remote_copy(
+            src_ref=x_ref.at[peer],
+            dst_ref=o_ref.at[dst_slot],
+            send_sem=send_sem.at[i],
+            recv_sem=recv_sem.at[dst_slot],
+            device_id=(sec, peer),
+            device_id_type=MESH,
+        )
+
+    def send(i, carry):
+        remote(i, me).start()
+        return carry
+
+    lax.fori_loop(0, n - 1, send, 0)
+
+    def finish(i, carry):
+        remote(i, me).wait_send()
+        remote(i, lax.rem(me + n - 1 - i, n)).wait_recv()
+        return carry
+
+    lax.fori_loop(0, n - 1, finish, 0)
+    local.wait()
+
+
+def exchange_blk(x, cid):
+    n = x.shape[0]
+    return pl.pallas_call(
+        functools.partial(exchange_kernel, n),
+        out_shape=jax.ShapeDtypeStruct(x.shape, x.dtype),
+        in_specs=[pl.BlockSpec(memory_space=pl.ANY)],
+        out_specs=pl.BlockSpec(memory_space=pl.ANY),
+        scratch_shapes=[
+            pltpu.SemaphoreType.DMA((n,)),
+            pltpu.SemaphoreType.DMA((n,)),
+            pltpu.SemaphoreType.DMA,
+        ],
+        compiler_params=pltpu.CompilerParams(collective_id=cid, has_side_effects=True),
+    )(x)
+
+
+def cols_to_rows(columns, cid):
+    n = lax.axis_size("blk")
+    _, total, cols = columns.shape
+    rows = total // n
+    pieces = columns.reshape(n, rows, cols)
+    pr = -(-rows // 16) * 16
+    pc = -(-cols // 128) * 128
+    pieces = jnp.pad(pieces, ((0, 0), (0, pr - rows), (0, pc - cols)))
+    got = exchange_blk(pieces, cid)[:, :rows, :cols]
+    return jnp.transpose(got, (1, 0, 2)).reshape(1, rows, n * cols)
+
+
 def gather_rows(x, cid, active):
     n = lax.axis_size("blk")
     _, rows, width = x.shape
@@ -146,7 +215,7 @@
         qkv_cols,
         preferred_element_type=jnp.float32,
     ).astype(jnp.bfloat16)
-    projected = lax.all_to_all(columns, "blk", split_axis=1, concat_axis=2, tiled=True)
+    projected = cols_to_rows(columns, 8)
     num_req, num_rows, width = layer_in.shape
     queries = projected[:, :, :width]
     new_keys = projected[:, :, width : 2 * width]
@@ -188,7 +257,7 @@
         out_cols,
         preferred_element_type=jnp.float32,
     ).astype(jnp.bfloat16)
-    mixed_back = lax.all_to_all(out_part, "blk", split_axis=1, concat_axis=2, tiled=True)
+    mixed_back = cols_to_rows(out_part, 9)
     return (stream + modulate[2] * mixed_back.astype(jnp.float32)).astype(jnp.bfloat16)
 
 

time: 640 us -> 685 us (1.070)
  Pallas kernels: 391 us -> 556 us
  starting transfers between devices: 66.4 us -> 11.7 us
  blocking collectives: 34.1 us -> 0 us
  waiting for transfers between devices: 33.3 us -> 0.84 us
    pallas_call x0 -> x4, Pallas kernels: none -> 126 us  [exchange_blk(): pl.pallas_call(functools.partial(exchange_kernel, n), out_shape=jax.Shape...]
    all_to_all x3 -> x0, starting transfers between devices: 56.3 us -> none  [the longest x2 34.1 us: attend(): lax.all_to_all(columns, 'blk', split_axis=1, concat_axis=2, tiled=True)]
    pallas_call x6, Pallas kernels: 391 us -> 430 us  [gather_blk(): pl.pallas_call(functools.partial(gather_kernel, n, active), out_shape=jax...]
    all_to_all x1 -> x0, blocking collectives: 34.1 us -> none  [attend(): lax.all_to_all(out_part, 'blk', split_axis=1, concat_axis=2, tiled=True)]
    all_to_all x3 -> x0, waiting for transfers between devices: 29.2 us -> none  [the longest x2 21.6 us: attend(): lax.all_to_all(columns, 'blk', split_axis=1, concat_axis=2, tiled=True)]
  transfers between devices with their start and end apart: 10 -> 7, of which waited for: 4 -> 1; matrix products, arithmetic and copies ran while one was open for 9% -> 8% of each run, Pallas kernels for 32% -> 36%
where the time goes in v6:
time: 685 us; the launch traced here: 683 us
  Pallas kernels  556 us (81%)
  local copies, waits for them, and re-layouts  90.4 us (13%)
  matrix products  14.8 us (2%)
  starting transfers between devices  11.7 us (2%)
    pallas_call x6, Pallas kernels, gather_blk(): pl.pallas_call(functools.partial(gather_kernel, n, active), out_shape=jax...  430 us
    pallas_call x4, Pallas kernels, exchange_blk(): pl.pallas_call(functools.partial(exchange_kernel, n), out_shape=jax.Shape...  126 us
    transpose x6, local copies, waits for them, and re-layouts, gather_blk(): return jnp.swapaxes(out, 0, 1).reshape((n,) + x.shape)  17.3 us
    slice x4, local copies, waits for them, and re-layouts, attend(): key_piece = kv_piece[:, :, :width]  15.8 us
    another operation x2, local copies, waits for them, and re-layouts, gather_rows(): return out.reshape(1, n * rows, width)  15.3 us
  transfers between devices with their start and end apart: 7, of which 1 were waited for; matrix products, arithmetic and copies ran while one was open for 8% of the time, Pallas kernels for 36%

profile of v6, /device:TPU:1, one launch (start us, length us, event | category | flops | bytes accessed | tf_op | source)
XLA Modules:
  0.0 683.5 jit_solution(5472034078975330650)
XLA Ops:
  3.1 3.3 collective-permute-start
  15.2 53.9 %shard_map.91 = bf16[16,8,80,128]{3,2,1,0:T(8,128)(2,1)} custom-call(bf16[80,128]{1,0:T(8,128)(2,1)} %pad_bitcast_fusion.3.x_ref), custom_call_target="tpu_custom_call" | custom-call | tf_op jit(solution)/shard_map/pallas_call | solution.py:103
  73.4 3.3 reshape.425
  78.6 27.5 %shard_map.92 = bf16[128,16,128]{2,1,0:T(8,128)(2,1)} custom-call(bf16[128,16,128]{2,1,0:T(8,128)(2,1)} %pad.28.x_ref), custom_call_target="tpu_custom_call" | custom-call | tf_op jit(solution)/shard_map/pallas_call | solution.py:163
  108.1 78.5 %shard_map.93 = bf16[16,8,144,128]{3,2,1,0:T(8,128)(2,1)} custom-call(bf16[144,128]{1,0:T(8,128)(2,1)} %reshape.429.x_ref), custom_call_target="tpu_custom_call" | custom-call | tf_op jit(solution)/shard_map/pallas_call | solution.py:103
  186.6 4.8 copy.24
  191.4 7.6 %reshape_reshape_reshape.6 = bf16[1,384,6144]{2,1,0:T(8,128)(2,1)} reshape(bf16[8,16,144,128]{3,2,1,0:T(8,128)(2,1)} %copy.24) | data formatting | bytes 9437184 | tf_op jit(solution)/shard_map/reshape;reshape;reshape | solution.py:197
  199.0 4.9 fusion.63
  212.5 3.6 fusion.8
  216.8 84.5 %shard_map.94 = bf16[16,8,80,128]{3,2,1,0:T(8,128)(2,1)} custom-call(bf16[80,128]{1,0:T(8,128)(2,1)} %pad_bitcast_fusion.2.x_ref), custom_call_target="tpu_custom_call" | custom-call | tf_op jit(solution)/shard_map/pallas_call | solution.py:103
  305.6 3.2 reshape.433
  311.6 28.8 %shard_map.95 = bf16[128,16,128]{2,1,0:T(8,128)(2,1)} custom-call(bf16[128,16,128]{2,1,0:T(8,128)(2,1)} %pad.30.x_ref), custom_call_target="tpu_custom_call" | custom-call | tf_op jit(solution)/shard_map/pallas_call | solution.py:163
  342.6 45.3 %shard_map.96 = bf16[16,8,80,128]{3,2,1,0:T(8,128)(2,1)} custom-call(bf16[80,128]{1,0:T(8,128)(2,1)} %pad_bitcast_fusion.1.x_ref), custom_call_target="tpu_custom_call" | custom-call | tf_op jit(solution)/shard_map/pallas_call | solution.py:103
  392.1 3.2 reshape.437
  397.3 36.5 %shard_map.97 = bf16[128,16,128]{2,1,0:T(8,128)(2,1)} custom-call(bf16[128,16,128]{2,1,0:T(8,128)(2,1)} %pad.32.x_ref), custom_call_target="tpu_custom_call" | custom-call | tf_op jit(solution)/shard_map/pallas_call | solution.py:163
  435.7 78.8 %shard_map.98 = bf16[16,8,144,128]{3,2,1,0:T(8,128)(2,1)} custom-call(bf16[144,128]{1,0:T(8,128)(2,1)} %reshape.441.x_ref), custom_call_target="tpu_custom_call" | custom-call | tf_op jit(solution)/shard_map/pallas_call | solution.py:103
  514.5 4.8 copy.35
  519.3 7.6 %reshape_reshape_reshape.7 = bf16[1,384,6144]{2,1,0:T(8,128)(2,1)} reshape(bf16[8,16,144,128]{3,2,1,0:T(8,128)(2,1)} %copy.35) | data formatting | bytes 9437184 | tf_op jit(solution)/shard_map/reshape;reshape;reshape | solution.py:197
  527.0 4.9 fusion.62
  535.6 3.0 copy.38
  542.2 89.2 %shard_map.99 = bf16[16,8,80,128]{3,2,1,0:T(8,128)(2,1)} custom-call(bf16[80,128]{1,0:T(8,128)(2,1)} %pad_bitcast_fusion.x_ref), custom_call_target="tpu_custom_call" | custom-call | tf_op jit(solution)/shard_map/pallas_call | solution.py:103
  635.5 3.2 reshape.445
  640.6 32.9 %shard_map.100 = bf16[128,16,128]{2,1,0:T(8,128)(2,1)} custom-call(bf16[128,16,128]{2,1,0:T(8,128)(2,1)} %pad.34.x_ref), custom_call_target="tpu_custom_call" | custom-call | tf_op jit(solution)/shard_map/pallas_call | solution.py:163
  676.0 5.9 collective-permute-start.5
  (132 shorter events, 60.4 us)
Async XLA Ops:
  0.0 8.7 %copy-start = (bf16[2,3,3072]{2,0,1:T(2,128)(2,1)S(1)}, bf16[2,3,3072]{2,0,1:T(2,128)(2,1)}, u32[]{:S(2)}) copy-start(bf16[2,3,3072]{2,0,1:T(2,128)(2,1)} %param.9) | copy-start | bytes 110596
  0.0 7.9 %copy-start.10 = (s32[1,2,128]{2,1,0:T(2,128)S(1)}, s32[1,2,128]{2,1,0:T(2,128)}, u32[]{:S(2)}) copy-start(s32[1,2,128]{2,1,0:T(2,128)} %param.14) | copy-start | bytes 3076
  0.0 8.2 %copy-start.3 = (bf16[1,3072,24]{1,2,0:T(8,128)(2,1)S(1)}, bf16[1,3072,24]{1,2,0:T(8,128)(2,1)}, u32[]{:S(2)}) copy-start(bf16[1,3072,24]{1,2,0:T(8,128)(2,1)} %param.11) | copy-start | bytes 442372
  0.0 9.1 %copy-start.11 = (s32[2,128]{1,0:T(2,128)S(1)}, s32[2,128]{1,0:T(2,128)}, u32[]{:S(2)}) copy-start(s32[2,128]{1,0:T(2,128)} %param.15) | copy-start | bytes 3076
  3.1 10.0 %collective-permute-start = (f32[3,3072]{1,0:T(4,128)S(1)}, f32[3,3072]{1,0:T(4,128)S(1)}, u32[]{:S(2)}, u32[]{:S(2)}) collective-permute-start(f32[3,3072]{1,0:T(4,128)S(1)} %bitcast.154), channel_id=1, source_target_pairs={{0,128},{128,0},{1,129},{129,1},{2,130},{130,2},{3,131},{131,3},{4... | collective-permute-start | bytes 110600 | tf_op jit(solution)/shard_map/ppermute | solution.py:265
  6.5 70.2 %collective-permute-start.1 = (bf16[3072,72]{0,1:T(8,128)(2,1)}, bf16[3072,72]{0,1:T(8,128)(2,1)S(1)}, u32[]{:S(2)}, u32[]{:S(2)}) collective-permute-start(bf16[3072,72]{0,1:T(8,128)(2,1)} %bitcast.147), channel_id=1, source_target_pairs={{0,128},{128,0},{1,129},{129,1},{2,130},{130,2},{3,131},{131,3},{4... | collective-permute-start | bytes 1327112 | tf_op jit(solution)/shard_map/ppermute | solution.py:265
  7.4 6.4 collective-permute-start.3
  8.1 1.9 collective-permute-start.2
  8.2 300.6 %collective-permute-start.4 = (bf16[3072,24]{0,1:T(8,128)(2,1)S(1)}, bf16[3072,24]{0,1:T(8,128)(2,1)}, u32[]{:S(2)}, u32[]{:S(2)}) collective-permute-start(bf16[3072,24]{0,1:T(8,128)(2,1)S(1)} %bitcast.149), channel_id=1, source_target_pairs={{0,128},{128,0},{1,129},{129,1},{2,130},{130,2},{3,131},{131,3},{4... | collective-permute-start | bytes 442376 | tf_op jit(solution)/shard_map/ppermute | solution.py:265
  73.4 3.3 copy-start.2
  77.5 29.8 %copy-start.5 = (bf16[1,3,6144]{2,1,0:T(4,128)(2,1)S(1)}, bf16[1,3,6144]{2,1,0:T(4,128)(2,1)}, u32[]{:S(2)}) copy-start(bf16[1,3,6144]{2,1,0:T(4,128)(2,1)} %get-tuple-element.12) | copy-start | bytes 110596
  308.8 32.7 %copy-start.9 = (f32[1,3072]{1,0:T(1,128)S(1)}, f32[1,3072]{1,0:T(1,128)}, u32[]{:S(2)}) copy-start(f32[1,3072]{1,0:T(1,128)} %get-tuple-element.35) | copy-start | bytes 36868
  308.8 33.1 %copy-start.7 = (f32[1,3072]{1,0:T(1,128)S(1)}, f32[1,3072]{1,0:T(1,128)}, u32[]{:S(2)}) copy-start(f32[1,3072]{1,0:T(1,128)} %get-tuple-element.22) | copy-start | bytes 36868
  308.8 33.1 %copy-start.8 = (f32[1,3072]{1,0:T(1,128)S(1)}, f32[1,3072]{1,0:T(1,128)}, u32[]{:S(2)}) copy-start(f32[1,3072]{1,0:T(1,128)} %get-tuple-element.23) | copy-start | bytes 36868
  396.2 38.8 %copy-start.4 = (bf16[1,3,6144]{2,1,0:T(4,128)(2,1)S(1)}, bf16[1,3,6144]{2,1,0:T(4,128)(2,1)}, u32[]{:S(2)}) copy-start(bf16[1,3,6144]{2,1,0:T(4,128)(2,1)} %get-tuple-element.11) | copy-start | bytes 110596
  638.8 35.9 %copy-start.6 = (f32[1,3072]{1,0:T(1,128)S(1)}, f32[1,3072]{1,0:T(1,128)}, u32[]{:S(2)}) copy-start(f32[1,3072]{1,0:T(1,128)} %get-tuple-element.21) | copy-start | bytes 36868
  638.8 44.7 %copy-start.1 = (bf16[2,3,3072]{2,0,1:T(2,128)(2,1)S(1)}, bf16[2,3,3072]{2,0,1:T(2,128)(2,1)}, u32[]{:S(2)}) copy-start(bf16[2,3,3072]{2,0,1:T(2,128)(2,1)} %param.9) | copy-start | bytes 110596
  674.7 7.2 %collective-permute-start.6 = (bf16[1,3,3072]{2,1,0:T(4,128)(2,1)S(1)}, bf16[1,3,3072]{2,1,0:T(4,128)(2,1)S(1)}, u32[]{:S(2)}, u32[]{:S(2)}) collective-permute-start(bf16[1,3,3072]{2,1,0:T(4,128)(2,1)S(1)} %fusion.39), channel_id=1, source_target_pairs={{0,128},{1,129},{2,130},{3,131},{4,132},{5,133},{6,134},{7,135},{8... | collective-permute-start | bytes 55304 | tf_op jit(solution)/shard_map/ppermute | solution.py:311
  676.0 6.7 collective-permute-start.5

commit v7 on v5

--- a/solution.py
+++ b/solution.py
@@ -114,7 +114,7 @@
         ],
         compiler_params=pltpu.CompilerParams(collective_id=cid, has_side_effects=True),
     )(x)
-    return jnp.swapaxes(out, 0, 1).reshape((n,) + x.shape)
+    return out.reshape((n,) + x.shape)
 
 
 def gather_rows(x, cid, active):
@@ -123,9 +123,28 @@
     size = rows * width
     tile = 16 * 128
     padded = -(-size // tile) * tile
-    flat = jnp.pad(x.reshape(size), (0, padded - size)).reshape(padded // 128, 128)
-    out = gather_blk(flat, n, cid + (0 if active is None else 2 + active) * 2, active).reshape(n, padded)[:, :size]
-    return out.reshape(1, n * rows, width)
+    flat = x.reshape(size)
+    if padded != size:
+        flat = jnp.pad(flat, (0, padded - size))
+    flat = flat.reshape(padded // 128, 128)
+    cid = cid + (0 if active is None else 2 + active) * 2
+    out = gather_blk(flat, n, cid, active).reshape(n, padded)
+    if padded != size:
+        out = out[:, :size]
+    return out.reshape(n * rows, width)
+
+
+def to_blk_order(rows_in_gather_order, n):
+    total, cols = rows_in_gather_order.shape
+    nz = n // PLANE
+    parts = rows_in_gather_order.reshape(PLANE, nz, total // n, cols)
+    return jnp.swapaxes(parts, 0, 1).reshape(1, total, cols)
+
+
+def blk_of_gather_slot(n):
+    nz = n // PLANE
+    slot = jnp.arange(n)
+    return (slot % nz) * PLANE + slot // nz
 
 
 def from_behind(shard, axis, by):
@@ -135,60 +154,46 @@
 
 
 def attend(layer_in, qkv_cols, out_cols, modulate, fresh_own, old_keys, old_values, live, active):
+    n = lax.axis_size("blk")
     stream = layer_in.astype(jnp.float32)
     center = jnp.mean(stream, axis=-1, keepdims=True)
     variance = jnp.mean((stream - center) ** 2, axis=-1, keepdims=True)
     normed = (stream - center) / jnp.sqrt(variance + 1e-06) * (1.0 + modulate[0]) + modulate[1]
     normed_b = normed.astype(jnp.bfloat16)
-    columns = jnp.einsum(
-        "rnd,dc->rnc",
-        gather_rows(normed_b, 0, active),
-        qkv_cols,
-        preferred_element_type=jnp.float32,
+    columns = jnp.dot(
+        gather_rows(normed_b, 0, active), qkv_cols, preferred_element_type=jnp.float32
     ).astype(jnp.bfloat16)
-    projected = lax.all_to_all(columns, "blk", split_axis=1, concat_axis=2, tiled=True)
+    projected = lax.all_to_all(to_blk_order(columns, n), "blk", split_axis=1, concat_axis=2, tiled=True)
     num_req, num_rows, width = layer_in.shape
-    queries = projected[:, :, :width]
+    queries = projected[0, :, :width]
     new_keys = projected[:, :, width : 2 * width]
     new_values = projected[:, :, 2 * width :]
     use_fresh = (fresh_own == 1)[:, None, None]
     keys = jnp.where(use_fresh, new_keys, old_keys)
     values = jnp.where(use_fresh, new_values, old_values)
+    kv_all = gather_rows(jnp.concatenate([keys, values], axis=2), 1, active)
+    key_all = kv_all[:, :width]
+    value_all = kv_all[:, width:]
+    key_blk = jnp.repeat(blk_of_gather_slot(n), num_rows)
+    usable = (jnp.take(live[0], key_blk) == 1)[None, None, :]
     num_heads = width // 64
-    num_blocks = live.shape[1]
-    q_heads = queries.reshape(num_req, num_rows, num_heads, 64)
-    live_float = live.astype(jnp.float32)
-    run_max = jnp.full((num_req, num_heads, num_rows), -1e30, jnp.float32)
-    kv_piece = gather_rows(jnp.concatenate([keys, values], axis=2), 1, active)
-    key_piece = kv_piece[:, :, :width]
-    value_piece = kv_piece[:, :, width:]
-    piece_rows = key_piece.shape[1]
-    key_heads = key_piece.reshape(num_req, piece_rows, num_heads, 64)
-    value_heads = value_piece.reshape(num_req, piece_rows, num_heads, 64)
-    scores = (
-        jnp.einsum("qrhd,qnhd->qhrn", q_heads, key_heads, preferred_element_type=jnp.float32)
-        * 0.125
+    head_of_col = jnp.arange(width) // 64
+    in_head = head_of_col[None, :] == jnp.arange(num_heads)[:, None]
+    q_diag = jnp.where(in_head[None], queries[:, None, :], jnp.zeros((), queries.dtype))
+    scores = jnp.einsum("qhc,kc->qhk", q_diag, key_all, preferred_element_type=jnp.float32) * 0.125
+    scores = jnp.where(usable, scores, -1e30)
+    top = jnp.max(scores, axis=-1, keepdims=True)
+    weights = jnp.where(usable, jnp.exp(scores - top), 0.0)
+    total = jnp.sum(weights, axis=-1)
+    mixed_all = jnp.einsum(
+        "qhk,kc->qhc", weights, value_all.astype(jnp.float32), precision=lax.Precision.HIGHEST
     )
-    block_ids = jnp.arange(piece_rows) // num_rows
-    one_hot = (block_ids[:, None] == jnp.arange(num_blocks)[None, :]).astype(jnp.float32)
-    usable = jnp.einsum("qb,nb->qn", live_float, one_hot) > 0.5
-    usable = usable[:, None, None, :]
-    scores = jnp.where(usable, scores, -1e30)
-    new_max = jnp.maximum(run_max, jnp.max(scores, axis=-1))
-    weights = jnp.where(usable, jnp.exp(scores - new_max[..., None]), 0.0)
-    new_sum = jnp.sum(weights, axis=-1)
-    new_acc = jnp.einsum(
-        "qhrn,qnhd->qhrd", weights, value_heads.astype(jnp.float32), precision=lax.Precision.HIGHEST
-    )
-    attn = new_acc / new_sum[..., None]
-    attn = jnp.transpose(attn, (0, 2, 1, 3)).reshape(num_req, num_rows, width).astype(jnp.bfloat16)
-    out_part = jnp.einsum(
-        "rnd,dc->rnc",
-        gather_rows(attn, 0, active),
-        out_cols,
-        preferred_element_type=jnp.float32,
+    own_head = jnp.sum(jnp.where(in_head[None], mixed_all, 0.0), axis=1)
+    attn = (own_head / jnp.take(total, head_of_col, axis=1)).astype(jnp.bfloat16)[None]
+    out_part = jnp.dot(
+        gather_rows(attn, 0, active), out_cols, preferred_element_type=jnp.float32
     ).astype(jnp.bfloat16)
-    mixed_back = lax.all_to_all(out_part, "blk", split_axis=1, concat_axis=2, tiled=True)
+    mixed_back = lax.all_to_all(to_blk_order(out_part, n), "blk", split_axis=1, concat_axis=2, tiled=True)
     return (stream + modulate[2] * mixed_back.astype(jnp.float32)).astype(jnp.bfloat16)
 
 

time: 640 us -> 632 us (0.988)
  local copies, waits for them, and re-layouts: 87.7 us -> 77.4 us
    slice x10 -> x4, local copies, waits for them, and re-layouts: 28.1 us -> 6.38 us  [gather_rows(): out = out[:, :size]]
    gather x0 -> x5, local copies, waits for them, and re-layouts: none -> 19.9 us  [the longest x4 17.2 us: attend(): jnp.take(total, head_of_col, axis=1)]
    transpose x6 -> x4, local copies, waits for them, and re-layouts: 17.3 us -> 0.19 us  [to_blk_order(): return jnp.swapaxes(parts, 0, 1).reshape(1, total, cols)]
    reshape x8 -> x19, local copies, waits for them, and re-layouts: 3.85 us -> 18.4 us  [the longest x4 13 us: gather_rows(): return out.reshape(n * rows, width)]
    another operation x8 -> x6, local copies, waits for them, and re-layouts: 29.1 us -> 16.8 us  [the longest x2 15.4 us: gather_rows(): return out.reshape(n * rows, width)]
    unnamed x26 -> x40, local copies, waits for them, and re-layouts: 2.81 us -> 10.5 us
    dot_general x9 -> x8, matrix products: 13.2 us -> 13.6 us  [the longest x2 5.54 us: attend(): jnp.einsum('qhc,kc->qhk', q_diag, key_all, preferred_element_type=jnp.flo...]
  transfers between devices with their start and end apart: 10 -> 10, of which waited for: 4 -> 4; matrix products, arithmetic and copies ran while one was open for 9% -> 8% of each run, Pallas kernels for 32% -> 33%
where the time goes in v7:
time: 632 us; the launch traced here: 631 us
  Pallas kernels  391 us (62%)
  local copies, waits for them, and re-layouts  77.4 us (12%)
  starting transfers between devices  70.9 us (11%)
  waiting for transfers between devices  32.6 us (5%)
  blocking collectives  31.4 us (5%)
  matrix products  16 us (3%)
  other arithmetic  7.32 us (1%)
    pallas_call x6, Pallas kernels, gather_blk(): pl.pallas_call(functools.partial(gather_kernel, n, active), out_shape=jax...  391 us
    all_to_all x2, starting transfers between devices, attend(): lax.all_to_all(to_blk_order(columns, n), 'blk', split_axis=1, concat_axis...  36.3 us
    all_to_all x1, blocking collectives, attend(): lax.all_to_all(to_blk_order(out_part, n), 'blk', split_axis=1, concat_axi...  31.4 us
    all_to_all x1, starting transfers between devices, attend(): lax.all_to_all(to_blk_order(out_part, n), 'blk', split_axis=1, concat_axi...  23.8 us
    all_to_all x2, waiting for transfers between devices, attend(): lax.all_to_all(to_blk_order(columns, n), 'blk', split_axis=1, concat_axis...  20.9 us
    gather x4, local copies, waits for them, and re-layouts, attend(): jnp.take(total, head_of_col, axis=1)  17.2 us
    another operation x2, local copies, waits for them, and re-layouts, gather_rows(): return out.reshape(n * rows, width)  15.4 us
    reshape x4, local copies, waits for them, and re-layouts, gather_rows(): return out.reshape(n * rows, width)  13 us
  transfers between devices with their start and end apart: 10, of which 4 were waited for; matrix products, arithmetic and copies ran while one was open for 8% of the time, Pallas kernels for 33%

profile of v7, /device:TPU:1, one launch (start us, length us, event | category | flops | bytes accessed | tf_op | source)
XLA Modules:
  0.0 630.8 jit_solution(4358994765104088882)
XLA Ops:
  3.1 3.3 collective-permute-start
  18.1 54.0 %shard_map.91 = bf16[16,8,80,128]{3,2,1,0:T(8,128)(2,1)} custom-call(bf16[80,128]{1,0:T(8,128)(2,1)} %pad_bitcast_fusion.3.x_ref), custom_call_target="tpu_custom_call" | custom-call | tf_op jit(solution)/shard_map/pallas_call | solution.py:103
  76.0 3.3 reshape.339
  82.7 15.2 %all-to-all-start = ((bf16[1,384,72]{2,0,1:T(2,128)(2,1)}), bf16[1,384,72]{2,0,1:T(2,128)(2,1)S(1)}, u32[]{:S(2)}, u32[]{:S(2)}) async-start(bf16[1,384,72]{2,0,1:T(2,128)(2,1)} %reshape.398), calls=%async_computation | async-start | bytes 393216 | tf_op jit(solution)/shard_map/all_to_all | solution.py:166
  99.4 10.2 %all-to-all-done = bf16[1,384,72]{2,0,1:T(2,128)(2,1)S(1)} async-done(((bf16[1,384,72]{2,0,1:T(2,128)(2,1)}), bf16[1,384,72]{2,0,1:T(2,128)(2,1)S(1)}, u32[]{:S(2)}, u32[]{:S(2)}) %all-to-all-start) | async-done | bytes 55328 | tf_op jit(solution)/shard_map/all_to_all | solution.py:166
  111.3 76.6 %shard_map.92 = bf16[16,8,144,128]{3,2,1,0:T(8,128)(2,1)} custom-call(bf16[144,128]{1,0:T(8,128)(2,1)} %reshape_reshape.19.x_ref), custom_call_target="tpu_custom_call" | custom-call | tf_op jit(solution)/shard_map/pallas_call | solution.py:103
  187.9 7.7 %reshape_reshape_reshape.6 = bf16[384,6144]{1,0:T(8,128)(2,1)} reshape(bf16[16,8,144,128]{3,2,1,0:T(8,128)(2,1)} %shard_map.92) | data formatting | bytes 9437184 | tf_op jit(solution)/shard_map/reshape;reshape;reshape | solution.py:134
  200.5 8.1 %gather_fusion.1 = f32[3072,3]{1,0:T(8,128)S(1)} fusion(f32[3,48]{0,1:T(8,128)S(1)} %copy.101, s32[3072]{0:T(1024)S(1)} %fusion.42), kind=kCustom, calls=%fused_computation.1.clone | custom fusion | bytes 86016 | tf_op jit(solution)/shard_map/jit(_take)/gather | solution.py:192
  209.8 75.8 %shard_map.93 = bf16[16,8,80,128]{3,2,1,0:T(8,128)(2,1)} custom-call(bf16[80,128]{1,0:T(8,128)(2,1)} %pad_bitcast_fusion.2.x_ref), custom_call_target="tpu_custom_call" | custom-call | tf_op jit(solution)/shard_map/pallas_call | solution.py:103
  289.6 3.2 reshape.343
  294.9 31.4 %all_to_all.54 = bf16[1,384,24]{2,0,1:T(2,128)(2,1)S(1)} all-to-all(bf16[1,384,24]{2,0,1:T(2,128)(2,1)S(1)} %reshape.399), channel_id=1, replica_groups=mesh['section'=2,'blk'=128] {'blk'}, dimensions={1} | all-to-all | bytes 36864 | tf_op jit(solution)/shard_map/all_to_all | solution.py:196
  327.9 38.6 %shard_map.94 = bf16[16,8,80,128]{3,2,1,0:T(8,128)(2,1)} custom-call(bf16[80,128]{1,0:T(8,128)(2,1)} %pad_bitcast_fusion.1.x_ref), custom_call_target="tpu_custom_call" | custom-call | tf_op jit(solution)/shard_map/pallas_call | solution.py:103
  370.5 3.2 reshape.348
  375.7 21.0 %all-to-all-start.2 = ((bf16[1,384,72]{2,0,1:T(2,128)(2,1)}), bf16[1,384,72]{2,0,1:T(2,128)(2,1)S(1)}, u32[]{:S(2)}, u32[]{:S(2)}) async-start(bf16[1,384,72]{2,0,1:T(2,128)(2,1)} %reshape.400), calls=%async_computation.2 | async-start | bytes 393216 | tf_op jit(solution)/shard_map/all_to_all | solution.py:166
  398.0 10.7 %all-to-all-done.2 = bf16[1,384,72]{2,0,1:T(2,128)(2,1)S(1)} async-done(((bf16[1,384,72]{2,0,1:T(2,128)(2,1)}), bf16[1,384,72]{2,0,1:T(2,128)(2,1)S(1)}, u32[]{:S(2)}, u32[]{:S(2)}) %all-to-all-start.2) | async-done | bytes 55328 | tf_op jit(solution)/shard_map/all_to_all | solution.py:166
  410.3 74.2 %shard_map.95 = bf16[16,8,144,128]{3,2,1,0:T(8,128)(2,1)} custom-call(bf16[144,128]{1,0:T(8,128)(2,1)} %reshape_reshape.22.x_ref), custom_call_target="tpu_custom_call" | custom-call | tf_op jit(solution)/shard_map/pallas_call | solution.py:103
  484.5 7.7 %reshape_reshape_reshape.7 = bf16[384,6144]{1,0:T(8,128)(2,1)} reshape(bf16[16,8,144,128]{3,2,1,0:T(8,128)(2,1)} %shard_map.95) | data formatting | bytes 9437184 | tf_op jit(solution)/shard_map/reshape;reshape;reshape | solution.py:134
  497.0 8.1 %gather_fusion.2 = f32[3072,3]{1,0:T(8,128)S(1)} fusion(f32[3,48]{0,1:T(8,128)S(1)} %copy.111, s32[3072]{0:T(1024)S(1)} %fusion.42), kind=kCustom, calls=%fused_computation.2.clone | custom fusion | bytes 86016 | tf_op jit(solution)/shard_map/jit(_take)/gather | solution.py:192
  506.3 72.2 %shard_map.96 = bf16[16,8,80,128]{3,2,1,0:T(8,128)(2,1)} custom-call(bf16[80,128]{1,0:T(8,128)(2,1)} %pad_bitcast_fusion.x_ref), custom_call_target="tpu_custom_call" | custom-call | tf_op jit(solution)/shard_map/pallas_call | solution.py:103
  582.6 3.2 reshape.352
  587.6 23.8 %all-to-all-start.3 = ((bf16[1,384,24]{2,0,1:T(2,128)(2,1)}), bf16[1,384,24]{2,0,1:T(2,128)(2,1)S(1)}, u32[]{:S(2)}, u32[]{:S(2)}) async-start(bf16[1,384,24]{2,0,1:T(2,128)(2,1)} %reshape.401), calls=%async_computation.3 | async-start | bytes 393216 | tf_op jit(solution)/shard_map/all_to_all | solution.py:196
  611.4 5.1 collective-permute-start.5
  616.5 6.9 %all-to-all-done.3 = bf16[1,384,24]{2,0,1:T(2,128)(2,1)S(1)} async-done(((bf16[1,384,24]{2,0,1:T(2,128)(2,1)}), bf16[1,384,24]{2,0,1:T(2,128)(2,1)S(1)}, u32[]{:S(2)}, u32[]{:S(2)}) %all-to-all-start.3) | async-done | bytes 18464 | tf_op jit(solution)/shard_map/all_to_all | solution.py:196
  625.2 4.9 collective-permute-done.6
  (151 shorter events, 58.5 us)
Async XLA Ops:
  0.0 10.2 %copy-start = (s32[2,128]{1,0:T(2,128)S(1)}, s32[2,128]{1,0:T(2,128)}, u32[]{:S(2)}) copy-start(s32[2,128]{1,0:T(2,128)} %param.19) | copy-start | bytes 3076
  0.0 9.1 %copy-start.15 = (s32[1,2,128]{2,1,0:T(2,128)S(1)}, s32[1,2,128]{2,1,0:T(2,128)}, u32[]{:S(2)}) copy-start(s32[1,2,128]{2,1,0:T(2,128)} %param.18) | copy-start | bytes 3076
  0.0 9.4 %copy-start.5 = (bf16[1,3072,24]{1,2,0:T(8,128)(2,1)S(1)}, bf16[1,3072,24]{1,2,0:T(8,128)(2,1)}, u32[]{:S(2)}) copy-start(bf16[1,3072,24]{1,2,0:T(8,128)(2,1)} %param.15) | copy-start | bytes 442372
  0.0 9.8 %copy-start.6 = (bf16[2,3,3072]{2,0,1:T(2,128)(2,1)S(1)}, bf16[2,3,3072]{2,0,1:T(2,128)(2,1)}, u32[]{:S(2)}) copy-start(bf16[2,3,3072]{2,0,1:T(2,128)(2,1)} %param.13) | copy-start | bytes 110596
  3.1 13.4 %collective-permute-start = (f32[3,3072]{1,0:T(4,128)S(1)}, f32[3,3072]{1,0:T(4,128)S(1)}, u32[]{:S(2)}, u32[]{:S(2)}) collective-permute-start(f32[3,3072]{1,0:T(4,128)S(1)} %bitcast.185), channel_id=1, source_target_pairs={{0,128},{128,0},{1,129},{129,1},{2,130},{130,2},{3,131},{131,3},{4... | collective-permute-start | bytes 110600 | tf_op jit(solution)/shard_map/ppermute | solution.py:201
  6.5 72.9 %collective-permute-start.1 = (bf16[3072,72]{0,1:T(8,128)(2,1)}, bf16[3072,72]{0,1:T(8,128)(2,1)S(1)}, u32[]{:S(2)}, u32[]{:S(2)}) collective-permute-start(bf16[3072,72]{0,1:T(8,128)(2,1)} %bitcast.171), channel_id=1, source_target_pairs={{0,128},{128,0},{1,129},{129,1},{2,130},{130,2},{3,131},{131,3},{4... | collective-permute-start | bytes 1327112 | tf_op jit(solution)/shard_map/ppermute | solution.py:201
  8.7 89.3 %collective-permute-start.3 = (bf16[1,3,6144]{2,1,0:T(4,128)(2,1)}, bf16[1,3,6144]{2,1,0:T(4,128)(2,1)}, u32[]{:S(2)}, u32[]{:S(2)}) collective-permute-start(bf16[1,3,6144]{2,1,0:T(4,128)(2,1)} %fusion.35), channel_id=1, source_target_pairs={{0,128},{128,0},{1,129},{129,1},{2,130},{130,2},{3,131},{131,3},{4... | collective-permute-start | bytes 110600 | tf_op jit(solution)/shard_map/ppermute | solution.py:201
  9.2 5.5 collective-permute-start.2
  9.4 283.5 %collective-permute-start.4 = (bf16[3072,24]{0,1:T(8,128)(2,1)S(1)}, bf16[3072,24]{0,1:T(8,128)(2,1)}, u32[]{:S(2)}, u32[]{:S(2)}) collective-permute-start(bf16[3072,24]{0,1:T(8,128)(2,1)S(1)} %bitcast.174), channel_id=1, source_target_pairs={{0,128},{128,0},{1,129},{129,1},{2,130},{130,2},{3,131},{131,3},{4... | collective-permute-start | bytes 442376 | tf_op jit(solution)/shard_map/ppermute | solution.py:201
  76.0 3.3 copy-start.4
  82.7 27.0 %all-to-all-start = ((bf16[1,384,72]{2,0,1:T(2,128)(2,1)}), bf16[1,384,72]{2,0,1:T(2,128)(2,1)S(1)}, u32[]{:S(2)}, u32[]{:S(2)}) async-start(bf16[1,384,72]{2,0,1:T(2,128)(2,1)} %reshape.398), calls=%async_computation | async-start | bytes 393216 | tf_op jit(solution)/shard_map/all_to_all | solution.py:166
  187.9 7.8 %copy-start.9 = (pred[48,3072]{1,0:T(8,128)(4,1)S(1)}, pred[48,3072]{1,0:T(8,128)(4,1)}, u32[]{:S(2)}) copy-start(pred[48,3072]{1,0:T(8,128)(4,1)} %iota_compare_fusion) | copy-start | bytes 442372
  195.7 3.0 copy-start.3
  292.8 33.8 %copy-start.14 = (f32[1,3072]{1,0:T(1,128)S(1)}, f32[1,3072]{1,0:T(1,128)}, u32[]{:S(2)}) copy-start(f32[1,3072]{1,0:T(1,128)} %get-tuple-element.33) | copy-start | bytes 36868
  292.8 34.2 %copy-start.11 = (f32[1,3072]{1,0:T(1,128)S(1)}, f32[1,3072]{1,0:T(1,128)}, u32[]{:S(2)}) copy-start(f32[1,3072]{1,0:T(1,128)} %get-tuple-element.20) | copy-start | bytes 36868
  292.8 34.2 %copy-start.12 = (f32[1,3072]{1,0:T(1,128)S(1)}, f32[1,3072]{1,0:T(1,128)}, u32[]{:S(2)}) copy-start(f32[1,3072]{1,0:T(1,128)} %get-tuple-element.21) | copy-start | bytes 36868
  373.8 35.8 %copy-start.8 = (bf16[1,3,6144]{2,1,0:T(4,128)(2,1)S(1)}, bf16[1,3,6144]{2,1,0:T(4,128)(2,1)}, u32[]{:S(2)}) copy-start(bf16[1,3,6144]{2,1,0:T(4,128)(2,1)} %get-tuple-element.9) | copy-start | bytes 110596
  375.7 33.0 %all-to-all-start.2 = ((bf16[1,384,72]{2,0,1:T(2,128)(2,1)}), bf16[1,384,72]{2,0,1:T(2,128)(2,1)S(1)}, u32[]{:S(2)}, u32[]{:S(2)}) async-start(bf16[1,384,72]{2,0,1:T(2,128)(2,1)} %reshape.400), calls=%async_computation.2 | async-start | bytes 393216 | tf_op jit(solution)/shard_map/all_to_all | solution.py:166
  484.5 7.7 %copy-start.10 = (pred[48,3072]{1,0:T(8,128)(4,1)S(1)}, pred[48,3072]{1,0:T(8,128)(4,1)}, u32[]{:S(2)}) copy-start(pred[48,3072]{1,0:T(8,128)(4,1)} %iota_compare_fusion) | copy-start | bytes 442372
  582.5 48.2 %copy-start.1 = (s32[2,128]{1,0:T(2,128)S(1)}, s32[2,128]{1,0:T(2,128)}, u32[]{:S(2)}) copy-start(s32[2,128]{1,0:T(2,128)} %param.19) | copy-start | bytes 3076
  585.8 38.0 %copy-start.13 = (f32[1,3072]{1,0:T(1,128)S(1)}, f32[1,3072]{1,0:T(1,128)}, u32[]{:S(2)}) copy-start(f32[1,3072]{1,0:T(1,128)} %get-tuple-element.19) | copy-start | bytes 36868
  587.6 35.8 %all-to-all-start.3 = ((bf16[1,384,24]{2,0,1:T(2,128)(2,1)}), bf16[1,384,24]{2,0,1:T(2,128)(2,1)S(1)}, u32[]{:S(2)}, u32[]{:S(2)}) async-start(bf16[1,384,24]{2,0,1:T(2,128)(2,1)} %reshape.401), calls=%async_computation.3 | async-start | bytes 393216 | tf_op jit(solution)/shard_map/all_to_all | solution.py:196
  611.4 13.7 %collective-permute-start.5 = (bf16[1,3,3072]{2,0,1:T(2,128)(2,1)S(1)}, bf16[1,3,3072]{2,0,1:T(2,128)(2,1)S(1)}, u32[]{:S(2)}, u32[]{:S(2)}) collective-permute-start(bf16[1,3,3072]{2,0,1:T(2,128)(2,1)S(1)} %get-tuple-element.8), channel_id=1, source_target_pairs={{128,0},{129,1},{130,2},{131,3},{132,4},{133,5},{134,6},{135,7},{1... | collective-permute-start | bytes 55304 | tf_op jit(solution)/shard_map/ppermute | solution.py:246
  623.8 6.2 collective-permute-start.6
  (2 other events, 3.7 us)

commit v8 on v7

--- a/solution.py
+++ b/solution.py
@@ -139,12 +139,6 @@
     nz = n // PLANE
     parts = rows_in_gather_order.reshape(PLANE, nz, total // n, cols)
     return jnp.swapaxes(parts, 0, 1).reshape(1, total, cols)
-
-
-def blk_of_gather_slot(n):
-    nz = n // PLANE
-    slot = jnp.arange(n)
-    return (slot % nz) * PLANE + slot // nz
 
 
 def from_behind(shard, axis, by):
@@ -174,8 +168,9 @@
     kv_all = gather_rows(jnp.concatenate([keys, values], axis=2), 1, active)
     key_all = kv_all[:, :width]
     value_all = kv_all[:, width:]
-    key_blk = jnp.repeat(blk_of_gather_slot(n), num_rows)
-    usable = (jnp.take(live[0], key_blk) == 1)[None, None, :]
+    nz = n // PLANE
+    live_by_slot = jnp.swapaxes(live[0].reshape(nz, PLANE), 0, 1).reshape(n)
+    usable = (jnp.repeat(live_by_slot, num_rows) == 1)[None, None, :]
     num_heads = width // 64
     head_of_col = jnp.arange(width) // 64
     in_head = head_of_col[None, :] == jnp.arange(num_heads)[:, None]
@@ -189,7 +184,8 @@
         "qhk,kc->qhc", weights, value_all.astype(jnp.float32), precision=lax.Precision.HIGHEST
     )
     own_head = jnp.sum(jnp.where(in_head[None], mixed_all, 0.0), axis=1)
-    attn = (own_head / jnp.take(total, head_of_col, axis=1)).astype(jnp.bfloat16)[None]
+    total_col = jnp.broadcast_to(total[:, :, None], (num_rows, num_heads, 64)).reshape(num_rows, width)
+    attn = (own_head / total_col).astype(jnp.bfloat16)[None]
     out_part = jnp.dot(
         gather_rows(attn, 0, active), out_cols, preferred_element_type=jnp.float32
     ).astype(jnp.bfloat16)

time: 632 us -> 613 us (0.970)
  local copies, waits for them, and re-layouts: 77.4 us -> 57.9 us
    gather x5 -> x0, local copies, waits for them, and re-layouts: 19.9 us -> none  [the longest x4 17.2 us: attend(): jnp.take(total, head_of_col, axis=1)]
  transfers between devices with their start and end apart: 10 -> 10, of which waited for: 4 -> 4; matrix products, arithmetic and copies ran while one was open for 8% -> 7% of each run, Pallas kernels for 33% -> 33%
where the time goes in v8:
time: 613 us; the launch traced here: 612 us
  Pallas kernels  391 us (64%)
  starting transfers between devices  69.6 us (11%)
  local copies, waits for them, and re-layouts  57.9 us (9%)
  blocking collectives  33.8 us (6%)
  waiting for transfers between devices  32.6 us (5%)
  matrix products  16 us (3%)
  other arithmetic  7.18 us (1%)
    pallas_call x6, Pallas kernels, gather_blk(): pl.pallas_call(functools.partial(gather_kernel, n, active), out_shape=jax...  391 us
    all_to_all x2, starting transfers between devices, attend(): lax.all_to_all(to_blk_order(columns, n), 'blk', split_axis=1, concat_axis...  37.4 us
    all_to_all x1, blocking collectives, attend(): lax.all_to_all(to_blk_order(out_part, n), 'blk', split_axis=1, concat_axi...  33.8 us
    all_to_all x1, starting transfers between devices, attend(): lax.all_to_all(to_blk_order(out_part, n), 'blk', split_axis=1, concat_axi...  21.4 us
    all_to_all x2, waiting for transfers between devices, attend(): lax.all_to_all(to_blk_order(columns, n), 'blk', split_axis=1, concat_axis...  20.9 us
    another operation x2, local copies, waits for them, and re-layouts, gather_rows(): return out.reshape(n * rows, width)  15.4 us
    reshape x4, local copies, waits for them, and re-layouts, gather_rows(): return out.reshape(n * rows, width)  13 us
  transfers between devices with their start and end apart: 10, of which 4 were waited for; matrix products, arithmetic and copies ran while one was open for 7% of the time, Pallas kernels for 33%

profile of v8, /device:TPU:1, one launch (start us, length us, event | category | flops | bytes accessed | tf_op | source)
XLA Modules:
  0.0 611.7 jit_solution(8238034837592216345)
XLA Ops:
  3.1 3.3 collective-permute-start
  15.5 54.0 %shard_map.91 = bf16[16,8,80,128]{3,2,1,0:T(8,128)(2,1)} custom-call(bf16[80,128]{1,0:T(8,128)(2,1)} %pad_bitcast_fusion.3.x_ref), custom_call_target="tpu_custom_call" | custom-call | tf_op jit(solution)/shard_map/pallas_call | solution.py:103
  73.5 3.3 reshape.350
  80.1 15.3 %all-to-all-start = ((bf16[1,384,72]{2,0,1:T(2,128)(2,1)}), bf16[1,384,72]{2,0,1:T(2,128)(2,1)S(1)}, u32[]{:S(2)}, u32[]{:S(2)}) async-start(bf16[1,384,72]{2,0,1:T(2,128)(2,1)} %reshape.378), calls=%async_computation | async-start | bytes 393216 | tf_op jit(solution)/shard_map/all_to_all | solution.py:160
  96.9 10.2 %all-to-all-done = bf16[1,384,72]{2,0,1:T(2,128)(2,1)S(1)} async-done(((bf16[1,384,72]{2,0,1:T(2,128)(2,1)}), bf16[1,384,72]{2,0,1:T(2,128)(2,1)S(1)}, u32[]{:S(2)}, u32[]{:S(2)}) %all-to-all-start) | async-done | bytes 55328 | tf_op jit(solution)/shard_map/all_to_all | solution.py:160
  108.7 76.6 %shard_map.92 = bf16[16,8,144,128]{3,2,1,0:T(8,128)(2,1)} custom-call(bf16[144,128]{1,0:T(8,128)(2,1)} %reshape_reshape.19.x_ref), custom_call_target="tpu_custom_call" | custom-call | tf_op jit(solution)/shard_map/pallas_call | solution.py:103
  185.4 7.7 %reshape_reshape_reshape.6 = bf16[384,6144]{1,0:T(8,128)(2,1)} reshape(bf16[16,8,144,128]{3,2,1,0:T(8,128)(2,1)} %shard_map.92) | data formatting | bytes 9437184 | tf_op jit(solution)/shard_map/reshape;reshape;reshape | solution.py:134
  193.1 2.8 fusion.55
  198.7 73.5 %shard_map.93 = bf16[16,8,80,128]{3,2,1,0:T(8,128)(2,1)} custom-call(bf16[80,128]{1,0:T(8,128)(2,1)} %pad_bitcast_fusion.2.x_ref), custom_call_target="tpu_custom_call" | custom-call | tf_op jit(solution)/shard_map/pallas_call | solution.py:103
  276.2 3.2 reshape.355
  281.5 33.8 %all_to_all.54 = bf16[1,384,24]{2,0,1:T(2,128)(2,1)S(1)} all-to-all(bf16[1,384,24]{2,0,1:T(2,128)(2,1)S(1)} %reshape.379), channel_id=1, replica_groups=mesh['section'=2,'blk'=128] {'blk'}, dimensions={1} | all-to-all | bytes 36864 | tf_op jit(solution)/shard_map/all_to_all | solution.py:192
  317.0 38.1 %shard_map.94 = bf16[16,8,80,128]{3,2,1,0:T(8,128)(2,1)} custom-call(bf16[80,128]{1,0:T(8,128)(2,1)} %pad_bitcast_fusion.1.x_ref), custom_call_target="tpu_custom_call" | custom-call | tf_op jit(solution)/shard_map/pallas_call | solution.py:103
  359.1 3.2 reshape.360
  364.3 22.1 %all-to-all-start.2 = ((bf16[1,384,72]{2,0,1:T(2,128)(2,1)}), bf16[1,384,72]{2,0,1:T(2,128)(2,1)S(1)}, u32[]{:S(2)}, u32[]{:S(2)}) async-start(bf16[1,384,72]{2,0,1:T(2,128)(2,1)} %reshape.380), calls=%async_computation.2 | async-start | bytes 393216 | tf_op jit(solution)/shard_map/all_to_all | solution.py:160
  387.6 10.7 %all-to-all-done.2 = bf16[1,384,72]{2,0,1:T(2,128)(2,1)S(1)} async-done(((bf16[1,384,72]{2,0,1:T(2,128)(2,1)}), bf16[1,384,72]{2,0,1:T(2,128)(2,1)S(1)}, u32[]{:S(2)}, u32[]{:S(2)}) %all-to-all-start.2) | async-done | bytes 55328 | tf_op jit(solution)/shard_map/all_to_all | solution.py:160
  399.9 74.6 %shard_map.95 = bf16[16,8,144,128]{3,2,1,0:T(8,128)(2,1)} custom-call(bf16[144,128]{1,0:T(8,128)(2,1)} %reshape_reshape.22.x_ref), custom_call_target="tpu_custom_call" | custom-call | tf_op jit(solution)/shard_map/pallas_call | solution.py:103
  474.6 7.7 %reshape_reshape_reshape.7 = bf16[384,6144]{1,0:T(8,128)(2,1)} reshape(bf16[16,8,144,128]{3,2,1,0:T(8,128)(2,1)} %shard_map.95) | data formatting | bytes 9437184 | tf_op jit(solution)/shard_map/reshape;reshape;reshape | solution.py:134
  482.3 2.8 fusion.56
  487.9 74.0 %shard_map.96 = bf16[16,8,80,128]{3,2,1,0:T(8,128)(2,1)} custom-call(bf16[80,128]{1,0:T(8,128)(2,1)} %pad_bitcast_fusion.x_ref), custom_call_target="tpu_custom_call" | custom-call | tf_op jit(solution)/shard_map/pallas_call | solution.py:103
  565.9 3.2 reshape.365
  570.9 21.4 %all-to-all-start.3 = ((bf16[1,384,24]{2,0,1:T(2,128)(2,1)}), bf16[1,384,24]{2,0,1:T(2,128)(2,1)S(1)}, u32[]{:S(2)}, u32[]{:S(2)}) async-start(bf16[1,384,24]{2,0,1:T(2,128)(2,1)} %reshape.381), calls=%async_computation.3 | async-start | bytes 393216 | tf_op jit(solution)/shard_map/all_to_all | solution.py:192
  592.3 5.1 collective-permute-start.5
  597.4 6.8 %all-to-all-done.3 = bf16[1,384,24]{2,0,1:T(2,128)(2,1)S(1)} async-done(((bf16[1,384,24]{2,0,1:T(2,128)(2,1)}), bf16[1,384,24]{2,0,1:T(2,128)(2,1)S(1)}, u32[]{:S(2)}, u32[]{:S(2)}) %all-to-all-start.3) | async-done | bytes 18464 | tf_op jit(solution)/shard_map/all_to_all | solution.py:192
  606.0 4.9 collective-permute-done.6
  (137 shorter events, 49.6 us)
Async XLA Ops:
  0.0 9.1 %copy-start.10 = (s32[1,2,128]{2,1,0:T(2,128)S(1)}, s32[1,2,128]{2,1,0:T(2,128)}, u32[]{:S(2)}) copy-start(s32[1,2,128]{2,1,0:T(2,128)} %param.14) | copy-start | bytes 3076
  0.0 9.4 %copy-start.3 = (bf16[1,3072,24]{1,2,0:T(8,128)(2,1)S(1)}, bf16[1,3072,24]{1,2,0:T(8,128)(2,1)}, u32[]{:S(2)}) copy-start(bf16[1,3072,24]{1,2,0:T(8,128)(2,1)} %param.11) | copy-start | bytes 442372
  0.0 9.8 %copy-start.4 = (bf16[2,3,3072]{2,0,1:T(2,128)(2,1)S(1)}, bf16[2,3,3072]{2,0,1:T(2,128)(2,1)}, u32[]{:S(2)}) copy-start(bf16[2,3,3072]{2,0,1:T(2,128)(2,1)} %param.9) | copy-start | bytes 110596
  0.0 11.5 %copy-start.11 = (s32[2,128]{1,0:T(2,128)S(1)}, s32[2,128]{1,0:T(2,128)}, u32[]{:S(2)}) copy-start(s32[2,128]{1,0:T(2,128)} %param.15) | copy-start | bytes 3076
  3.1 10.8 %collective-permute-start = (f32[3,3072]{1,0:T(4,128)S(1)}, f32[3,3072]{1,0:T(4,128)S(1)}, u32[]{:S(2)}, u32[]{:S(2)}) collective-permute-start(f32[3,3072]{1,0:T(4,128)S(1)} %bitcast.176), channel_id=1, source_target_pairs={{0,128},{128,0},{1,129},{129,1},{2,130},{130,2},{3,131},{131,3},{4... | collective-permute-start | bytes 110600 | tf_op jit(solution)/shard_map/ppermute | solution.py:197
  6.5 70.3 %collective-permute-start.1 = (bf16[3072,72]{0,1:T(8,128)(2,1)}, bf16[3072,72]{0,1:T(8,128)(2,1)S(1)}, u32[]{:S(2)}, u32[]{:S(2)}) collective-permute-start(bf16[3072,72]{0,1:T(8,128)(2,1)} %bitcast.162), channel_id=1, source_target_pairs={{0,128},{128,0},{1,129},{129,1},{2,130},{130,2},{3,131},{131,3},{4... | collective-permute-start | bytes 1327112 | tf_op jit(solution)/shard_map/ppermute | solution.py:197
  7.4 0.6 copy-start.5
  8.7 86.7 %collective-permute-start.3 = (bf16[1,3,6144]{2,1,0:T(4,128)(2,1)}, bf16[1,3,6144]{2,1,0:T(4,128)(2,1)}, u32[]{:S(2)}, u32[]{:S(2)}) collective-permute-start(bf16[1,3,6144]{2,1,0:T(4,128)(2,1)} %fusion.35), channel_id=1, source_target_pairs={{0,128},{128,0},{1,129},{129,1},{2,130},{130,2},{3,131},{131,3},{4... | collective-permute-start | bytes 110600 | tf_op jit(solution)/shard_map/ppermute | solution.py:197
  9.2 2.9 collective-permute-start.2
  9.4 270.1 %collective-permute-start.4 = (bf16[3072,24]{0,1:T(8,128)(2,1)S(1)}, bf16[3072,24]{0,1:T(8,128)(2,1)}, u32[]{:S(2)}, u32[]{:S(2)}) collective-permute-start(bf16[3072,24]{0,1:T(8,128)(2,1)S(1)} %bitcast.165), channel_id=1, source_target_pairs={{0,128},{128,0},{1,129},{129,1},{2,130},{130,2},{3,131},{131,3},{4... | collective-permute-start | bytes 442376 | tf_op jit(solution)/shard_map/ppermute | solution.py:197
  73.5 3.3 copy-start.2
  80.1 27.0 %all-to-all-start = ((bf16[1,384,72]{2,0,1:T(2,128)(2,1)}), bf16[1,384,72]{2,0,1:T(2,128)(2,1)S(1)}, u32[]{:S(2)}, u32[]{:S(2)}) async-start(bf16[1,384,72]{2,0,1:T(2,128)(2,1)} %reshape.378), calls=%async_computation | async-start | bytes 393216 | tf_op jit(solution)/shard_map/all_to_all | solution.py:160
  185.3 7.8 %copy-start.7 = (pred[48,3072]{1,0:T(8,128)(4,1)S(1)}, pred[48,3072]{1,0:T(8,128)(4,1)}, u32[]{:S(2)}) copy-start(pred[48,3072]{1,0:T(8,128)(4,1)} %iota_compare_fusion) | copy-start | bytes 442372
  193.1 3.0 copy-start.1
  279.4 36.3 %copy-start.9 = (f32[1,3072]{1,0:T(1,128)S(1)}, f32[1,3072]{1,0:T(1,128)}, u32[]{:S(2)}) copy-start(f32[1,3072]{1,0:T(1,128)} %get-tuple-element.31) | copy-start | bytes 36868
  362.4 36.8 %copy-start.6 = (bf16[1,3,6144]{2,1,0:T(4,128)(2,1)S(1)}, bf16[1,3,6144]{2,1,0:T(4,128)(2,1)}, u32[]{:S(2)}) copy-start(bf16[1,3,6144]{2,1,0:T(4,128)(2,1)} %get-tuple-element.7) | copy-start | bytes 110596
  364.3 34.0 %all-to-all-start.2 = ((bf16[1,384,72]{2,0,1:T(2,128)(2,1)}), bf16[1,384,72]{2,0,1:T(2,128)(2,1)S(1)}, u32[]{:S(2)}, u32[]{:S(2)}) async-start(bf16[1,384,72]{2,0,1:T(2,128)(2,1)} %reshape.380), calls=%async_computation.2 | async-start | bytes 393216 | tf_op jit(solution)/shard_map/all_to_all | solution.py:160
  474.6 7.7 %copy-start.8 = (pred[48,3072]{1,0:T(8,128)(4,1)S(1)}, pred[48,3072]{1,0:T(8,128)(4,1)}, u32[]{:S(2)}) copy-start(pred[48,3072]{1,0:T(8,128)(4,1)} %iota_compare_fusion) | copy-start | bytes 442372
  482.3 3.0 copy-start
  570.9 33.3 %all-to-all-start.3 = ((bf16[1,384,24]{2,0,1:T(2,128)(2,1)}), bf16[1,384,24]{2,0,1:T(2,128)(2,1)S(1)}, u32[]{:S(2)}, u32[]{:S(2)}) async-start(bf16[1,384,24]{2,0,1:T(2,128)(2,1)} %reshape.381), calls=%async_computation.3 | async-start | bytes 393216 | tf_op jit(solution)/shard_map/all_to_all | solution.py:192
  592.3 13.7 %collective-permute-start.5 = (bf16[1,3,3072]{2,0,1:T(2,128)(2,1)S(1)}, bf16[1,3,3072]{2,0,1:T(2,128)(2,1)S(1)}, u32[]{:S(2)}, u32[]{:S(2)}) collective-permute-start(bf16[1,3,3072]{2,0,1:T(2,128)(2,1)S(1)} %get-tuple-element.6), channel_id=1, source_target_pairs={{128,0},{129,1},{130,2},{131,3},{132,4},{133,5},{134,6},{135,7},{1... | collective-permute-start | bytes 55304 | tf_op jit(solution)/shard_map/ppermute | solution.py:242
  604.7 6.3 %collective-permute-start.6 = (bf16[1,3,3072]{2,0,1:T(2,128)(2,1)S(1)}, bf16[1,3,3072]{2,0,1:T(2,128)(2,1)S(1)}, u32[]{:S(2)}, u32[]{:S(2)}) collective-permute-start(bf16[1,3,3072]{2,0,1:T(2,128)(2,1)S(1)} %add_convert_fusion), channel_id=1, source_target_pairs={{0,128},{1,129},{2,130},{3,131},{4,132},{5,133},{6,134},{7,135},{8... | collective-permute-start | bytes 55304 | tf_op jit(solution)/shard_map/ppermute | solution.py:243

commit v9 on v8

--- a/solution.py
+++ b/solution.py
@@ -10,106 +10,110 @@
 MESH = pl.DeviceIdType.MESH
 
 
-PLANE = 16
-
-
-def gather_kernel(n, active, x_ref, o_ref, send1, recv1, send2, recv2, local_sem):
+NX = 4
+NY = 4
+PLANE = NX * NY
+
+
+def gather_kernel(n, x_ref, o_ref, zs, zr, xs, xr, ys, yr, local_sem):
     sec = lax.axis_index("section")
-    args = (n, sec, x_ref, o_ref, send1, recv1, send2, recv2, local_sem)
-    if active is None:
-        gather_body(*args)
-    else:
-        pl.when(sec == active)(lambda: gather_body(*args))
-
-
-def gather_body(n, sec, x_ref, o_ref, send1, recv1, send2, recv2, local_sem):
     nz = n // PLANE
     me = lax.axis_index("blk")
-    zme = me // PLANE
-    xy = me % PLANE
+    y = me % NY
+    x = (me // NY) % NX
+    z = me // PLANE
+
+    def dev(zz, xx, yy):
+        return (sec, (zz * NX + xx) * NY + yy)
+
+    xp, xm, x2 = (x + 1) % NX, (x + NX - 1) % NX, (x + 2) % NX
+    yp, ym, y2 = (y + 1) % NY, (y + NY - 1) % NY, (y + 2) % NY
     barrier = pltpu.get_barrier_semaphore()
 
     def z_peer(i):
-        return lax.rem(zme + 1 + i, nz)
-
-    def xy_peer(i):
-        return lax.rem(xy + 1 + i, PLANE)
+        return lax.rem(z + 1 + i, nz)
 
     def greet_z(i, carry):
-        pl.semaphore_signal(barrier, inc=1, device_id=(sec, z_peer(i) * PLANE + xy), device_id_type=MESH)
+        pl.semaphore_signal(barrier, inc=1, device_id=dev(z_peer(i), x, y), device_id_type=MESH)
         return carry
 
-    def greet_xy(i, carry):
-        pl.semaphore_signal(barrier, inc=1, device_id=(sec, zme * PLANE + xy_peer(i)), device_id_type=MESH)
-        return carry
-
     lax.fori_loop(0, nz - 1, greet_z, 0)
-    lax.fori_loop(0, PLANE - 1, greet_xy, 0)
-    pl.semaphore_wait(barrier, nz - 1 + PLANE - 1)
-
-    local = pltpu.make_async_copy(x_ref, o_ref.at[xy, zme], local_sem)
+    for target in (dev(z, xp, y), dev(z, xm, y), dev(z, x, yp), dev(z, x, ym)):
+        pl.semaphore_signal(barrier, inc=1, device_id=target, device_id_type=MESH)
+    pl.semaphore_wait(barrier, nz - 1 + 4)
+
+    local = pltpu.make_async_copy(x_ref, o_ref.at[y, x, z], local_sem)
     local.start()
 
-    def copy1(i, src_z):
+    def copy_z(i, src_z):
         return pltpu.make_async_remote_copy(
             src_ref=x_ref,
-            dst_ref=o_ref.at[xy, src_z],
-            send_sem=send1.at[i],
-            recv_sem=recv1.at[src_z],
-            device_id=(sec, z_peer(i) * PLANE + xy),
+            dst_ref=o_ref.at[y, x, src_z],
+            send_sem=zs.at[i],
+            recv_sem=zr.at[src_z],
+            device_id=dev(z_peer(i), x, y),
             device_id_type=MESH,
         )
 
-    def send1_step(i, carry):
-        copy1(i, zme).start()
+    def send_z(i, carry):
+        copy_z(i, z).start()
         return carry
 
-    lax.fori_loop(0, nz - 1, send1_step, 0)
-
-    def finish1(i, carry):
-        copy1(i, zme).wait_send()
-        copy1(i, lax.rem(zme + nz - 1 - i, nz)).wait_recv()
+    lax.fori_loop(0, nz - 1, send_z, 0)
+
+    def finish_z(i, carry):
+        copy_z(i, z).wait_send()
+        copy_z(i, lax.rem(z + nz - 1 - i, nz)).wait_recv()
         return carry
 
-    lax.fori_loop(0, nz - 1, finish1, 0)
+    lax.fori_loop(0, nz - 1, finish_z, 0)
     local.wait()
 
-    def copy2(i, src_xy):
-        return pltpu.make_async_remote_copy(
-            src_ref=o_ref.at[src_xy],
-            dst_ref=o_ref.at[src_xy],
-            send_sem=send2.at[i],
-            recv_sem=recv2.at[src_xy],
-            device_id=(sec, zme * PLANE + xy_peer(i)),
-            device_id_type=MESH,
-        )
-
-    def send2_step(i, carry):
-        copy2(i, xy).start()
-        return carry
-
-    lax.fori_loop(0, PLANE - 1, send2_step, 0)
-
-    def finish2(i, carry):
-        copy2(i, xy).wait_send()
-        copy2(i, lax.rem(xy + PLANE - 1 - i, PLANE)).wait_recv()
-        return carry
-
-    lax.fori_loop(0, PLANE - 1, finish2, 0)
-
-
-def gather_blk(x, n, cid, active):
+    def ring(block, send_sems, recv_sems, up, down, far, count, target_up, target_down):
+        def rcopy(ref, k, target):
+            return pltpu.make_async_remote_copy(
+                src_ref=ref, dst_ref=ref, send_sem=send_sems.at[k], recv_sem=recv_sems.at[k],
+                device_id=target, device_id_type=MESH,
+            )
+
+        mine_up = rcopy(block(None), 0, target_up)
+        mine_down = rcopy(block(None), 1, target_down)
+        mine_up.start()
+        mine_down.start()
+        mine_up.wait_send()
+        mine_down.wait_send()
+        rcopy(block(down), 0, target_down).wait_recv()
+        rcopy(block(up), 1, target_up).wait_recv()
+        half = count // 2
+        fwd_up = rcopy(block(down).at[pl.ds(0, half)], 2, target_up)
+        fwd_down = rcopy(block(up).at[pl.ds(half, count - half)], 3, target_down)
+        fwd_up.start()
+        fwd_down.start()
+        fwd_up.wait_send()
+        fwd_down.wait_send()
+        rcopy(block(far).at[pl.ds(0, half)], 2, target_down).wait_recv()
+        rcopy(block(far).at[pl.ds(half, count - half)], 3, target_up).wait_recv()
+
+    ring(lambda p: o_ref.at[y, x if p is None else p], xs, xr, xp, xm, x2, nz,
+         dev(z, xp, y), dev(z, xm, y))
+    ring(lambda p: o_ref.at[y if p is None else p], ys, yr, yp, ym, y2, NX,
+         dev(z, x, yp), dev(z, x, ym))
+
+
+def gather_blk(x, n, cid, active=None):
     nz = n // PLANE
     out = pl.pallas_call(
-        functools.partial(gather_kernel, n, active),
-        out_shape=jax.ShapeDtypeStruct((PLANE, nz) + x.shape, x.dtype),
+        functools.partial(gather_kernel, n),
+        out_shape=jax.ShapeDtypeStruct((NY, NX, nz) + x.shape, x.dtype),
         in_specs=[pl.BlockSpec(memory_space=pl.ANY)],
         out_specs=pl.BlockSpec(memory_space=pl.ANY),
         scratch_shapes=[
             pltpu.SemaphoreType.DMA((nz,)),
             pltpu.SemaphoreType.DMA((nz,)),
-            pltpu.SemaphoreType.DMA((PLANE,)),
-            pltpu.SemaphoreType.DMA((PLANE,)),
+            pltpu.SemaphoreType.DMA((4,)),
+            pltpu.SemaphoreType.DMA((4,)),
+            pltpu.SemaphoreType.DMA((4,)),
+            pltpu.SemaphoreType.DMA((4,)),
             pltpu.SemaphoreType.DMA,
         ],
         compiler_params=pltpu.CompilerParams(collective_id=cid, has_side_effects=True),
@@ -137,8 +141,8 @@
 def to_blk_order(rows_in_gather_order, n):
     total, cols = rows_in_gather_order.shape
     nz = n // PLANE
-    parts = rows_in_gather_order.reshape(PLANE, nz, total // n, cols)
-    return jnp.swapaxes(parts, 0, 1).reshape(1, total, cols)
+    parts = rows_in_gather_order.reshape(NY, NX, nz, total // n, cols)
+    return jnp.transpose(parts, (2, 1, 0, 3, 4)).reshape(1, total, cols)
 
 
 def from_behind(shard, axis, by):
@@ -169,7 +173,7 @@
     key_all = kv_all[:, :width]
     value_all = kv_all[:, width:]
     nz = n // PLANE
-    live_by_slot = jnp.swapaxes(live[0].reshape(nz, PLANE), 0, 1).reshape(n)
+    live_by_slot = jnp.transpose(live[0].reshape(nz, NX, NY), (2, 1, 0)).reshape(n)
     usable = (jnp.repeat(live_by_slot, num_rows) == 1)[None, None, :]
     num_heads = width // 64
     head_of_col = jnp.arange(width) // 64

time: 613 us -> 440 us (0.72)
  Pallas kernels: 391 us -> 241 us
  blocking collectives: 33.8 us -> 17.7 us
  starting transfers between devices: 69.6 us -> 62.5 us
    pallas_call x6, Pallas kernels: 391 us -> 241 us  [gather_blk(): pl.pallas_call(functools.partial(gather_kernel, n), out_shape=jax.ShapeDt...]
    ppermute x1, starting transfers between devices: 5.13 us -> 31.1 us  [per_device(): first_req1 = lax.ppermute(outs[0], 'section', [(1, 0)])]
    all_to_all x2, starting transfers between devices: 37.4 us -> 17.1 us  [attend(): lax.all_to_all(to_blk_order(columns, n), 'blk', split_axis=1, concat_axis...]
    all_to_all x1, blocking collectives: 33.8 us -> 17.7 us  [attend(): lax.all_to_all(to_blk_order(out_part, n), 'blk', split_axis=1, concat_axi...]
    all_to_all x1, starting transfers between devices: 21.4 us -> 8.61 us  [attend(): lax.all_to_all(to_blk_order(out_part, n), 'blk', split_axis=1, concat_axi...]
    ppermute x1, waiting for transfers between devices: 4.9 us -> 11.7 us  [per_device(): second_req0 = lax.ppermute(outs[1], 'section', [(0, 1)])]
    all_to_all x1, waiting for transfers between devices: 6.8 us -> 0.01 us  [attend(): lax.all_to_all(to_blk_order(out_part, n), 'blk', split_axis=1, concat_axi...]
  transfers between devices with their start and end apart: 10 -> 10, of which waited for: 4 -> 3; matrix products, arithmetic and copies ran while one was open for 7% -> 9% of each run, Pallas kernels for 33% -> 30%
where the time goes in v9:
time: 440 us; the launch traced here: 439 us
  Pallas kernels  241 us (55%)
  starting transfers between devices  62.5 us (14%)
  local copies, waits for them, and re-layouts  58 us (13%)
  waiting for transfers between devices  32.6 us (7%)
  blocking collectives  17.7 us (4%)
  matrix products  16 us (4%)
  other arithmetic  7.18 us (2%)
    pallas_call x6, Pallas kernels, gather_blk(): pl.pallas_call(functools.partial(gather_kernel, n), out_shape=jax.ShapeDt...  241 us
    ppermute x1, starting transfers between devices, per_device(): first_req1 = lax.ppermute(outs[0], 'section', [(1, 0)])  31.1 us
    all_to_all x2, waiting for transfers between devices, attend(): lax.all_to_all(to_blk_order(columns, n), 'blk', split_axis=1, concat_axis...  20.9 us
    all_to_all x1, blocking collectives, attend(): lax.all_to_all(to_blk_order(out_part, n), 'blk', split_axis=1, concat_axi...  17.7 us
    all_to_all x2, starting transfers between devices, attend(): lax.all_to_all(to_blk_order(columns, n), 'blk', split_axis=1, concat_axis...  17.1 us
    another operation x2, local copies, waits for them, and re-layouts, gather_rows(): return out.reshape(n * rows, width)  15.4 us
    reshape x4, local copies, waits for them, and re-layouts, gather_rows(): return out.reshape(n * rows, width)  13 us
    ppermute x1, waiting for transfers between devices, per_device(): second_req0 = lax.ppermute(outs[1], 'section', [(0, 1)])  11.7 us
  transfers between devices with their start and end apart: 10, of which 3 were waited for; matrix products, arithmetic and copies ran while one was open for 9% of the time, Pallas kernels for 30%

profile of v9, /device:TPU:1, one launch (start us, length us, event | category | flops | bytes accessed | tf_op | source)
XLA Modules:
  0.0 438.9 jit_solution(3432298088267479161)
XLA Ops:
  0.7 2.4 fusion.2
  3.1 3.3 collective-permute-start
  15.6 41.3 %shard_map.91 = bf16[4,4,8,80,128]{4,3,2,1,0:T(8,128)(2,1)} custom-call(bf16[80,128]{1,0:T(8,128)(2,1)} %pad_bitcast_fusion.3.x_ref), custom_call_target="tpu_custom_call" | custom-call | tf_op jit(solution)/shard_map/pallas_call | solution.py:105
  60.9 3.3 reshape.350
  67.5 10.7 %all-to-all-start = ((bf16[1,384,72]{2,0,1:T(2,128)(2,1)}), bf16[1,384,72]{2,0,1:T(2,128)(2,1)S(1)}, u32[]{:S(2)}, u32[]{:S(2)}) async-start(bf16[1,384,72]{2,0,1:T(2,128)(2,1)} %reshape.378), calls=%async_computation | async-start | bytes 393216 | tf_op jit(solution)/shard_map/all_to_all | solution.py:164
  79.7 10.2 %all-to-all-done = bf16[1,384,72]{2,0,1:T(2,128)(2,1)S(1)} async-done(((bf16[1,384,72]{2,0,1:T(2,128)(2,1)}), bf16[1,384,72]{2,0,1:T(2,128)(2,1)S(1)}, u32[]{:S(2)}, u32[]{:S(2)}) %all-to-all-start) | async-done | bytes 55328 | tf_op jit(solution)/shard_map/all_to_all | solution.py:164
  91.6 55.4 %shard_map.92 = bf16[4,4,8,144,128]{4,3,2,1,0:T(8,128)(2,1)} custom-call(bf16[144,128]{1,0:T(8,128)(2,1)} %reshape_reshape.19.x_ref), custom_call_target="tpu_custom_call" | custom-call | tf_op jit(solution)/shard_map/pallas_call | solution.py:105
  147.1 7.7 %reshape_reshape_reshape.6 = bf16[384,6144]{1,0:T(8,128)(2,1)} reshape(bf16[4,4,8,144,128]{4,3,2,1,0:T(8,128)(2,1)} %shard_map.92) | data formatting | bytes 9437184 | tf_op jit(solution)/shard_map/reshape;reshape;reshape | solution.py:138
  154.8 2.8 fusion.55
  160.4 33.8 %shard_map.93 = bf16[4,4,8,80,128]{4,3,2,1,0:T(8,128)(2,1)} custom-call(bf16[80,128]{1,0:T(8,128)(2,1)} %pad_bitcast_fusion.2.x_ref), custom_call_target="tpu_custom_call" | custom-call | tf_op jit(solution)/shard_map/pallas_call | solution.py:105
  198.2 3.2 reshape.355
  203.5 17.7 %all_to_all.54 = bf16[1,384,24]{2,0,1:T(2,128)(2,1)S(1)} all-to-all(bf16[1,384,24]{2,0,1:T(2,128)(2,1)S(1)} %reshape.379), channel_id=1, replica_groups=mesh['section'=2,'blk'=128] {'blk'}, dimensions={1} | all-to-all | bytes 36864 | tf_op jit(solution)/shard_map/all_to_all | solution.py:196
  222.8 34.3 %shard_map.94 = bf16[4,4,8,80,128]{4,3,2,1,0:T(8,128)(2,1)} custom-call(bf16[80,128]{1,0:T(8,128)(2,1)} %pad_bitcast_fusion.1.x_ref), custom_call_target="tpu_custom_call" | custom-call | tf_op jit(solution)/shard_map/pallas_call | solution.py:105
  261.1 3.2 reshape.360
  266.2 6.4 %all-to-all-start.2 = ((bf16[1,384,72]{2,0,1:T(2,128)(2,1)}), bf16[1,384,72]{2,0,1:T(2,128)(2,1)S(1)}, u32[]{:S(2)}, u32[]{:S(2)}) async-start(bf16[1,384,72]{2,0,1:T(2,128)(2,1)} %reshape.380), calls=%async_computation.2 | async-start | bytes 393216 | tf_op jit(solution)/shard_map/all_to_all | solution.py:164
  273.8 10.7 %all-to-all-done.2 = bf16[1,384,72]{2,0,1:T(2,128)(2,1)S(1)} async-done(((bf16[1,384,72]{2,0,1:T(2,128)(2,1)}), bf16[1,384,72]{2,0,1:T(2,128)(2,1)S(1)}, u32[]{:S(2)}, u32[]{:S(2)}) %all-to-all-start.2) | async-done | bytes 55328 | tf_op jit(solution)/shard_map/all_to_all | solution.py:164
  286.2 44.0 %shard_map.95 = bf16[4,4,8,144,128]{4,3,2,1,0:T(8,128)(2,1)} custom-call(bf16[144,128]{1,0:T(8,128)(2,1)} %reshape_reshape.22.x_ref), custom_call_target="tpu_custom_call" | custom-call | tf_op jit(solution)/shard_map/pallas_call | solution.py:105
  330.2 7.7 %reshape_reshape_reshape.7 = bf16[384,6144]{1,0:T(8,128)(2,1)} reshape(bf16[4,4,8,144,128]{4,3,2,1,0:T(8,128)(2,1)} %shard_map.95) | data formatting | bytes 9437184 | tf_op jit(solution)/shard_map/reshape;reshape;reshape | solution.py:138
  337.9 2.8 fusion.56
  343.5 32.3 %shard_map.96 = bf16[4,4,8,80,128]{4,3,2,1,0:T(8,128)(2,1)} custom-call(bf16[80,128]{1,0:T(8,128)(2,1)} %pad_bitcast_fusion.x_ref), custom_call_target="tpu_custom_call" | custom-call | tf_op jit(solution)/shard_map/pallas_call | solution.py:105
  379.8 3.2 reshape.365
  384.8 8.6 %all-to-all-start.3 = ((bf16[1,384,24]{2,0,1:T(2,128)(2,1)}), bf16[1,384,24]{2,0,1:T(2,128)(2,1)S(1)}, u32[]{:S(2)}, u32[]{:S(2)}) async-start(bf16[1,384,24]{2,0,1:T(2,128)(2,1)} %reshape.381), calls=%async_computation.3 | async-start | bytes 393216 | tf_op jit(solution)/shard_map/all_to_all | solution.py:196
  393.4 31.1 %collective-permute-start.5 = (bf16[1,3,3072]{2,0,1:T(2,128)(2,1)S(1)}, bf16[1,3,3072]{2,0,1:T(2,128)(2,1)S(1)}, u32[]{:S(2)}, u32[]{:S(2)}) collective-permute-start(bf16[1,3,3072]{2,0,1:T(2,128)(2,1)S(1)} %get-tuple-element.6), channel_id=1, source_target_pairs={{128,0},{129,1},{130,2},{131,3},{132,4},{133,5},{134,6},{135,7},{1... | collective-permute-start | bytes 55304 | tf_op jit(solution)/shard_map/ppermute | solution.py:246
  426.4 11.7 %collective-permute-done.6 = bf16[1,3,3072]{2,0,1:T(2,128)(2,1)S(1)} collective-permute-done((bf16[1,3,3072]{2,0,1:T(2,128)(2,1)S(1)}, bf16[1,3,3072]{2,0,1:T(2,128)(2,1)S(1)}, u32[]{:S(2)}, u32[]{:S(2)}) %collective-permute-start.6) | collective-permute-done | bytes 18464 | tf_op jit(solution)/shard_map/ppermute | solution.py:247
  (137 shorter events, 47.2 us)
Async XLA Ops:
  0.0 9.1 %copy-start.10 = (s32[1,2,128]{2,1,0:T(2,128)S(1)}, s32[1,2,128]{2,1,0:T(2,128)}, u32[]{:S(2)}) copy-start(s32[1,2,128]{2,1,0:T(2,128)} %param.14) | copy-start | bytes 3076
  0.0 9.4 %copy-start.3 = (bf16[1,3072,24]{1,2,0:T(8,128)(2,1)S(1)}, bf16[1,3072,24]{1,2,0:T(8,128)(2,1)}, u32[]{:S(2)}) copy-start(bf16[1,3072,24]{1,2,0:T(8,128)(2,1)} %param.11) | copy-start | bytes 442372
  0.0 9.8 %copy-start.4 = (bf16[2,3,3072]{2,0,1:T(2,128)(2,1)S(1)}, bf16[2,3,3072]{2,0,1:T(2,128)(2,1)}, u32[]{:S(2)}) copy-start(bf16[2,3,3072]{2,0,1:T(2,128)(2,1)} %param.9) | copy-start | bytes 110596
  0.0 11.5 %copy-start.11 = (s32[2,128]{1,0:T(2,128)S(1)}, s32[2,128]{1,0:T(2,128)}, u32[]{:S(2)}) copy-start(s32[2,128]{1,0:T(2,128)} %param.15) | copy-start | bytes 3076
  3.1 10.9 %collective-permute-start = (f32[3,3072]{1,0:T(4,128)S(1)}, f32[3,3072]{1,0:T(4,128)S(1)}, u32[]{:S(2)}, u32[]{:S(2)}) collective-permute-start(f32[3,3072]{1,0:T(4,128)S(1)} %bitcast.180), channel_id=1, source_target_pairs={{0,128},{128,0},{1,129},{129,1},{2,130},{130,2},{3,131},{131,3},{4... | collective-permute-start | bytes 110600 | tf_op jit(solution)/shard_map/ppermute | solution.py:201
  6.5 57.7 %collective-permute-start.1 = (bf16[3072,72]{0,1:T(8,128)(2,1)}, bf16[3072,72]{0,1:T(8,128)(2,1)S(1)}, u32[]{:S(2)}, u32[]{:S(2)}) collective-permute-start(bf16[3072,72]{0,1:T(8,128)(2,1)} %bitcast.166), channel_id=1, source_target_pairs={{0,128},{128,0},{1,129},{129,1},{2,130},{130,2},{3,131},{131,3},{4... | collective-permute-start | bytes 1327112 | tf_op jit(solution)/shard_map/ppermute | solution.py:201
  7.4 0.6 copy-start.5
  8.7 69.6 %collective-permute-start.3 = (bf16[1,3,6144]{2,1,0:T(4,128)(2,1)}, bf16[1,3,6144]{2,1,0:T(4,128)(2,1)}, u32[]{:S(2)}, u32[]{:S(2)}) collective-permute-start(bf16[1,3,6144]{2,1,0:T(4,128)(2,1)} %fusion.35), channel_id=1, source_target_pairs={{0,128},{128,0},{1,129},{129,1},{2,130},{130,2},{3,131},{131,3},{4... | collective-permute-start | bytes 110600 | tf_op jit(solution)/shard_map/ppermute | solution.py:201
  9.2 3.0 collective-permute-start.2
  9.4 192.1 %collective-permute-start.4 = (bf16[3072,24]{0,1:T(8,128)(2,1)S(1)}, bf16[3072,24]{0,1:T(8,128)(2,1)}, u32[]{:S(2)}, u32[]{:S(2)}) collective-permute-start(bf16[3072,24]{0,1:T(8,128)(2,1)S(1)} %bitcast.169), channel_id=1, source_target_pairs={{0,128},{128,0},{1,129},{129,1},{2,130},{130,2},{3,131},{131,3},{4... | collective-permute-start | bytes 442376 | tf_op jit(solution)/shard_map/ppermute | solution.py:201
  60.9 3.3 copy-start.2
  67.5 22.4 %all-to-all-start = ((bf16[1,384,72]{2,0,1:T(2,128)(2,1)}), bf16[1,384,72]{2,0,1:T(2,128)(2,1)S(1)}, u32[]{:S(2)}, u32[]{:S(2)}) async-start(bf16[1,384,72]{2,0,1:T(2,128)(2,1)} %reshape.378), calls=%async_computation | async-start | bytes 393216 | tf_op jit(solution)/shard_map/all_to_all | solution.py:164
  147.0 7.8 %copy-start.7 = (pred[48,3072]{1,0:T(8,128)(4,1)S(1)}, pred[48,3072]{1,0:T(8,128)(4,1)}, u32[]{:S(2)}) copy-start(pred[48,3072]{1,0:T(8,128)(4,1)} %iota_compare_fusion) | copy-start | bytes 442372
  154.8 3.0 copy-start.1
  201.4 20.1 %copy-start.9 = (f32[1,3072]{1,0:T(1,128)S(1)}, f32[1,3072]{1,0:T(1,128)}, u32[]{:S(2)}) copy-start(f32[1,3072]{1,0:T(1,128)} %get-tuple-element.31) | copy-start | bytes 36868
  264.4 21.0 %copy-start.6 = (bf16[1,3,6144]{2,1,0:T(4,128)(2,1)S(1)}, bf16[1,3,6144]{2,1,0:T(4,128)(2,1)}, u32[]{:S(2)}) copy-start(bf16[1,3,6144]{2,1,0:T(4,128)(2,1)} %get-tuple-element.7) | copy-start | bytes 110596
  266.2 18.3 %all-to-all-start.2 = ((bf16[1,384,72]{2,0,1:T(2,128)(2,1)}), bf16[1,384,72]{2,0,1:T(2,128)(2,1)S(1)}, u32[]{:S(2)}, u32[]{:S(2)}) async-start(bf16[1,384,72]{2,0,1:T(2,128)(2,1)} %reshape.380), calls=%async_computation.2 | async-start | bytes 393216 | tf_op jit(solution)/shard_map/all_to_all | solution.py:164
  330.2 7.7 %copy-start.8 = (pred[48,3072]{1,0:T(8,128)(4,1)S(1)}, pred[48,3072]{1,0:T(8,128)(4,1)}, u32[]{:S(2)}) copy-start(pred[48,3072]{1,0:T(8,128)(4,1)} %iota_compare_fusion) | copy-start | bytes 442372
  337.9 3.0 copy-start
  384.8 39.7 %all-to-all-start.3 = ((bf16[1,384,24]{2,0,1:T(2,128)(2,1)}), bf16[1,384,24]{2,0,1:T(2,128)(2,1)S(1)}, u32[]{:S(2)}, u32[]{:S(2)}) async-start(bf16[1,384,24]{2,0,1:T(2,128)(2,1)} %reshape.381), calls=%async_computation.3 | async-start | bytes 393216 | tf_op jit(solution)/shard_map/all_to_all | solution.py:196
  393.4 32.9 %collective-permute-start.5 = (bf16[1,3,3072]{2,0,1:T(2,128)(2,1)S(1)}, bf16[1,3,3072]{2,0,1:T(2,128)(2,1)S(1)}, u32[]{:S(2)}, u32[]{:S(2)}) collective-permute-start(bf16[1,3,3072]{2,0,1:T(2,128)(2,1)S(1)} %get-tuple-element.6), channel_id=1, source_target_pairs={{128,0},{129,1},{130,2},{131,3},{132,4},{133,5},{134,6},{135,7},{1... | collective-permute-start | bytes 55304 | tf_op jit(solution)/shard_map/ppermute | solution.py:246
  425.0 13.1 %collective-permute-start.6 = (bf16[1,3,3072]{2,0,1:T(2,128)(2,1)S(1)}, bf16[1,3,3072]{2,0,1:T(2,128)(2,1)S(1)}, u32[]{:S(2)}, u32[]{:S(2)}) collective-permute-start(bf16[1,3,3072]{2,0,1:T(2,128)(2,1)S(1)} %add_convert_fusion), channel_id=1, source_target_pairs={{0,128},{1,129},{2,130},{3,131},{4,132},{5,133},{6,134},{7,135},{8... | collective-permute-start | bytes 55304 | tf_op jit(solution)/shard_map/ppermute | solution.py:247

commit v10 on v9

--- a/solution.py
+++ b/solution.py
@@ -15,9 +15,10 @@
 PLANE = NX * NY
 
 
-def gather_kernel(n, x_ref, o_ref, zs, zr, xs, xr, ys, yr, local_sem):
+def gather_kernel(n, x_ref, oa_ref, ob_ref, zbuf, zs, zr, rs, rr, local_sem):
     sec = lax.axis_index("section")
     nz = n // PLANE
+    h = nz // 2
     me = lax.axis_index("blk")
     y = me % NY
     x = (me // NY) % NX
@@ -42,13 +43,13 @@
         pl.semaphore_signal(barrier, inc=1, device_id=target, device_id_type=MESH)
     pl.semaphore_wait(barrier, nz - 1 + 4)
 
-    local = pltpu.make_async_copy(x_ref, o_ref.at[y, x, z], local_sem)
+    local = pltpu.make_async_copy(x_ref, zbuf.at[z], local_sem.at[0])
     local.start()
 
     def copy_z(i, src_z):
         return pltpu.make_async_remote_copy(
             src_ref=x_ref,
-            dst_ref=o_ref.at[y, x, src_z],
+            dst_ref=zbuf.at[src_z],
             send_sem=zs.at[i],
             recv_sem=zr.at[src_z],
             device_id=dev(z_peer(i), x, y),
@@ -68,57 +69,101 @@
 
     lax.fori_loop(0, nz - 1, finish_z, 0)
     local.wait()
-
-    def ring(block, send_sems, recv_sems, up, down, far, count, target_up, target_down):
-        def rcopy(ref, k, target):
-            return pltpu.make_async_remote_copy(
-                src_ref=ref, dst_ref=ref, send_sem=send_sems.at[k], recv_sem=recv_sems.at[k],
-                device_id=target, device_id_type=MESH,
-            )
-
-        mine_up = rcopy(block(None), 0, target_up)
-        mine_down = rcopy(block(None), 1, target_down)
-        mine_up.start()
-        mine_down.start()
-        mine_up.wait_send()
-        mine_down.wait_send()
-        rcopy(block(down), 0, target_down).wait_recv()
-        rcopy(block(up), 1, target_up).wait_recv()
-        half = count // 2
-        fwd_up = rcopy(block(down).at[pl.ds(0, half)], 2, target_up)
-        fwd_down = rcopy(block(up).at[pl.ds(half, count - half)], 3, target_down)
-        fwd_up.start()
-        fwd_down.start()
-        fwd_up.wait_send()
-        fwd_down.wait_send()
-        rcopy(block(far).at[pl.ds(0, half)], 2, target_down).wait_recv()
-        rcopy(block(far).at[pl.ds(half, count - half)], 3, target_up).wait_recv()
-
-    ring(lambda p: o_ref.at[y, x if p is None else p], xs, xr, xp, xm, x2, nz,
-         dev(z, xp, y), dev(z, xm, y))
-    ring(lambda p: o_ref.at[y if p is None else p], ys, yr, yp, ym, y2, NX,
-         dev(z, x, yp), dev(z, x, ym))
+    own_a = pltpu.make_async_copy(zbuf.at[pl.ds(0, h)], oa_ref.at[y, x], local_sem.at[1])
+    own_b = pltpu.make_async_copy(zbuf.at[pl.ds(h, nz - h)], ob_ref.at[x, y], local_sem.at[2])
+    own_a.start()
+    own_b.start()
+
+    def rcopy(stage, src, dst, k, target):
+        return pltpu.make_async_remote_copy(
+            src_ref=src, dst_ref=dst, send_sem=rs.at[stage, k], recv_sem=rr.at[stage, k],
+            device_id=target, device_id_type=MESH,
+        )
+
+    class Ring:
+        def __init__(self, stage, mine, block, up, down, far, count, target_up, target_down):
+            self.stage, self.mine, self.block = stage, mine, block
+            self.up, self.down, self.far, self.count = up, down, far, count
+            self.target_up, self.target_down = target_up, target_down
+
+        def step1(self):
+            s, me_ref = self.stage, self.block(None)
+            self.a = rcopy(s, self.mine, me_ref, 0, self.target_up)
+            self.b = rcopy(s, self.mine, me_ref, 1, self.target_down)
+            self.a.start()
+            self.b.start()
+
+        def wait1(self):
+            s = self.stage
+            self.a.wait_send()
+            self.b.wait_send()
+            rcopy(s, self.block(self.down), self.block(self.down), 0, self.target_down).wait_recv()
+            rcopy(s, self.block(self.up), self.block(self.up), 1, self.target_up).wait_recv()
+
+        def step2(self):
+            s, half = self.stage, self.count // 2
+            first = self.block(self.down).at[pl.ds(0, half)]
+            second = self.block(self.up).at[pl.ds(half, self.count - half)]
+            self.c = rcopy(s, first, first, 2, self.target_up)
+            self.d = rcopy(s, second, second, 3, self.target_down)
+            self.c.start()
+            self.d.start()
+
+        def wait2(self):
+            s, half = self.stage, self.count // 2
+            self.c.wait_send()
+            self.d.wait_send()
+            first = self.block(self.far).at[pl.ds(0, half)]
+            second = self.block(self.far).at[pl.ds(half, self.count - half)]
+            rcopy(s, first, first, 2, self.target_down).wait_recv()
+            rcopy(s, second, second, 3, self.target_up).wait_recv()
+
+    x_targets = (dev(z, xp, y), dev(z, xm, y))
+    y_targets = (dev(z, x, yp), dev(z, x, ym))
+    a_x = Ring(0, zbuf.at[pl.ds(0, h)], lambda p: oa_ref.at[y, x if p is None else p],
+               xp, xm, x2, h, *x_targets)
+    b_y = Ring(1, zbuf.at[pl.ds(h, nz - h)], lambda p: ob_ref.at[x, y if p is None else p],
+               yp, ym, y2, nz - h, *y_targets)
+    a_y = Ring(2, oa_ref.at[y], lambda p: oa_ref.at[y if p is None else p],
+               yp, ym, y2, NX, *y_targets)
+    b_x = Ring(3, ob_ref.at[x], lambda p: ob_ref.at[x if p is None else p],
+               xp, xm, x2, NY, *x_targets)
+    for first, second in ((a_x, b_y), (a_y, b_x)):
+        first.step1()
+        second.step1()
+        first.wait1()
+        second.wait1()
+        first.step2()
+        second.step2()
+        first.wait2()
+        second.wait2()
+        if first is a_x:
+            own_a.wait()
+            own_b.wait()
 
 
 def gather_blk(x, n, cid, active=None):
     nz = n // PLANE
-    out = pl.pallas_call(
+    h = nz // 2
+    oa, ob = pl.pallas_call(
         functools.partial(gather_kernel, n),
-        out_shape=jax.ShapeDtypeStruct((NY, NX, nz) + x.shape, x.dtype),
+        out_shape=(
+            jax.ShapeDtypeStruct((NY, NX, h) + x.shape, x.dtype),
+            jax.ShapeDtypeStruct((NX, NY, nz - h) + x.shape, x.dtype),
+        ),
         in_specs=[pl.BlockSpec(memory_space=pl.ANY)],
-        out_specs=pl.BlockSpec(memory_space=pl.ANY),
+        out_specs=(pl.BlockSpec(memory_space=pl.ANY), pl.BlockSpec(memory_space=pl.ANY)),
         scratch_shapes=[
+            pltpu.VMEM((nz,) + x.shape, x.dtype),
             pltpu.SemaphoreType.DMA((nz,)),
             pltpu.SemaphoreType.DMA((nz,)),
-            pltpu.SemaphoreType.DMA((4,)),
-            pltpu.SemaphoreType.DMA((4,)),
-            pltpu.SemaphoreType.DMA((4,)),
-            pltpu.SemaphoreType.DMA((4,)),
-            pltpu.SemaphoreType.DMA,
+            pltpu.SemaphoreType.DMA((4, 4)),
+            pltpu.SemaphoreType.DMA((4, 4)),
+            pltpu.SemaphoreType.DMA((3,)),
         ],
         compiler_params=pltpu.CompilerParams(collective_id=cid, has_side_effects=True),
     )(x)
-    return out.reshape((n,) + x.shape)
+    return jnp.concatenate([oa.reshape((-1,) + x.shape), ob.reshape((-1,) + x.shape)], axis=0)
 
 
 def gather_rows(x, cid, active):
@@ -141,8 +186,14 @@
 def to_blk_order(rows_in_gather_order, n):
     total, cols = rows_in_gather_order.shape
     nz = n // PLANE
-    parts = rows_in_gather_order.reshape(NY, NX, nz, total // n, cols)
-    return jnp.transpose(parts, (2, 1, 0, 3, 4)).reshape(1, total, cols)
+    h = nz // 2
+    rows = total // n
+    part_a = rows_in_gather_order[: h * PLANE * rows].reshape(NY, NX, h, rows, cols)
+    part_b = rows_in_gather_order[h * PLANE * rows :].reshape(NX, NY, nz - h, rows, cols)
+    ordered = jnp.concatenate(
+        [jnp.transpose(part_a, (2, 1, 0, 3, 4)), jnp.transpose(part_b, (2, 0, 1, 3, 4))], axis=0
+    )
+    return ordered.reshape(1, total, cols)
 
 
 def from_behind(shard, axis, by):
@@ -173,7 +224,11 @@
     key_all = kv_all[:, :width]
     value_all = kv_all[:, width:]
     nz = n // PLANE
-    live_by_slot = jnp.transpose(live[0].reshape(nz, NX, NY), (2, 1, 0)).reshape(n)
+    live_zxy = live[0].reshape(nz, NX, NY)
+    live_by_slot = jnp.concatenate([
+        jnp.transpose(live_zxy[: nz // 2], (2, 1, 0)).reshape(-1),
+        jnp.transpose(live_zxy[nz // 2 :], (1, 2, 0)).reshape(-1),
+    ])
     usable = (jnp.repeat(live_by_slot, num_rows) == 1)[None, None, :]
     num_heads = width // 64
     head_of_col = jnp.arange(width) // 64

time: 440 us -> 389 us (0.88)
  Pallas kernels: 241 us -> 180 us
  other arithmetic: 7.18 us -> 24.6 us
  local copies, waits for them, and re-layouts: 58 us -> 50.8 us
    pallas_call x6, Pallas kernels: 241 us -> 180 us  [gather_blk(): pl.pallas_call(functools.partial(gather_kernel, n), out_shape=(jax.ShapeD...]
    concatenate x0 -> x10, other arithmetic: none -> 16.7 us  [the longest x6 16.2 us: gather_blk(): jnp.concatenate([oa.reshape((-1,) + x.shape), ob.reshape((-1,) + x.shape)...]
    slice x4 -> x15, local copies, waits for them, and re-layouts: 6.38 us -> 1.51 us  [the longest x8 0.79 us: to_blk_order(): rows_in_gather_order[:h * PLANE * rows].reshape(NY, NX, h, rows, cols)]
    unnamed x32 -> x50, local copies, waits for them, and re-layouts: 10.5 us -> 9.19 us
  transfers between devices with their start and end apart: 10 -> 10, of which waited for: 3 -> 3; matrix products, arithmetic and copies ran while one was open for 9% -> 12% of each run, Pallas kernels for 30% -> 24%
where the time goes in v10:
time: 389 us; the launch traced here: 387 us
  Pallas kernels  180 us (46%)
  starting transfers between devices  60.8 us (16%)
  local copies, waits for them, and re-layouts  50.8 us (13%)
  waiting for transfers between devices  32.4 us (8%)
  other arithmetic  24.6 us (6%)
  blocking collectives  19.2 us (5%)
  matrix products  16 us (4%)
  between operations  4.06 us (1%)
    pallas_call x6, Pallas kernels, gather_blk(): pl.pallas_call(functools.partial(gather_kernel, n), out_shape=(jax.ShapeD...  180 us
    ppermute x1, starting transfers between devices, per_device(): first_req1 = lax.ppermute(outs[0], 'section', [(1, 0)])  29.4 us
    all_to_all x2, waiting for transfers between devices, attend(): lax.all_to_all(to_blk_order(columns, n), 'blk', split_axis=1, concat_axis...  20.7 us
    all_to_all x1, blocking collectives, attend(): lax.all_to_all(to_blk_order(out_part, n), 'blk', split_axis=1, concat_axi...  19.2 us
    all_to_all x2, starting transfers between devices, attend(): lax.all_to_all(to_blk_order(columns, n), 'blk', split_axis=1, concat_axis...  17.1 us
    concatenate x6, other arithmetic, gather_blk(): jnp.concatenate([oa.reshape((-1,) + x.shape), ob.reshape((-1,) + x.shape)...  16.2 us
    another operation x2, local copies, waits for them, and re-layouts, gather_rows(): return out.reshape(n * rows, width)  15.5 us
    reshape x4, local copies, waits for them, and re-layouts, gather_rows(): return out.reshape(n * rows, width)  13 us
  transfers between devices with their start and end apart: 10, of which 3 were waited for; matrix products, arithmetic and copies ran while one was open for 12% of the time, Pallas kernels for 24%

profile of v10, /device:TPU:1, one launch (start us, length us, event | category | flops | bytes accessed | tf_op | source)
XLA Modules:
  0.0 387.4 jit_solution(17068434953862399977)
XLA Ops:
  3.1 3.3 collective-permute-start
  16.1 30.5 %shard_map.91 = (bf16[4,4,4,80,128]{4,3,2,1,0:T(8,128)(2,1)}, bf16[4,4,4,80,128]{4,3,2,1,0:T(8,128)(2,1)}) custom-call(bf16[80,128]{1,0:T(8,128)(2,1)} %pad_bitcast_fusion.3.x_ref), custom_call_target="tpu_custom_call" | custom-call | tf_op jit(solution)/shard_map/pallas_call | solution.py:148
  50.4 3.3 reshape.408
  55.9 10.4 %all-to-all-start = ((bf16[1,384,72]{2,0,1:T(2,128)(2,1)}), bf16[1,384,72]{2,0,1:T(2,128)(2,1)S(1)}, u32[]{:S(2)}, u32[]{:S(2)}) async-start(bf16[1,384,72]{2,0,1:T(2,128)(2,1)} %reshape.444), calls=%async_computation | async-start | bytes 393216 | tf_op jit(solution)/shard_map/all_to_all | solution.py:215
  67.8 10.2 %all-to-all-done = bf16[1,384,72]{2,0,1:T(2,128)(2,1)S(1)} async-done(((bf16[1,384,72]{2,0,1:T(2,128)(2,1)}), bf16[1,384,72]{2,0,1:T(2,128)(2,1)S(1)}, u32[]{:S(2)}, u32[]{:S(2)}) %all-to-all-start) | async-done | bytes 55328 | tf_op jit(solution)/shard_map/all_to_all | solution.py:215
  79.7 36.9 %shard_map.92 = (bf16[4,4,4,144,128]{4,3,2,1,0:T(8,128)(2,1)}, bf16[4,4,4,144,128]{4,3,2,1,0:T(8,128)(2,1)}) custom-call(bf16[144,128]{1,0:T(8,128)(2,1)} %reshape_reshape.12.x_ref), custom_call_target="tpu_custom_call" | custom-call | tf_op jit(solution)/shard_map/pallas_call | solution.py:148
  116.6 4.9 %pad_maximum_fusion = bf16[128,144,128]{2,1,0:T(8,128)(2,1)} fusion(bf16[64,144,128]{2,1,0:T(8,128)(2,1)} %bitcast.200, bf16[64,144,128]{2,1,0:T(8,128)(2,1)} %bitcast.199), kind=kLoop, calls=%fused_computation | loop fusion | flops 2359296 | bytes 9437184 | tf_op jit(solution)/shard_map/concatenate | solution.py:166
  121.5 7.7 %reshape_reshape.13 = bf16[384,6144]{1,0:T(8,128)(2,1)} reshape(bf16[128,144,128]{2,1,0:T(8,128)(2,1)} %pad_maximum_fusion) | data formatting | bytes 9437184 | tf_op jit(solution)/shard_map/reshape;reshape | solution.py:183
  136.0 25.6 %shard_map.93 = (bf16[4,4,4,80,128]{4,3,2,1,0:T(8,128)(2,1)}, bf16[4,4,4,80,128]{4,3,2,1,0:T(8,128)(2,1)}) custom-call(bf16[80,128]{1,0:T(8,128)(2,1)} %pad_bitcast_fusion.2.x_ref), custom_call_target="tpu_custom_call" | custom-call | tf_op jit(solution)/shard_map/pallas_call | solution.py:148
  165.4 3.2 reshape.416
  171.0 19.2 %all_to_all.54 = bf16[1,384,24]{2,0,1:T(2,128)(2,1)S(1)} all-to-all(bf16[1,384,24]{2,0,1:T(2,128)(2,1)S(1)} %reshape.445), channel_id=1, replica_groups=mesh['section'=2,'blk'=128] {'blk'}, dimensions={1} | all-to-all | bytes 36864 | tf_op jit(solution)/shard_map/all_to_all | solution.py:251
  191.8 27.8 %shard_map.94 = (bf16[4,4,4,80,128]{4,3,2,1,0:T(8,128)(2,1)}, bf16[4,4,4,80,128]{4,3,2,1,0:T(8,128)(2,1)}) custom-call(bf16[80,128]{1,0:T(8,128)(2,1)} %pad_bitcast_fusion.1.x_ref), custom_call_target="tpu_custom_call" | custom-call | tf_op jit(solution)/shard_map/pallas_call | solution.py:148
  223.4 3.2 reshape.422
  228.8 6.7 %all-to-all-start.2 = ((bf16[1,384,72]{2,0,1:T(2,128)(2,1)}), bf16[1,384,72]{2,0,1:T(2,128)(2,1)S(1)}, u32[]{:S(2)}, u32[]{:S(2)}) async-start(bf16[1,384,72]{2,0,1:T(2,128)(2,1)} %reshape.446), calls=%async_computation.2 | async-start | bytes 393216 | tf_op jit(solution)/shard_map/all_to_all | solution.py:215
  236.8 10.4 %all-to-all-done.2 = bf16[1,384,72]{2,0,1:T(2,128)(2,1)S(1)} async-done(((bf16[1,384,72]{2,0,1:T(2,128)(2,1)}), bf16[1,384,72]{2,0,1:T(2,128)(2,1)S(1)}, u32[]{:S(2)}, u32[]{:S(2)}) %all-to-all-start.2) | async-done | bytes 55328 | tf_op jit(solution)/shard_map/all_to_all | solution.py:215
  248.9 34.1 %shard_map.95 = (bf16[4,4,4,144,128]{4,3,2,1,0:T(8,128)(2,1)}, bf16[4,4,4,144,128]{4,3,2,1,0:T(8,128)(2,1)}) custom-call(bf16[144,128]{1,0:T(8,128)(2,1)} %reshape_reshape.14.x_ref), custom_call_target="tpu_custom_call" | custom-call | tf_op jit(solution)/shard_map/pallas_call | solution.py:148
  283.0 4.9 %pad_maximum_fusion.1 = bf16[128,144,128]{2,1,0:T(8,128)(2,1)} fusion(bf16[64,144,128]{2,1,0:T(8,128)(2,1)} %bitcast.202, bf16[64,144,128]{2,1,0:T(8,128)(2,1)} %bitcast.201), kind=kLoop, calls=%fused_computation.1 | loop fusion | flops 2359296 | bytes 9437184 | tf_op jit(solution)/shard_map/concatenate | solution.py:166
  287.9 7.7 %reshape_reshape.15 = bf16[384,6144]{1,0:T(8,128)(2,1)} reshape(bf16[128,144,128]{2,1,0:T(8,128)(2,1)} %pad_maximum_fusion.1) | data formatting | bytes 9437184 | tf_op jit(solution)/shard_map/reshape;reshape | solution.py:183
  295.7 2.8 fusion.60
  301.2 24.8 %shard_map.96 = (bf16[4,4,4,80,128]{4,3,2,1,0:T(8,128)(2,1)}, bf16[4,4,4,80,128]{4,3,2,1,0:T(8,128)(2,1)}) custom-call(bf16[80,128]{1,0:T(8,128)(2,1)} %pad_bitcast_fusion.x_ref), custom_call_target="tpu_custom_call" | custom-call | tf_op jit(solution)/shard_map/pallas_call | solution.py:148
  329.7 3.2 reshape.430
  335.1 8.6 %all-to-all-start.3 = ((bf16[1,384,24]{2,0,1:T(2,128)(2,1)}), bf16[1,384,24]{2,0,1:T(2,128)(2,1)S(1)}, u32[]{:S(2)}, u32[]{:S(2)}) async-start(bf16[1,384,24]{2,0,1:T(2,128)(2,1)} %reshape.447), calls=%async_computation.3 | async-start | bytes 393216 | tf_op jit(solution)/shard_map/all_to_all | solution.py:251
  343.7 29.4 %collective-permute-start.5 = (bf16[1,3,3072]{2,0,1:T(2,128)(2,1)S(1)}, bf16[1,3,3072]{2,0,1:T(2,128)(2,1)S(1)}, u32[]{:S(2)}, u32[]{:S(2)}) collective-permute-start(bf16[1,3,3072]{2,0,1:T(2,128)(2,1)S(1)} %get-tuple-element.32), channel_id=1, source_target_pairs={{128,0},{129,1},{130,2},{131,3},{132,4},{133,5},{134,6},{135,7},{1... | collective-permute-start | bytes 55304 | tf_op jit(solution)/shard_map/ppermute | solution.py:301
  374.9 11.7 %collective-permute-done.6 = bf16[1,3,3072]{2,0,1:T(2,128)(2,1)S(1)} collective-permute-done((bf16[1,3,3072]{2,0,1:T(2,128)(2,1)S(1)}, bf16[1,3,3072]{2,0,1:T(2,128)(2,1)S(1)}, u32[]{:S(2)}, u32[]{:S(2)}) %collective-permute-start.6) | collective-permute-done | bytes 18464 | tf_op jit(solution)/shard_map/ppermute | solution.py:302
  (182 shorter events, 52.7 us)
Async XLA Ops:
  0.0 10.2 %copy-start = (s32[2,128]{1,0:T(2,128)S(1)}, s32[2,128]{1,0:T(2,128)}, u32[]{:S(2)}) copy-start(s32[2,128]{1,0:T(2,128)} %param.15) | copy-start | bytes 3076
  0.0 9.1 %copy-start.18 = (s32[1,2,128]{2,1,0:T(2,128)S(1)}, s32[1,2,128]{2,1,0:T(2,128)}, u32[]{:S(2)}) copy-start(s32[1,2,128]{2,1,0:T(2,128)} %param.14) | copy-start | bytes 3076
  0.0 9.4 %copy-start.9 = (bf16[1,3072,24]{1,2,0:T(8,128)(2,1)S(1)}, bf16[1,3072,24]{1,2,0:T(8,128)(2,1)}, u32[]{:S(2)}) copy-start(bf16[1,3072,24]{1,2,0:T(8,128)(2,1)} %param.11) | copy-start | bytes 442372
  0.0 9.8 %copy-start.10 = (bf16[2,3,3072]{2,0,1:T(2,128)(2,1)S(1)}, bf16[2,3,3072]{2,0,1:T(2,128)(2,1)}, u32[]{:S(2)}) copy-start(bf16[2,3,3072]{2,0,1:T(2,128)(2,1)} %param.9) | copy-start | bytes 110596
  3.1 11.4 %collective-permute-start = (f32[3,3072]{1,0:T(4,128)S(1)}, f32[3,3072]{1,0:T(4,128)S(1)}, u32[]{:S(2)}, u32[]{:S(2)}) collective-permute-start(f32[3,3072]{1,0:T(4,128)S(1)} %bitcast.229), channel_id=1, source_target_pairs={{0,128},{128,0},{1,129},{129,1},{2,130},{130,2},{3,131},{131,3},{4... | collective-permute-start | bytes 110600 | tf_op jit(solution)/shard_map/ppermute | solution.py:256
  6.5 47.2 %collective-permute-start.1 = (bf16[3072,72]{0,1:T(8,128)(2,1)}, bf16[3072,72]{0,1:T(8,128)(2,1)S(1)}, u32[]{:S(2)}, u32[]{:S(2)}) collective-permute-start(bf16[3072,72]{0,1:T(8,128)(2,1)} %bitcast.203), channel_id=1, source_target_pairs={{0,128},{128,0},{1,129},{129,1},{2,130},{130,2},{3,131},{131,3},{4... | collective-permute-start | bytes 1327112 | tf_op jit(solution)/shard_map/ppermute | solution.py:256
  8.6 57.7 %collective-permute-start.3 = (bf16[1,3,6144]{2,1,0:T(4,128)(2,1)}, bf16[1,3,6144]{2,1,0:T(4,128)(2,1)}, u32[]{:S(2)}, u32[]{:S(2)}) collective-permute-start(bf16[1,3,6144]{2,1,0:T(4,128)(2,1)} %fusion.35), channel_id=1, source_target_pairs={{0,128},{128,0},{1,129},{129,1},{2,130},{130,2},{3,131},{131,3},{4... | collective-permute-start | bytes 110600 | tf_op jit(solution)/shard_map/ppermute | solution.py:256
  9.2 3.5 collective-permute-start.2
  9.4 159.2 %collective-permute-start.4 = (bf16[3072,24]{0,1:T(8,128)(2,1)S(1)}, bf16[3072,24]{0,1:T(8,128)(2,1)}, u32[]{:S(2)}, u32[]{:S(2)}) collective-permute-start(bf16[3072,24]{0,1:T(8,128)(2,1)S(1)} %bitcast.214), channel_id=1, source_target_pairs={{0,128},{128,0},{1,129},{129,1},{2,130},{130,2},{3,131},{131,3},{4... | collective-permute-start | bytes 442376 | tf_op jit(solution)/shard_map/ppermute | solution.py:256
  12.7 116.6 %copy-start.16 = (pred[384]{0:T(512)(128)(4,1)}, pred[384]{0:T(512)(128)(4,1)S(1)}, u32[]{:S(2)}) copy-start(pred[384]{0:T(512)(128)(4,1)S(1)} %eq.90) | copy-start | bytes 1156
  50.4 3.3 copy-start.4
  55.9 22.2 %all-to-all-start = ((bf16[1,384,72]{2,0,1:T(2,128)(2,1)}), bf16[1,384,72]{2,0,1:T(2,128)(2,1)S(1)}, u32[]{:S(2)}, u32[]{:S(2)}) async-start(bf16[1,384,72]{2,0,1:T(2,128)(2,1)} %reshape.444), calls=%async_computation | async-start | bytes 393216 | tf_op jit(solution)/shard_map/all_to_all | solution.py:215
  121.5 7.7 %copy-start.13 = (pred[48,3072]{1,0:T(8,128)(4,1)S(1)}, pred[48,3072]{1,0:T(8,128)(4,1)}, u32[]{:S(2)}) copy-start(pred[48,3072]{1,0:T(8,128)(4,1)} %iota_compare_fusion) | copy-start | bytes 442372
  129.3 3.6 copy-start.3
  168.6 22.0 %copy-start.15 = (f32[1,3072]{1,0:T(1,128)S(1)}, f32[1,3072]{1,0:T(1,128)}, u32[]{:S(2)}) copy-start(f32[1,3072]{1,0:T(1,128)} %get-tuple-element.65) | copy-start | bytes 36868
  227.5 20.7 %copy-start.12 = (bf16[1,3,6144]{2,1,0:T(4,128)(2,1)S(1)}, bf16[1,3,6144]{2,1,0:T(4,128)(2,1)}, u32[]{:S(2)}) copy-start(bf16[1,3,6144]{2,1,0:T(4,128)(2,1)} %get-tuple-element.33) | copy-start | bytes 110596
  228.8 18.4 %all-to-all-start.2 = ((bf16[1,384,72]{2,0,1:T(2,128)(2,1)}), bf16[1,384,72]{2,0,1:T(2,128)(2,1)S(1)}, u32[]{:S(2)}, u32[]{:S(2)}) async-start(bf16[1,384,72]{2,0,1:T(2,128)(2,1)} %reshape.446), calls=%async_computation.2 | async-start | bytes 393216 | tf_op jit(solution)/shard_map/all_to_all | solution.py:215
  287.9 7.7 %copy-start.14 = (pred[48,3072]{1,0:T(8,128)(4,1)S(1)}, pred[48,3072]{1,0:T(8,128)(4,1)}, u32[]{:S(2)}) copy-start(pred[48,3072]{1,0:T(8,128)(4,1)} %iota_compare_fusion) | copy-start | bytes 442372
  287.9 7.7 %copy-start.17 = (pred[384]{0:T(512)(128)(4,1)S(1)}, pred[384]{0:T(512)(128)(4,1)}, u32[]{:S(2)}) copy-start(pred[384]{0:T(512)(128)(4,1)} %copy-done.16) | copy-start | bytes 1156
  295.7 3.0 copy-start.2
  333.0 54.4 %copy-start.1 = (s32[2,128]{1,0:T(2,128)S(1)}, s32[2,128]{1,0:T(2,128)}, u32[]{:S(2)}) copy-start(s32[2,128]{1,0:T(2,128)} %param.15) | copy-start | bytes 3076
  335.1 38.0 %all-to-all-start.3 = ((bf16[1,384,24]{2,0,1:T(2,128)(2,1)}), bf16[1,384,24]{2,0,1:T(2,128)(2,1)S(1)}, u32[]{:S(2)}, u32[]{:S(2)}) async-start(bf16[1,384,24]{2,0,1:T(2,128)(2,1)} %reshape.447), calls=%async_computation.3 | async-start | bytes 393216 | tf_op jit(solution)/shard_map/all_to_all | solution.py:251
  343.7 31.2 %collective-permute-start.5 = (bf16[1,3,3072]{2,0,1:T(2,128)(2,1)S(1)}, bf16[1,3,3072]{2,0,1:T(2,128)(2,1)S(1)}, u32[]{:S(2)}, u32[]{:S(2)}) collective-permute-start(bf16[1,3,3072]{2,0,1:T(2,128)(2,1)S(1)} %get-tuple-element.32), channel_id=1, source_target_pairs={{128,0},{129,1},{130,2},{131,3},{132,4},{133,5},{134,6},{135,7},{1... | collective-permute-start | bytes 55304 | tf_op jit(solution)/shard_map/ppermute | solution.py:301
  373.6 13.1 %collective-permute-start.6 = (bf16[1,3,3072]{2,0,1:T(2,128)(2,1)S(1)}, bf16[1,3,3072]{2,0,1:T(2,128)(2,1)S(1)}, u32[]{:S(2)}, u32[]{:S(2)}) collective-permute-start(bf16[1,3,3072]{2,0,1:T(2,128)(2,1)S(1)} %add_convert_fusion), channel_id=1, source_target_pairs={{0,128},{1,129},{2,130},{3,131},{4,132},{5,133},{6,134},{7,135},{8... | collective-permute-start | bytes 55304 | tf_op jit(solution)/shard_map/ppermute | solution.py:302
  (5 other events, 7.7 us)

commit v11 on v10

--- a/solution.py
+++ b/solution.py
@@ -282,12 +282,12 @@
     width = hidden.shape[2]
 
     layer_in = lax.dynamic_index_in_dim(hidden, sec, 0, keepdims=True)
-    outs = []
-    for layer in range(2):
+
+    def run_layer(stream, layer):
         own = sec == layer
         stale = jnp.where(own, stale_mine, stale_other)
-        layer_in = attend(
-            layer_in,
+        out = attend(
+            stream,
             jnp.where(own, qkv_own, qkv_other),
             jnp.where(own, out_own, out_other),
             jnp.where(own, modulate_own, modulate_other),
@@ -297,7 +297,10 @@
             live_mine,
             None,
         )
-        outs.append(layer_in)
+        return out, out
+
+    _, stacked = lax.scan(run_layer, layer_in, jnp.arange(2))
+    outs = [stacked[0], stacked[1]]
     first_req1 = lax.ppermute(outs[0], "section", [(1, 0)])
     second_req0 = lax.ppermute(outs[1], "section", [(0, 1)])
     result = jnp.where(

time: 389 us -> 395 us (1.015)
  blocking collectives: 19.2 us -> 0 us
  waiting for transfers between devices: 32.4 us -> 45.4 us
  starting transfers between devices: 60.8 us -> 71.2 us
  other arithmetic: 24.6 us -> 18.9 us
  matrix products: 16 us -> 21.4 us
  loops' own time: 0 us -> 4.57 us
    all_to_all x1 -> x2, waiting for transfers between devices: 0.01 us -> 23.9 us  [attend(): lax.all_to_all(to_blk_order(out_part, n), 'blk', split_axis=1, concat_axi...]
    all_to_all x1 -> x0, blocking collectives: 19.2 us -> none  [attend(): lax.all_to_all(to_blk_order(out_part, n), 'blk', split_axis=1, concat_axi...]
    another operation x4 -> x0, local copies, waits for them, and re-layouts: 16.8 us -> none  [the longest x2 15.5 us: gather_rows(): return out.reshape(n * rows, width)]
    reshape x4 -> x6, local copies, waits for them, and re-layouts: 13 us -> 26.4 us  [gather_rows(): return out.reshape(n * rows, width)]
    ppermute x1, waiting for transfers between devices: 11.7 us -> 1.77 us  [per_device(): second_req0 = lax.ppermute(outs[1], 'section', [(0, 1)])]
    unnamed x50 -> x8, local copies, waits for them, and re-layouts: 9.19 us -> 0.02 us
    while x0 -> x26, local copies, waits for them, and re-layouts: none -> 7.1 us
    all_to_all x1 -> x2, starting transfers between devices: 8.57 us -> 14.4 us  [attend(): lax.all_to_all(to_blk_order(out_part, n), 'blk', split_axis=1, concat_axi...]
  transfers between devices with their start and end apart: 10 -> 11, of which waited for: 3 -> 5; matrix products, arithmetic and copies ran while one was open for 12% -> 2% of each run, Pallas kernels for 24% -> 0%
where the time goes in v11:
time: 395 us; the launch traced here: 393 us
  Pallas kernels  177 us (45%)
  starting transfers between devices  71.2 us (18%)
  local copies, waits for them, and re-layouts  54.7 us (14%)
  waiting for transfers between devices  45.4 us (11%)
  matrix products  21.4 us (5%)
  other arithmetic  18.9 us (5%)
  loops' own time  4.57 us (1%)
    pallas_call x6, Pallas kernels, gather_blk(): pl.pallas_call(functools.partial(gather_kernel, n), out_shape=(jax.ShapeD...  177 us
    ppermute x1, starting transfers between devices, per_device(): first_req1 = lax.ppermute(outs[0], 'section', [(1, 0)])  34 us
    reshape x6, local copies, waits for them, and re-layouts, gather_rows(): return out.reshape(n * rows, width)  26.4 us
    all_to_all x2, waiting for transfers between devices, attend(): lax.all_to_all(to_blk_order(out_part, n), 'blk', split_axis=1, concat_axi...  23.9 us
    all_to_all x2, waiting for transfers between devices, attend(): lax.all_to_all(to_blk_order(columns, n), 'blk', split_axis=1, concat_axis...  19.7 us
    all_to_all x2, starting transfers between devices, attend(): lax.all_to_all(to_blk_order(columns, n), 'blk', split_axis=1, concat_axis...  17.2 us
    all_to_all x2, starting transfers between devices, attend(): lax.all_to_all(to_blk_order(out_part, n), 'blk', split_axis=1, concat_axi...  14.4 us
    concatenate x6, other arithmetic, gather_blk(): jnp.concatenate([oa.reshape((-1,) + x.shape), ob.reshape((-1,) + x.shape)...  10.6 us
  transfers between devices with their start and end apart: 11, of which 5 were waited for; matrix products, arithmetic and copies ran while one was open for 2% of the time, Pallas kernels for 0%

profile of v11, /device:TPU:1, one launch (start us, length us, event | category | flops | bytes accessed | tf_op | source)
XLA Modules:
  0.0 393.5 jit_solution(9752490610648124465)
XLA Ops:
  1.6 3.2 collective-permute-start.3
  14.1 340.8 %while.14 = (s32[]{:T(128)}, bf16[1,3,3072]{2,0,1:T(2,128)(2,1)S(1)}, bf16[2,1,3,3072]{3,2,1,0:T(4,128)(2,1)}, s32[2]{0:T(128)S(1)}, s32[]{:T(128)}, /*index=5*/...) while((s32[]{:T(128)}, ...), condition=%wide.region_7.8_spmd, body=%wide.region_1.7_spmd.sunk | while | flops 2619057920 | bytes 88893352 | solution.py:302
  17.6 30.5 %eval_jaxpr.12 = (bf16[4,4,4,80,128]{4,3,2,1,0:T(8,128)(2,1)}, bf16[4,4,4,80,128]{4,3,2,1,0:T(8,128)(2,1)}) custom-call(bf16[80,128]{1,0:T(8,128)(2,1)} %pad_bitcast_fusion.4.x_ref), custom_call_target="tpu_custom_call" | custom-call | tf_op jit(solution)/shard_map/while/body/eval_jaxpr/pallas_call | solution.py:148
  50.5 2.7 reshape.396
  57.4 10.2 %all-to-all-start = ((bf16[1,384,72]{2,0,1:T(2,128)(2,1)}), bf16[1,384,72]{2,0,1:T(2,128)(2,1)S(1)}, u32[]{:S(2)}, u32[]{:S(2)}) async-start(bf16[1,384,72]{2,0,1:T(2,128)(2,1)} %reshape.399), calls=%async_computation | async-start | bytes 393216 | tf_op jit(solution)/shard_map/while/body/eval_jaxpr/all_to_all | solution.py:215
  70.1 9.5 %all-to-all-done = bf16[1,384,72]{2,0,1:T(2,128)(2,1)S(1)} async-done(((bf16[1,384,72]{2,0,1:T(2,128)(2,1)}), bf16[1,384,72]{2,0,1:T(2,128)(2,1)S(1)}, u32[]{:S(2)}, u32[]{:S(2)}) %all-to-all-start) | async-done | bytes 55328 | tf_op jit(solution)/shard_map/while/body/eval_jaxpr/all_to_all | solution.py:215
  81.2 36.9 %eval_jaxpr.13 = (bf16[4,4,4,144,128]{4,3,2,1,0:T(8,128)(2,1)}, bf16[4,4,4,144,128]{4,3,2,1,0:T(8,128)(2,1)}) custom-call(bf16[144,128]{1,0:T(8,128)(2,1)} %reshape.400.x_ref), custom_call_target="tpu_custom_call" | custom-call | tf_op jit(solution)/shard_map/while/body/eval_jaxpr/pallas_call | solution.py:148
  118.1 4.9 %pad_maximum_fusion.15 = bf16[128,144,128]{2,1,0:T(8,128)(2,1)} fusion(bf16[64,144,128]{2,1,0:T(8,128)(2,1)} %bitcast.159, bf16[64,144,128]{2,1,0:T(8,128)(2,1)} %bitcast.158), kind=kLoop, calls=%fused_computation.clone.1 | loop fusion | flops 2359296 | bytes 9437184 | tf_op jit(solution)/shard_map/while/body/eval_jaxpr/concatenate | solution.py:166
  123.0 7.7 %reshape.401 = bf16[384,6144]{1,0:T(8,128)(2,1)} reshape(bf16[128,144,128]{2,1,0:T(8,128)(2,1)} %pad_maximum_fusion.15) | data formatting | bytes 9437184 | tf_op jit(solution)/shard_map/while/body/eval_jaxpr/reshape;while/body/eval_jaxpr/reshape | solution.py:183
  130.7 2.8 fusion.53
  136.3 25.4 %eval_jaxpr.14 = (bf16[4,4,4,80,128]{4,3,2,1,0:T(8,128)(2,1)}, bf16[4,4,4,80,128]{4,3,2,1,0:T(8,128)(2,1)}) custom-call(bf16[80,128]{1,0:T(8,128)(2,1)} %pad_bitcast_fusion.5.x_ref), custom_call_target="tpu_custom_call" | custom-call | tf_op jit(solution)/shard_map/while/body/eval_jaxpr/pallas_call | solution.py:148
  170.6 7.1 %all-to-all-start.1 = ((bf16[1,384,24]{2,0,1:T(2,128)(2,1)}), bf16[1,384,24]{2,0,1:T(2,128)(2,1)S(1)}, u32[]{:S(2)}, u32[]{:S(2)}) async-start(bf16[1,384,24]{2,0,1:T(2,128)(2,1)} %reshape.406), calls=%async_computation.1 | async-start | bytes 393216 | tf_op jit(solution)/shard_map/while/body/eval_jaxpr/all_to_all | solution.py:251
  177.6 11.9 %all-to-all-done.1 = bf16[1,384,24]{2,0,1:T(2,128)(2,1)S(1)} async-done(((bf16[1,384,24]{2,0,1:T(2,128)(2,1)}), bf16[1,384,24]{2,0,1:T(2,128)(2,1)S(1)}, u32[]{:S(2)}, u32[]{:S(2)}) %all-to-all-start.1) | async-done | bytes 18464 | tf_op jit(solution)/shard_map/while/body/eval_jaxpr/all_to_all | solution.py:251
  194.0 26.1 %eval_jaxpr.12 = (bf16[4,4,4,80,128]{4,3,2,1,0:T(8,128)(2,1)}, bf16[4,4,4,80,128]{4,3,2,1,0:T(8,128)(2,1)}) custom-call(bf16[80,128]{1,0:T(8,128)(2,1)} %pad_bitcast_fusion.4.x_ref), custom_call_target="tpu_custom_call" | custom-call | tf_op jit(solution)/shard_map/while/body/eval_jaxpr/pallas_call | solution.py:148
  229.2 7.0 %all-to-all-start = ((bf16[1,384,72]{2,0,1:T(2,128)(2,1)}), bf16[1,384,72]{2,0,1:T(2,128)(2,1)S(1)}, u32[]{:S(2)}, u32[]{:S(2)}) async-start(bf16[1,384,72]{2,0,1:T(2,128)(2,1)} %reshape.399), calls=%async_computation | async-start | bytes 393216 | tf_op jit(solution)/shard_map/while/body/eval_jaxpr/all_to_all | solution.py:215
  237.8 10.3 %all-to-all-done = bf16[1,384,72]{2,0,1:T(2,128)(2,1)S(1)} async-done(((bf16[1,384,72]{2,0,1:T(2,128)(2,1)}), bf16[1,384,72]{2,0,1:T(2,128)(2,1)S(1)}, u32[]{:S(2)}, u32[]{:S(2)}) %all-to-all-start) | async-done | bytes 55328 | tf_op jit(solution)/shard_map/while/body/eval_jaxpr/all_to_all | solution.py:215
  249.7 32.4 %eval_jaxpr.13 = (bf16[4,4,4,144,128]{4,3,2,1,0:T(8,128)(2,1)}, bf16[4,4,4,144,128]{4,3,2,1,0:T(8,128)(2,1)}) custom-call(bf16[144,128]{1,0:T(8,128)(2,1)} %reshape.400.x_ref), custom_call_target="tpu_custom_call" | custom-call | tf_op jit(solution)/shard_map/while/body/eval_jaxpr/pallas_call | solution.py:148
  282.2 4.9 %pad_maximum_fusion.15 = bf16[128,144,128]{2,1,0:T(8,128)(2,1)} fusion(bf16[64,144,128]{2,1,0:T(8,128)(2,1)} %bitcast.159, bf16[64,144,128]{2,1,0:T(8,128)(2,1)} %bitcast.158), kind=kLoop, calls=%fused_computation.clone.1 | loop fusion | flops 2359296 | bytes 9437184 | tf_op jit(solution)/shard_map/while/body/eval_jaxpr/concatenate | solution.py:166
  287.1 7.7 %reshape.401 = bf16[384,6144]{1,0:T(8,128)(2,1)} reshape(bf16[128,144,128]{2,1,0:T(8,128)(2,1)} %pad_maximum_fusion.15) | data formatting | bytes 9437184 | tf_op jit(solution)/shard_map/while/body/eval_jaxpr/reshape;while/body/eval_jaxpr/reshape | solution.py:183
  294.8 2.8 fusion.53
  300.3 25.2 %eval_jaxpr.14 = (bf16[4,4,4,80,128]{4,3,2,1,0:T(8,128)(2,1)}, bf16[4,4,4,80,128]{4,3,2,1,0:T(8,128)(2,1)}) custom-call(bf16[80,128]{1,0:T(8,128)(2,1)} %pad_bitcast_fusion.5.x_ref), custom_call_target="tpu_custom_call" | custom-call | tf_op jit(solution)/shard_map/while/body/eval_jaxpr/pallas_call | solution.py:148
  334.4 7.3 %all-to-all-start.1 = ((bf16[1,384,24]{2,0,1:T(2,128)(2,1)}), bf16[1,384,24]{2,0,1:T(2,128)(2,1)S(1)}, u32[]{:S(2)}, u32[]{:S(2)}) async-start(bf16[1,384,24]{2,0,1:T(2,128)(2,1)} %reshape.406), calls=%async_computation.1 | async-start | bytes 393216 | tf_op jit(solution)/shard_map/while/body/eval_jaxpr/all_to_all | solution.py:251
  341.7 12.0 %all-to-all-done.1 = bf16[1,384,24]{2,0,1:T(2,128)(2,1)S(1)} async-done(((bf16[1,384,24]{2,0,1:T(2,128)(2,1)}), bf16[1,384,24]{2,0,1:T(2,128)(2,1)S(1)}, u32[]{:S(2)}, u32[]{:S(2)}) %all-to-all-start.1) | async-done | bytes 18464 | tf_op jit(solution)/shard_map/while/body/eval_jaxpr/all_to_all | solution.py:251
  355.7 34.0 %collective-permute-start.5 = (bf16[1,3,3072]{2,1,0:T(4,128)(2,1)S(1)}, bf16[1,3,3072]{2,1,0:T(4,128)(2,1)S(1)}, u32[]{:S(2)}, u32[]{:S(2)}) collective-permute-start(bf16[1,3,3072]{2,1,0:T(4,128)(2,1)S(1)} %get-tuple-element.280), channel_id=1, source_target_pairs={{128,0},{129,1},{130,2},{131,3},{132,4},{133,5},{134,6},{135,7},{1... | collective-permute-start | bytes 55304 | tf_op jit(solution)/shard_map/ppermute | solution.py:304
  (188 shorter events, 65.6 us)
Async XLA Ops:
  0.0 10.5 %copy-start = (bf16[2,3,3072]{2,0,1:T(2,128)(2,1)S(1)}, bf16[2,3,3072]{2,0,1:T(2,128)(2,1)}, u32[]{:S(2)}) copy-start(bf16[2,3,3072]{2,0,1:T(2,128)(2,1)} %param.11) | copy-start | bytes 110596
  0.0 11.9 %copy-start.5 = (bf16[1,3072,72]{1,2,0:T(8,128)(2,1)S(1)}, bf16[1,3072,72]{1,2,0:T(8,128)(2,1)}, u32[]{:S(2)}) copy-start(bf16[1,3072,72]{1,2,0:T(8,128)(2,1)} %param.12) | copy-start | bytes 1327108
  0.0 10.5 %copy-start.8 = (s32[2,128]{1,0:T(2,128)S(1)}, s32[2,128]{1,0:T(2,128)}, u32[]{:S(2)}) copy-start(s32[2,128]{1,0:T(2,128)} %param.17) | copy-start | bytes 3076
  1.6 12.5 %collective-permute-start.3 = (bf16[1,3,6144]{2,1,0:T(4,128)(2,1)S(1)}, bf16[1,3,6144]{2,1,0:T(4,128)(2,1)}, u32[]{:S(2)}, u32[]{:S(2)}) collective-permute-start(bf16[1,3,6144]{2,1,0:T(4,128)(2,1)S(1)} %get-tuple-element.277), channel_id=1, source_target_pairs={{0,128},{128,0},{1,129},{129,1},{2,130},{130,2},{3,131},{131,3},{4... | collective-permute-start | bytes 110600 | tf_op jit(solution)/shard_map/ppermute | solution.py:256
  5.6 6.7 %collective-permute-start.2 = (s32[2]{0:T(128)S(1)}, s32[2]{0:T(128)S(1)}, u32[]{:S(2)}, u32[]{:S(2)}) collective-permute-start(s32[2]{0:T(128)S(1)} %fusion.28), channel_id=1, source_target_pairs={{0,128},{128,0},{1,129},{129,1},{2,130},{130,2},{3,131},{131,3},{4... | collective-permute-start | bytes 32 | tf_op jit(solution)/shard_map/ppermute | solution.py:256
  5.7 7.2 %collective-permute-start.1 = (bf16[3072,72]{0,1:T(8,128)(2,1)}, bf16[3072,72]{0,1:T(8,128)(2,1)S(1)}, u32[]{:S(2)}, u32[]{:S(2)}) collective-permute-start(bf16[3072,72]{0,1:T(8,128)(2,1)} %bitcast.175), channel_id=1, source_target_pairs={{0,128},{128,0},{1,129},{129,1},{2,130},{130,2},{3,131},{131,3},{4... | collective-permute-start | bytes 1327112 | tf_op jit(solution)/shard_map/ppermute | solution.py:256
  6.2 7.9 %collective-permute-start.4 = (bf16[3072,24]{0,1:T(8,128)(2,1)}, bf16[3072,24]{0,1:T(8,128)(2,1)S(1)}, u32[]{:S(2)}, u32[]{:S(2)}) collective-permute-start(bf16[3072,24]{0,1:T(8,128)(2,1)} %bitcast.170), channel_id=1, source_target_pairs={{0,128},{128,0},{1,129},{129,1},{2,130},{130,2},{3,131},{131,3},{4... | collective-permute-start | bytes 442376 | tf_op jit(solution)/shard_map/ppermute | solution.py:256
  7.0 7.1 %copy-start.3 = (bf16[1,3072,24]{1,2,0:T(8,128)(2,1)S(1)}, bf16[1,3072,24]{1,2,0:T(8,128)(2,1)}, u32[]{:S(2)}) copy-start(bf16[1,3072,24]{1,2,0:T(8,128)(2,1)} %param.13) | copy-start | bytes 442372
  10.1 4.0 %collective-permute-start = (f32[3,3072]{1,0:T(4,128)}, f32[3,3072]{1,0:T(4,128)}, u32[]{:S(2)}, u32[]{:S(2)}) collective-permute-start(f32[3,3072]{1,0:T(4,128)} %bitcast.96), channel_id=1, source_target_pairs={{0,128},{128,0},{1,129},{129,1},{2,130},{130,2},{3,131},{131,3},{4... | collective-permute-start | bytes 110600 | tf_op jit(solution)/shard_map/ppermute | solution.py:256
  53.3 14.4 %copy-start.4 = (bf16[1,3,6144]{2,1,0:T(4,128)(2,1)S(1)}, bf16[1,3,6144]{2,1,0:T(4,128)(2,1)}, u32[]{:S(2)}) copy-start(bf16[1,3,6144]{2,1,0:T(4,128)(2,1)} %get-tuple-element.472) | copy-start | bytes 110596 | tf_op jit(solution)/shard_map/while
  57.4 22.1 %all-to-all-start = ((bf16[1,384,72]{2,0,1:T(2,128)(2,1)}), bf16[1,384,72]{2,0,1:T(2,128)(2,1)S(1)}, u32[]{:S(2)}, u32[]{:S(2)}) async-start(bf16[1,384,72]{2,0,1:T(2,128)(2,1)} %reshape.399), calls=%async_computation | async-start | bytes 393216 | tf_op jit(solution)/shard_map/while/body/eval_jaxpr/all_to_all | solution.py:215
  130.7 3.0 copy-start.1
  161.7 1.8 copy-start.2
  166.8 23.3 %copy-start.6 = (bf16[2,1,3,3072]{3,2,1,0:T(4,128)(2,1)S(1)}, bf16[2,1,3,3072]{3,2,1,0:T(4,128)(2,1)}, u32[]{:S(2)}) copy-start(bf16[2,1,3,3072]{3,2,1,0:T(4,128)(2,1)} %get-tuple-element.443) | copy-start | bytes 110596 | tf_op jit(solution)/shard_map/while
  170.6 19.0 %all-to-all-start.1 = ((bf16[1,384,24]{2,0,1:T(2,128)(2,1)}), bf16[1,384,24]{2,0,1:T(2,128)(2,1)S(1)}, u32[]{:S(2)}, u32[]{:S(2)}) async-start(bf16[1,384,24]{2,0,1:T(2,128)(2,1)} %reshape.406), calls=%async_computation.1 | async-start | bytes 393216 | tf_op jit(solution)/shard_map/while/body/eval_jaxpr/all_to_all | solution.py:251
  190.1 0.6 copy-start.7
  225.3 11.0 %copy-start.4 = (bf16[1,3,6144]{2,1,0:T(4,128)(2,1)S(1)}, bf16[1,3,6144]{2,1,0:T(4,128)(2,1)}, u32[]{:S(2)}) copy-start(bf16[1,3,6144]{2,1,0:T(4,128)(2,1)} %get-tuple-element.472) | copy-start | bytes 110596 | tf_op jit(solution)/shard_map/while
  229.2 18.9 %all-to-all-start = ((bf16[1,384,72]{2,0,1:T(2,128)(2,1)}), bf16[1,384,72]{2,0,1:T(2,128)(2,1)S(1)}, u32[]{:S(2)}, u32[]{:S(2)}) async-start(bf16[1,384,72]{2,0,1:T(2,128)(2,1)} %reshape.399), calls=%async_computation | async-start | bytes 393216 | tf_op jit(solution)/shard_map/while/body/eval_jaxpr/all_to_all | solution.py:215
  294.8 3.0 copy-start.1
  325.5 1.8 copy-start.2
  330.6 23.6 %copy-start.6 = (bf16[2,1,3,3072]{3,2,1,0:T(4,128)(2,1)S(1)}, bf16[2,1,3,3072]{3,2,1,0:T(4,128)(2,1)}, u32[]{:S(2)}) copy-start(bf16[2,1,3,3072]{3,2,1,0:T(4,128)(2,1)} %get-tuple-element.443) | copy-start | bytes 110596 | tf_op jit(solution)/shard_map/while
  334.4 19.3 %all-to-all-start.1 = ((bf16[1,384,24]{2,0,1:T(2,128)(2,1)}), bf16[1,384,24]{2,0,1:T(2,128)(2,1)S(1)}, u32[]{:S(2)}, u32[]{:S(2)}) async-start(bf16[1,384,24]{2,0,1:T(2,128)(2,1)} %reshape.406), calls=%async_computation.1 | async-start | bytes 393216 | tf_op jit(solution)/shard_map/while/body/eval_jaxpr/all_to_all | solution.py:251
  355.7 35.3 %collective-permute-start.5 = (bf16[1,3,3072]{2,1,0:T(4,128)(2,1)S(1)}, bf16[1,3,3072]{2,1,0:T(4,128)(2,1)S(1)}, u32[]{:S(2)}, u32[]{:S(2)}) collective-permute-start(bf16[1,3,3072]{2,1,0:T(4,128)(2,1)S(1)} %get-tuple-element.280), channel_id=1, source_target_pairs={{128,0},{129,1},{130,2},{131,3},{132,4},{133,5},{134,6},{135,7},{1... | collective-permute-start | bytes 55304 | tf_op jit(solution)/shard_map/ppermute | solution.py:304
  389.7 3.1 collective-permute-start.6
  (1 other events, 0.6 us)

commit v12 on v10

--- a/solution.py
+++ b/solution.py
@@ -15,7 +15,9 @@
 PLANE = NX * NY
 
 
-def gather_kernel(n, x_ref, oa_ref, ob_ref, zbuf, zs, zr, rs, rr, local_sem):
+def gather_kernel(n, x_ref, o_ref, zbuf, zs, zr, rs, rr, local_sem):
+    oa_ref = o_ref.at[0]
+    ob_ref = o_ref.at[1]
     sec = lax.axis_index("section")
     nz = n // PLANE
     h = nz // 2
@@ -145,14 +147,12 @@
 def gather_blk(x, n, cid, active=None):
     nz = n // PLANE
     h = nz // 2
-    oa, ob = pl.pallas_call(
+    assert NX == NY and nz == 2 * h
+    out = pl.pallas_call(
         functools.partial(gather_kernel, n),
-        out_shape=(
-            jax.ShapeDtypeStruct((NY, NX, h) + x.shape, x.dtype),
-            jax.ShapeDtypeStruct((NX, NY, nz - h) + x.shape, x.dtype),
-        ),
+        out_shape=jax.ShapeDtypeStruct((2, NY, NX, h) + x.shape, x.dtype),
         in_specs=[pl.BlockSpec(memory_space=pl.ANY)],
-        out_specs=(pl.BlockSpec(memory_space=pl.ANY), pl.BlockSpec(memory_space=pl.ANY)),
+        out_specs=pl.BlockSpec(memory_space=pl.ANY),
         scratch_shapes=[
             pltpu.VMEM((nz,) + x.shape, x.dtype),
             pltpu.SemaphoreType.DMA((nz,)),
@@ -163,7 +163,7 @@
         ],
         compiler_params=pltpu.CompilerParams(collective_id=cid, has_side_effects=True),
     )(x)
-    return jnp.concatenate([oa.reshape((-1,) + x.shape), ob.reshape((-1,) + x.shape)], axis=0)
+    return out.reshape((n,) + x.shape)
 
 
 def gather_rows(x, cid, active):

time: 389 us -> 380 us (0.977)
  other arithmetic: 24.6 us -> 8.35 us
  local copies, waits for them, and re-layouts: 50.8 us -> 58.4 us
    concatenate x6 -> x0, other arithmetic: 16.2 us -> none  [gather_blk(): jnp.concatenate([oa.reshape((-1,) + x.shape), ob.reshape((-1,) + x.shape)...]
    slice x0 -> x4, local copies, waits for them, and re-layouts: none -> 6.38 us  [gather_rows(): out = out[:, :size]]
    unnamed x50 -> x38, local copies, waits for them, and re-layouts: 9.19 us -> 10.5 us
  transfers between devices with their start and end apart: 10 -> 10, of which waited for: 3 -> 3; matrix products, arithmetic and copies ran while one was open for 12% -> 11% of each run, Pallas kernels for 24% -> 25%
where the time goes in v12:
time: 380 us; the launch traced here: 379 us
  Pallas kernels  180 us (47%)
  starting transfers between devices  60.6 us (16%)
  local copies, waits for them, and re-layouts  58.4 us (15%)
  waiting for transfers between devices  32.4 us (9%)
  blocking collectives  19.2 us (5%)
  matrix products  16 us (4%)
  other arithmetic  8.35 us (2%)
  between operations  3.99 us (1%)
    pallas_call x6, Pallas kernels, gather_blk(): pl.pallas_call(functools.partial(gather_kernel, n), out_shape=jax.ShapeDt...  180 us
    ppermute x1, starting transfers between devices, per_device(): first_req1 = lax.ppermute(outs[0], 'section', [(1, 0)])  29.3 us
    all_to_all x2, waiting for transfers between devices, attend(): lax.all_to_all(to_blk_order(columns, n), 'blk', split_axis=1, concat_axis...  20.7 us
    all_to_all x1, blocking collectives, attend(): lax.all_to_all(to_blk_order(out_part, n), 'blk', split_axis=1, concat_axi...  19.2 us
    all_to_all x2, starting transfers between devices, attend(): lax.all_to_all(to_blk_order(columns, n), 'blk', split_axis=1, concat_axis...  17.1 us
    another operation x2, local copies, waits for them, and re-layouts, gather_rows(): return out.reshape(n * rows, width)  15.4 us
    reshape x4, local copies, waits for them, and re-layouts, gather_rows(): return out.reshape(n * rows, width)  13 us
    ppermute x1, waiting for transfers between devices, per_device(): second_req0 = lax.ppermute(outs[1], 'section', [(0, 1)])  11.7 us
  transfers between devices with their start and end apart: 10, of which 3 were waited for; matrix products, arithmetic and copies ran while one was open for 11% of the time, Pallas kernels for 25%

profile of v12, /device:TPU:1, one launch (start us, length us, event | category | flops | bytes accessed | tf_op | source)
XLA Modules:
  0.0 378.6 jit_solution(16988508641323770718)
XLA Ops:
  0.7 2.4 fusion.2
  3.1 3.3 collective-permute-start
  16.1 30.5 %shard_map.91 = bf16[2,4,4,4,80,128]{5,4,3,2,1,0:T(8,128)(2,1)} custom-call(bf16[80,128]{1,0:T(8,128)(2,1)} %pad_bitcast_fusion.3.x_ref), custom_call_target="tpu_custom_call" | custom-call | tf_op jit(solution)/shard_map/pallas_call | solution.py:151
  50.6 3.3 reshape.368
  56.2 10.4 %all-to-all-start = ((bf16[1,384,72]{2,0,1:T(2,128)(2,1)}), bf16[1,384,72]{2,0,1:T(2,128)(2,1)S(1)}, u32[]{:S(2)}, u32[]{:S(2)}) async-start(bf16[1,384,72]{2,0,1:T(2,128)(2,1)} %reshape.400), calls=%async_computation | async-start | bytes 393216 | tf_op jit(solution)/shard_map/all_to_all | solution.py:215
  68.1 10.2 %all-to-all-done = bf16[1,384,72]{2,0,1:T(2,128)(2,1)S(1)} async-done(((bf16[1,384,72]{2,0,1:T(2,128)(2,1)}), bf16[1,384,72]{2,0,1:T(2,128)(2,1)S(1)}, u32[]{:S(2)}, u32[]{:S(2)}) %all-to-all-start) | async-done | bytes 55328 | tf_op jit(solution)/shard_map/all_to_all | solution.py:215
  80.0 36.9 %shard_map.92 = bf16[2,4,4,4,144,128]{5,4,3,2,1,0:T(8,128)(2,1)} custom-call(bf16[144,128]{1,0:T(8,128)(2,1)} %reshape_reshape.19.x_ref), custom_call_target="tpu_custom_call" | custom-call | tf_op jit(solution)/shard_map/pallas_call | solution.py:151
  116.9 7.7 %reshape_reshape_reshape.6 = bf16[384,6144]{1,0:T(8,128)(2,1)} reshape(bf16[2,4,4,4,144,128]{5,4,3,2,1,0:T(8,128)(2,1)} %shard_map.92) | data formatting | bytes 9437184 | tf_op jit(solution)/shard_map/reshape;reshape;reshape | solution.py:183
  124.7 2.8 fusion.59
  131.4 25.6 %shard_map.93 = bf16[2,4,4,4,80,128]{5,4,3,2,1,0:T(8,128)(2,1)} custom-call(bf16[80,128]{1,0:T(8,128)(2,1)} %pad_bitcast_fusion.2.x_ref), custom_call_target="tpu_custom_call" | custom-call | tf_op jit(solution)/shard_map/pallas_call | solution.py:151
  161.0 3.2 reshape.374
  166.6 19.2 %all_to_all.54 = bf16[1,384,24]{2,0,1:T(2,128)(2,1)S(1)} all-to-all(bf16[1,384,24]{2,0,1:T(2,128)(2,1)S(1)} %reshape.401), channel_id=1, replica_groups=mesh['section'=2,'blk'=128] {'blk'}, dimensions={1} | all-to-all | bytes 36864 | tf_op jit(solution)/shard_map/all_to_all | solution.py:251
  187.5 27.8 %shard_map.94 = bf16[2,4,4,4,80,128]{5,4,3,2,1,0:T(8,128)(2,1)} custom-call(bf16[80,128]{1,0:T(8,128)(2,1)} %pad_bitcast_fusion.1.x_ref), custom_call_target="tpu_custom_call" | custom-call | tf_op jit(solution)/shard_map/pallas_call | solution.py:151
  219.4 3.2 reshape.380
  224.8 6.7 %all-to-all-start.2 = ((bf16[1,384,72]{2,0,1:T(2,128)(2,1)}), bf16[1,384,72]{2,0,1:T(2,128)(2,1)S(1)}, u32[]{:S(2)}, u32[]{:S(2)}) async-start(bf16[1,384,72]{2,0,1:T(2,128)(2,1)} %reshape.402), calls=%async_computation.2 | async-start | bytes 393216 | tf_op jit(solution)/shard_map/all_to_all | solution.py:215
  232.8 10.4 %all-to-all-done.2 = bf16[1,384,72]{2,0,1:T(2,128)(2,1)S(1)} async-done(((bf16[1,384,72]{2,0,1:T(2,128)(2,1)}), bf16[1,384,72]{2,0,1:T(2,128)(2,1)S(1)}, u32[]{:S(2)}, u32[]{:S(2)}) %all-to-all-start.2) | async-done | bytes 55328 | tf_op jit(solution)/shard_map/all_to_all | solution.py:215
  244.9 34.1 %shard_map.95 = bf16[2,4,4,4,144,128]{5,4,3,2,1,0:T(8,128)(2,1)} custom-call(bf16[144,128]{1,0:T(8,128)(2,1)} %reshape_reshape.22.x_ref), custom_call_target="tpu_custom_call" | custom-call | tf_op jit(solution)/shard_map/pallas_call | solution.py:151
  279.0 7.7 %reshape_reshape_reshape.7 = bf16[384,6144]{1,0:T(8,128)(2,1)} reshape(bf16[2,4,4,4,144,128]{5,4,3,2,1,0:T(8,128)(2,1)} %shard_map.95) | data formatting | bytes 9437184 | tf_op jit(solution)/shard_map/reshape;reshape;reshape | solution.py:183
  286.7 2.8 fusion.60
  292.3 24.8 %shard_map.96 = bf16[2,4,4,4,80,128]{5,4,3,2,1,0:T(8,128)(2,1)} custom-call(bf16[80,128]{1,0:T(8,128)(2,1)} %pad_bitcast_fusion.x_ref), custom_call_target="tpu_custom_call" | custom-call | tf_op jit(solution)/shard_map/pallas_call | solution.py:151
  321.0 3.2 reshape.386
  326.4 8.6 %all-to-all-start.3 = ((bf16[1,384,24]{2,0,1:T(2,128)(2,1)}), bf16[1,384,24]{2,0,1:T(2,128)(2,1)S(1)}, u32[]{:S(2)}, u32[]{:S(2)}) async-start(bf16[1,384,24]{2,0,1:T(2,128)(2,1)} %reshape.403), calls=%async_computation.3 | async-start | bytes 393216 | tf_op jit(solution)/shard_map/all_to_all | solution.py:251
  335.0 29.3 %collective-permute-start.5 = (bf16[1,3,3072]{2,0,1:T(2,128)(2,1)S(1)}, bf16[1,3,3072]{2,0,1:T(2,128)(2,1)S(1)}, u32[]{:S(2)}, u32[]{:S(2)}) collective-permute-start(bf16[1,3,3072]{2,0,1:T(2,128)(2,1)S(1)} %get-tuple-element.8), channel_id=1, source_target_pairs={{128,0},{129,1},{130,2},{131,3},{132,4},{133,5},{134,6},{135,7},{1... | collective-permute-start | bytes 55304 | tf_op jit(solution)/shard_map/ppermute | solution.py:301
  366.1 11.7 %collective-permute-done.6 = bf16[1,3,3072]{2,0,1:T(2,128)(2,1)S(1)} collective-permute-done((bf16[1,3,3072]{2,0,1:T(2,128)(2,1)S(1)}, bf16[1,3,3072]{2,0,1:T(2,128)(2,1)S(1)}, u32[]{:S(2)}, u32[]{:S(2)}) %collective-permute-start.6) | collective-permute-done | bytes 18464 | tf_op jit(solution)/shard_map/ppermute | solution.py:302
  (168 shorter events, 48.7 us)
Async XLA Ops:
  0.0 10.2 %copy-start = (s32[2,128]{1,0:T(2,128)S(1)}, s32[2,128]{1,0:T(2,128)}, u32[]{:S(2)}) copy-start(s32[2,128]{1,0:T(2,128)} %param.15) | copy-start | bytes 3076
  0.0 9.1 %copy-start.14 = (s32[1,2,128]{2,1,0:T(2,128)S(1)}, s32[1,2,128]{2,1,0:T(2,128)}, u32[]{:S(2)}) copy-start(s32[1,2,128]{2,1,0:T(2,128)} %param.14) | copy-start | bytes 3076
  0.0 9.4 %copy-start.5 = (bf16[1,3072,24]{1,2,0:T(8,128)(2,1)S(1)}, bf16[1,3072,24]{1,2,0:T(8,128)(2,1)}, u32[]{:S(2)}) copy-start(bf16[1,3072,24]{1,2,0:T(8,128)(2,1)} %param.11) | copy-start | bytes 442372
  0.0 9.8 %copy-start.6 = (bf16[2,3,3072]{2,0,1:T(2,128)(2,1)S(1)}, bf16[2,3,3072]{2,0,1:T(2,128)(2,1)}, u32[]{:S(2)}) copy-start(bf16[2,3,3072]{2,0,1:T(2,128)(2,1)} %param.9) | copy-start | bytes 110596
  3.1 11.4 %collective-permute-start = (f32[3,3072]{1,0:T(4,128)S(1)}, f32[3,3072]{1,0:T(4,128)S(1)}, u32[]{:S(2)}, u32[]{:S(2)}) collective-permute-start(f32[3,3072]{1,0:T(4,128)S(1)} %bitcast.197), channel_id=1, source_target_pairs={{0,128},{128,0},{1,129},{129,1},{2,130},{130,2},{3,131},{131,3},{4... | collective-permute-start | bytes 110600 | tf_op jit(solution)/shard_map/ppermute | solution.py:256
  6.5 47.5 %collective-permute-start.1 = (bf16[3072,72]{0,1:T(8,128)(2,1)}, bf16[3072,72]{0,1:T(8,128)(2,1)S(1)}, u32[]{:S(2)}, u32[]{:S(2)}) collective-permute-start(bf16[3072,72]{0,1:T(8,128)(2,1)} %bitcast.179), channel_id=1, source_target_pairs={{0,128},{128,0},{1,129},{129,1},{2,130},{130,2},{3,131},{131,3},{4... | collective-permute-start | bytes 1327112 | tf_op jit(solution)/shard_map/ppermute | solution.py:256
  8.7 57.9 %collective-permute-start.3 = (bf16[1,3,6144]{2,1,0:T(4,128)(2,1)}, bf16[1,3,6144]{2,1,0:T(4,128)(2,1)}, u32[]{:S(2)}, u32[]{:S(2)}) collective-permute-start(bf16[1,3,6144]{2,1,0:T(4,128)(2,1)} %fusion.35), channel_id=1, source_target_pairs={{0,128},{128,0},{1,129},{129,1},{2,130},{130,2},{3,131},{131,3},{4... | collective-permute-start | bytes 110600 | tf_op jit(solution)/shard_map/ppermute | solution.py:256
  9.2 3.5 collective-permute-start.2
  9.4 154.9 %collective-permute-start.4 = (bf16[3072,24]{0,1:T(8,128)(2,1)S(1)}, bf16[3072,24]{0,1:T(8,128)(2,1)}, u32[]{:S(2)}, u32[]{:S(2)}) collective-permute-start(bf16[3072,24]{0,1:T(8,128)(2,1)S(1)} %bitcast.182), channel_id=1, source_target_pairs={{0,128},{128,0},{1,129},{129,1},{2,130},{130,2},{3,131},{131,3},{4... | collective-permute-start | bytes 442376 | tf_op jit(solution)/shard_map/ppermute | solution.py:256
  12.6 112.0 %copy-start.12 = (pred[384]{0:T(512)(128)(4,1)}, pred[384]{0:T(512)(128)(4,1)S(1)}, u32[]{:S(2)}) copy-start(pred[384]{0:T(512)(128)(4,1)S(1)} %eq.90) | copy-start | bytes 1156
  50.6 3.3 copy-start.4
  56.2 22.2 %all-to-all-start = ((bf16[1,384,72]{2,0,1:T(2,128)(2,1)}), bf16[1,384,72]{2,0,1:T(2,128)(2,1)S(1)}, u32[]{:S(2)}, u32[]{:S(2)}) async-start(bf16[1,384,72]{2,0,1:T(2,128)(2,1)} %reshape.400), calls=%async_computation | async-start | bytes 393216 | tf_op jit(solution)/shard_map/all_to_all | solution.py:215
  116.9 7.8 %copy-start.9 = (pred[48,3072]{1,0:T(8,128)(4,1)S(1)}, pred[48,3072]{1,0:T(8,128)(4,1)}, u32[]{:S(2)}) copy-start(pred[48,3072]{1,0:T(8,128)(4,1)} %iota_compare_fusion) | copy-start | bytes 442372
  124.7 3.6 copy-start.3
  164.2 22.0 %copy-start.11 = (f32[1,3072]{1,0:T(1,128)S(1)}, f32[1,3072]{1,0:T(1,128)}, u32[]{:S(2)}) copy-start(f32[1,3072]{1,0:T(1,128)} %get-tuple-element.41) | copy-start | bytes 36868
  223.4 20.7 %copy-start.8 = (bf16[1,3,6144]{2,1,0:T(4,128)(2,1)S(1)}, bf16[1,3,6144]{2,1,0:T(4,128)(2,1)}, u32[]{:S(2)}) copy-start(bf16[1,3,6144]{2,1,0:T(4,128)(2,1)} %get-tuple-element.9) | copy-start | bytes 110596
  224.8 18.4 %all-to-all-start.2 = ((bf16[1,384,72]{2,0,1:T(2,128)(2,1)}), bf16[1,384,72]{2,0,1:T(2,128)(2,1)S(1)}, u32[]{:S(2)}, u32[]{:S(2)}) async-start(bf16[1,384,72]{2,0,1:T(2,128)(2,1)} %reshape.402), calls=%async_computation.2 | async-start | bytes 393216 | tf_op jit(solution)/shard_map/all_to_all | solution.py:215
  279.0 7.7 %copy-start.10 = (pred[48,3072]{1,0:T(8,128)(4,1)S(1)}, pred[48,3072]{1,0:T(8,128)(4,1)}, u32[]{:S(2)}) copy-start(pred[48,3072]{1,0:T(8,128)(4,1)} %iota_compare_fusion) | copy-start | bytes 442372
  279.0 7.7 %copy-start.13 = (pred[384]{0:T(512)(128)(4,1)S(1)}, pred[384]{0:T(512)(128)(4,1)}, u32[]{:S(2)}) copy-start(pred[384]{0:T(512)(128)(4,1)} %copy-done.12) | copy-start | bytes 1156
  286.7 3.0 copy-start.2
  324.3 54.3 %copy-start.1 = (s32[2,128]{1,0:T(2,128)S(1)}, s32[2,128]{1,0:T(2,128)}, u32[]{:S(2)}) copy-start(s32[2,128]{1,0:T(2,128)} %param.15) | copy-start | bytes 3076
  326.4 37.8 %all-to-all-start.3 = ((bf16[1,384,24]{2,0,1:T(2,128)(2,1)}), bf16[1,384,24]{2,0,1:T(2,128)(2,1)S(1)}, u32[]{:S(2)}, u32[]{:S(2)}) async-start(bf16[1,384,24]{2,0,1:T(2,128)(2,1)} %reshape.403), calls=%async_computation.3 | async-start | bytes 393216 | tf_op jit(solution)/shard_map/all_to_all | solution.py:251
  335.0 31.1 %collective-permute-start.5 = (bf16[1,3,3072]{2,0,1:T(2,128)(2,1)S(1)}, bf16[1,3,3072]{2,0,1:T(2,128)(2,1)S(1)}, u32[]{:S(2)}, u32[]{:S(2)}) collective-permute-start(bf16[1,3,3072]{2,0,1:T(2,128)(2,1)S(1)} %get-tuple-element.8), channel_id=1, source_target_pairs={{128,0},{129,1},{130,2},{131,3},{132,4},{133,5},{134,6},{135,7},{1... | collective-permute-start | bytes 55304 | tf_op jit(solution)/shard_map/ppermute | solution.py:301
  364.7 13.1 %collective-permute-start.6 = (bf16[1,3,3072]{2,0,1:T(2,128)(2,1)S(1)}, bf16[1,3,3072]{2,0,1:T(2,128)(2,1)S(1)}, u32[]{:S(2)}, u32[]{:S(2)}) collective-permute-start(bf16[1,3,3072]{2,0,1:T(2,128)(2,1)S(1)} %add_convert_fusion), channel_id=1, source_target_pairs={{0,128},{1,129},{2,130},{3,131},{4,132},{5,133},{6,134},{7,135},{8... | collective-permute-start | bytes 55304 | tf_op jit(solution)/shard_map/ppermute | solution.py:302
  (1 other events, 0.6 us)

commit v13 on v12

--- a/solution.py
+++ b/solution.py
@@ -183,6 +183,24 @@
     return out.reshape(n * rows, width)
 
 
+def gather_tokens(x, cid):
+    n = lax.axis_size("blk")
+    _, rows, width = x.shape
+    chunks = width // 128
+    per_token = -(-chunks // 16) * 16
+    shard = jnp.pad(x.reshape(rows, chunks, 128), ((0, 0), (0, per_token - chunks), (0, 0)))
+    out = gather_blk(shard.reshape(rows * per_token, 128), n, cid)
+    return out.reshape(n * rows, per_token, 128)[:, :chunks]
+
+
+def dot_tokens(tokens, weight):
+    chunks = tokens.shape[1]
+    return jnp.einsum(
+        "tal,alc->tc", tokens, weight.reshape(chunks, 128, weight.shape[1]),
+        preferred_element_type=jnp.float32,
+    ).astype(jnp.bfloat16)
+
+
 def to_blk_order(rows_in_gather_order, n):
     total, cols = rows_in_gather_order.shape
     nz = n // PLANE
@@ -209,9 +227,7 @@
     variance = jnp.mean((stream - center) ** 2, axis=-1, keepdims=True)
     normed = (stream - center) / jnp.sqrt(variance + 1e-06) * (1.0 + modulate[0]) + modulate[1]
     normed_b = normed.astype(jnp.bfloat16)
-    columns = jnp.dot(
-        gather_rows(normed_b, 0, active), qkv_cols, preferred_element_type=jnp.float32
-    ).astype(jnp.bfloat16)
+    columns = dot_tokens(gather_tokens(normed_b, 2), qkv_cols)
     projected = lax.all_to_all(to_blk_order(columns, n), "blk", split_axis=1, concat_axis=2, tiled=True)
     num_req, num_rows, width = layer_in.shape
     queries = projected[0, :, :width]
@@ -245,9 +261,7 @@
     own_head = jnp.sum(jnp.where(in_head[None], mixed_all, 0.0), axis=1)
     total_col = jnp.broadcast_to(total[:, :, None], (num_rows, num_heads, 64)).reshape(num_rows, width)
     attn = (own_head / total_col).astype(jnp.bfloat16)[None]
-    out_part = jnp.dot(
-        gather_rows(attn, 0, active), out_cols, preferred_element_type=jnp.float32
-    ).astype(jnp.bfloat16)
+    out_part = dot_tokens(gather_tokens(attn, 2), out_cols)
     mixed_back = lax.all_to_all(to_blk_order(out_part, n), "blk", split_axis=1, concat_axis=2, tiled=True)
     return (stream + modulate[2] * mixed_back.astype(jnp.float32)).astype(jnp.bfloat16)
 

time: 380 us -> 363 us (0.955)
  local copies, waits for them, and re-layouts: 58.4 us -> 37.5 us
  Pallas kernels: 180 us -> 187 us
  other arithmetic: 8.35 us -> 4.52 us
    reshape x10 -> x0, local copies, waits for them, and re-layouts: 15.5 us -> none  [the longest x4 13 us: gather_rows(): return out.reshape(n * rows, width)]
    unnamed x38 -> x20, local copies, waits for them, and re-layouts: 10.5 us -> 0.63 us
    pallas_call x6, Pallas kernels: 180 us -> 187 us  [gather_blk(): pl.pallas_call(functools.partial(gather_kernel, n), out_shape=jax.ShapeDt...]
  transfers between devices with their start and end apart: 10 -> 10, of which waited for: 3 -> 3; matrix products, arithmetic and copies ran while one was open for 11% -> 3% of each run, Pallas kernels for 25% -> 9%
where the time goes in v13:
time: 363 us; the launch traced here: 362 us
  Pallas kernels  187 us (52%)
  starting transfers between devices  59.9 us (17%)
  local copies, waits for them, and re-layouts  37.5 us (10%)
  waiting for transfers between devices  34.1 us (9%)
  blocking collectives  20.4 us (6%)
  matrix products  14.4 us (4%)
  other arithmetic  4.52 us (1%)
  between operations  4.02 us (1%)
    pallas_call x6, Pallas kernels, gather_blk(): pl.pallas_call(functools.partial(gather_kernel, n), out_shape=jax.ShapeDt...  187 us
    ppermute x1, starting transfers between devices, per_device(): first_req1 = lax.ppermute(outs[0], 'section', [(1, 0)])  28.8 us
    all_to_all x2, waiting for transfers between devices, attend(): lax.all_to_all(to_blk_order(columns, n), 'blk', split_axis=1, concat_axis...  22.3 us
    all_to_all x1, blocking collectives, attend(): lax.all_to_all(to_blk_order(out_part, n), 'blk', split_axis=1, concat_axi...  20.4 us
    all_to_all x2, starting transfers between devices, attend(): lax.all_to_all(to_blk_order(columns, n), 'blk', split_axis=1, concat_axis...  16.9 us
    another operation x2, local copies, waits for them, and re-layouts, gather_rows(): return out.reshape(n * rows, width)  15.4 us
    ppermute x1, waiting for transfers between devices, per_device(): second_req0 = lax.ppermute(outs[1], 'section', [(0, 1)])  11.7 us
    all_to_all x1, starting transfers between devices, attend(): lax.all_to_all(to_blk_order(out_part, n), 'blk', split_axis=1, concat_axi...  8.43 us
  transfers between devices with their start and end apart: 10, of which 3 were waited for; matrix products, arithmetic and copies ran while one was open for 3% of the time, Pallas kernels for 9%

profile of v13, /device:TPU:1, one launch (start us, length us, event | category | flops | bytes accessed | tf_op | source)
XLA Modules:
  0.0 361.8 jit_solution(11562600221240919629)
XLA Ops:
  0.7 2.4 fusion.10
  3.1 3.3 collective-permute-start
  13.9 33.3 %shard_map.91 = bf16[2,4,4,4,96,128]{5,4,3,2,1,0:T(8,128)(2,1)} custom-call(bf16[96,128]{1,0:T(8,128)(2,1)} %bitcast.208), custom_call_target="tpu_custom_call" | custom-call | tf_op jit(solution)/shard_map/pallas_call | solution.py:151
  47.2 2.1 slice.149
  51.7 10.4 %all-to-all-start = ((bf16[1,384,72]{2,0,1:T(2,128)(2,1)}), bf16[1,384,72]{2,0,1:T(2,128)(2,1)S(1)}, u32[]{:S(2)}, u32[]{:S(2)}) async-start(bf16[1,384,72]{2,0,1:T(2,128)(2,1)} %reshape.404), calls=%async_computation | async-start | bytes 393216 | tf_op jit(solution)/shard_map/all_to_all | solution.py:231
  62.2 11.7 %all-to-all-done = bf16[1,384,72]{2,0,1:T(2,128)(2,1)S(1)} async-done(((bf16[1,384,72]{2,0,1:T(2,128)(2,1)}), bf16[1,384,72]{2,0,1:T(2,128)(2,1)S(1)}, u32[]{:S(2)}, u32[]{:S(2)}) %all-to-all-start) | async-done | bytes 55328 | tf_op jit(solution)/shard_map/all_to_all | solution.py:231
  75.5 36.8 %shard_map.92 = bf16[2,4,4,4,144,128]{5,4,3,2,1,0:T(8,128)(2,1)} custom-call(bf16[144,128]{1,0:T(8,128)(2,1)} %reshape_reshape.19.x_ref), custom_call_target="tpu_custom_call" | custom-call | tf_op jit(solution)/shard_map/pallas_call | solution.py:151
  112.3 7.7 %reshape_reshape_reshape.6 = bf16[384,6144]{1,0:T(8,128)(2,1)} reshape(bf16[2,4,4,4,144,128]{5,4,3,2,1,0:T(8,128)(2,1)} %shard_map.92) | data formatting | bytes 9437184 | tf_op jit(solution)/shard_map/reshape;reshape;reshape | solution.py:183
  120.1 2.8 fusion.89
  125.8 26.8 %shard_map.93 = bf16[2,4,4,4,96,128]{5,4,3,2,1,0:T(8,128)(2,1)} custom-call(bf16[96,128]{1,0:T(8,128)(2,1)} %bitcast.209), custom_call_target="tpu_custom_call" | custom-call | tf_op jit(solution)/shard_map/pallas_call | solution.py:151
  152.6 2.1 slice.159
  156.1 20.4 %all_to_all.54 = bf16[1,384,24]{2,0,1:T(2,128)(2,1)S(1)} all-to-all(bf16[1,384,24]{2,0,1:T(2,128)(2,1)S(1)} %reshape.405), channel_id=1, replica_groups=mesh['section'=2,'blk'=128] {'blk'}, dimensions={1} | all-to-all | bytes 36864 | tf_op jit(solution)/shard_map/all_to_all | solution.py:265
  178.1 29.9 %shard_map.94 = bf16[2,4,4,4,96,128]{5,4,3,2,1,0:T(8,128)(2,1)} custom-call(bf16[96,128]{1,0:T(8,128)(2,1)} %bitcast.210), custom_call_target="tpu_custom_call" | custom-call | tf_op jit(solution)/shard_map/pallas_call | solution.py:151
  208.0 2.1 slice.165
  212.4 6.4 %all-to-all-start.2 = ((bf16[1,384,72]{2,0,1:T(2,128)(2,1)}), bf16[1,384,72]{2,0,1:T(2,128)(2,1)S(1)}, u32[]{:S(2)}, u32[]{:S(2)}) async-start(bf16[1,384,72]{2,0,1:T(2,128)(2,1)} %reshape.406), calls=%async_computation.2 | async-start | bytes 393216 | tf_op jit(solution)/shard_map/all_to_all | solution.py:231
  220.1 10.6 %all-to-all-done.2 = bf16[1,384,72]{2,0,1:T(2,128)(2,1)S(1)} async-done(((bf16[1,384,72]{2,0,1:T(2,128)(2,1)}), bf16[1,384,72]{2,0,1:T(2,128)(2,1)S(1)}, u32[]{:S(2)}, u32[]{:S(2)}) %all-to-all-start.2) | async-done | bytes 55328 | tf_op jit(solution)/shard_map/all_to_all | solution.py:231
  232.4 33.2 %shard_map.95 = bf16[2,4,4,4,144,128]{5,4,3,2,1,0:T(8,128)(2,1)} custom-call(bf16[144,128]{1,0:T(8,128)(2,1)} %reshape_reshape.22.x_ref), custom_call_target="tpu_custom_call" | custom-call | tf_op jit(solution)/shard_map/pallas_call | solution.py:151
  265.6 7.7 %reshape_reshape_reshape.7 = bf16[384,6144]{1,0:T(8,128)(2,1)} reshape(bf16[2,4,4,4,144,128]{5,4,3,2,1,0:T(8,128)(2,1)} %shard_map.95) | data formatting | bytes 9437184 | tf_op jit(solution)/shard_map/reshape;reshape;reshape | solution.py:183
  273.3 2.8 fusion.90
  279.0 27.0 %shard_map.96 = bf16[2,4,4,4,96,128]{5,4,3,2,1,0:T(8,128)(2,1)} custom-call(bf16[96,128]{1,0:T(8,128)(2,1)} %bitcast.207), custom_call_target="tpu_custom_call" | custom-call | tf_op jit(solution)/shard_map/pallas_call | solution.py:151
  306.0 2.1 slice.175
  310.2 8.4 %all-to-all-start.3 = ((bf16[1,384,24]{2,0,1:T(2,128)(2,1)}), bf16[1,384,24]{2,0,1:T(2,128)(2,1)S(1)}, u32[]{:S(2)}, u32[]{:S(2)}) async-start(bf16[1,384,24]{2,0,1:T(2,128)(2,1)} %reshape.407), calls=%async_computation.3 | async-start | bytes 393216 | tf_op jit(solution)/shard_map/all_to_all | solution.py:265
  318.7 28.8 %collective-permute-start.5 = (bf16[1,3,3072]{2,0,1:T(2,128)(2,1)S(1)}, bf16[1,3,3072]{2,0,1:T(2,128)(2,1)S(1)}, u32[]{:S(2)}, u32[]{:S(2)}) collective-permute-start(bf16[1,3,3072]{2,0,1:T(2,128)(2,1)S(1)} %get-tuple-element.8), channel_id=1, source_target_pairs={{128,0},{129,1},{130,2},{131,3},{132,4},{133,5},{134,6},{135,7},{1... | collective-permute-start | bytes 55304 | tf_op jit(solution)/shard_map/ppermute | solution.py:315
  349.3 11.7 %collective-permute-done.6 = bf16[1,3,3072]{2,0,1:T(2,128)(2,1)S(1)} collective-permute-done((bf16[1,3,3072]{2,0,1:T(2,128)(2,1)S(1)}, bf16[1,3,3072]{2,0,1:T(2,128)(2,1)S(1)}, u32[]{:S(2)}, u32[]{:S(2)}) %collective-permute-start.6) | collective-permute-done | bytes 18464 | tf_op jit(solution)/shard_map/ppermute | solution.py:316
  (144 shorter events, 27.2 us)
Async XLA Ops:
  0.0 9.0 %copy-start = (s32[2,128]{1,0:T(2,128)S(1)}, s32[2,128]{1,0:T(2,128)}, u32[]{:S(2)}) copy-start(s32[2,128]{1,0:T(2,128)} %param.15) | copy-start | bytes 3076
  0.0 7.9 %copy-start.6 = (s32[1,2,128]{2,1,0:T(2,128)S(1)}, s32[1,2,128]{2,1,0:T(2,128)}, u32[]{:S(2)}) copy-start(s32[1,2,128]{2,1,0:T(2,128)} %param.14) | copy-start | bytes 3076
  0.0 8.2 %copy-start.5 = (bf16[1,3072,24]{1,2,0:T(8,128)(2,1)S(1)}, bf16[1,3072,24]{1,2,0:T(8,128)(2,1)}, u32[]{:S(2)}) copy-start(bf16[1,3072,24]{1,2,0:T(8,128)(2,1)} %param.11) | copy-start | bytes 442372
  0.0 8.6 %copy-start.3 = (bf16[2,3,3072]{2,0,1:T(2,128)(2,1)S(1)}, bf16[2,3,3072]{2,0,1:T(2,128)(2,1)}, u32[]{:S(2)}) copy-start(bf16[2,3,3072]{2,0,1:T(2,128)(2,1)} %param.9) | copy-start | bytes 110596
  3.1 9.7 %collective-permute-start = (f32[3,3072]{1,0:T(4,128)S(1)}, f32[3,3072]{1,0:T(4,128)S(1)}, u32[]{:S(2)}, u32[]{:S(2)}) collective-permute-start(f32[3,3072]{1,0:T(4,128)S(1)} %bitcast.221), channel_id=1, source_target_pairs={{0,128},{128,0},{1,129},{129,1},{2,130},{130,2},{3,131},{131,3},{4... | collective-permute-start | bytes 110600 | tf_op jit(solution)/shard_map/ppermute | solution.py:270
  6.5 42.9 %collective-permute-start.1 = (bf16[3072,72]{0,1:T(8,128)(2,1)}, bf16[3072,72]{0,1:T(8,128)(2,1)S(1)}, u32[]{:S(2)}, u32[]{:S(2)}) collective-permute-start(bf16[3072,72]{0,1:T(8,128)(2,1)} %bitcast.197), channel_id=1, source_target_pairs={{0,128},{128,0},{1,129},{129,1},{2,130},{130,2},{3,131},{131,3},{4... | collective-permute-start | bytes 1327112 | tf_op jit(solution)/shard_map/ppermute | solution.py:270
  7.4 5.5 %collective-permute-start.3 = (bf16[1,3,6144]{2,1,0:T(4,128)(2,1)S(1)}, bf16[1,3,6144]{2,1,0:T(4,128)(2,1)S(1)}, u32[]{:S(2)}, u32[]{:S(2)}) collective-permute-start(bf16[1,3,6144]{2,1,0:T(4,128)(2,1)S(1)} %fusion.67), channel_id=1, source_target_pairs={{0,128},{128,0},{1,129},{129,1},{2,130},{130,2},{3,131},{131,3},{4... | collective-permute-start | bytes 110600 | tf_op jit(solution)/shard_map/ppermute | solution.py:270
  8.1 2.8 collective-permute-start.2
  8.2 53.9 %collective-permute-start.4 = (bf16[3072,24]{0,1:T(8,128)(2,1)S(1)}, bf16[3072,24]{0,1:T(8,128)(2,1)S(1)}, u32[]{:S(2)}, u32[]{:S(2)}) collective-permute-start(bf16[3072,24]{0,1:T(8,128)(2,1)S(1)} %bitcast.206), channel_id=1, source_target_pairs={{0,128},{128,0},{1,129},{129,1},{2,130},{130,2},{3,131},{131,3},{4... | collective-permute-start | bytes 442376 | tf_op jit(solution)/shard_map/ppermute | solution.py:270
  47.2 2.2 copy-start.4
  51.7 22.2 %all-to-all-start = ((bf16[1,384,72]{2,0,1:T(2,128)(2,1)}), bf16[1,384,72]{2,0,1:T(2,128)(2,1)S(1)}, u32[]{:S(2)}, u32[]{:S(2)}) async-start(bf16[1,384,72]{2,0,1:T(2,128)(2,1)} %reshape.404), calls=%async_computation | async-start | bytes 393216 | tf_op jit(solution)/shard_map/all_to_all | solution.py:231
  120.1 3.0 copy-start.2
  212.4 18.3 %all-to-all-start.2 = ((bf16[1,384,72]{2,0,1:T(2,128)(2,1)}), bf16[1,384,72]{2,0,1:T(2,128)(2,1)S(1)}, u32[]{:S(2)}, u32[]{:S(2)}) async-start(bf16[1,384,72]{2,0,1:T(2,128)(2,1)} %reshape.406), calls=%async_computation.2 | async-start | bytes 393216 | tf_op jit(solution)/shard_map/all_to_all | solution.py:231
  273.3 3.0 copy-start.1
  310.2 37.3 %all-to-all-start.3 = ((bf16[1,384,24]{2,0,1:T(2,128)(2,1)}), bf16[1,384,24]{2,0,1:T(2,128)(2,1)S(1)}, u32[]{:S(2)}, u32[]{:S(2)}) async-start(bf16[1,384,24]{2,0,1:T(2,128)(2,1)} %reshape.407), calls=%async_computation.3 | async-start | bytes 393216 | tf_op jit(solution)/shard_map/all_to_all | solution.py:265
  318.7 30.6 %collective-permute-start.5 = (bf16[1,3,3072]{2,0,1:T(2,128)(2,1)S(1)}, bf16[1,3,3072]{2,0,1:T(2,128)(2,1)S(1)}, u32[]{:S(2)}, u32[]{:S(2)}) collective-permute-start(bf16[1,3,3072]{2,0,1:T(2,128)(2,1)S(1)} %get-tuple-element.8), channel_id=1, source_target_pairs={{128,0},{129,1},{130,2},{131,3},{132,4},{133,5},{134,6},{135,7},{1... | collective-permute-start | bytes 55304 | tf_op jit(solution)/shard_map/ppermute | solution.py:315
  348.0 13.1 %collective-permute-start.6 = (bf16[1,3,3072]{2,0,1:T(2,128)(2,1)S(1)}, bf16[1,3,3072]{2,0,1:T(2,128)(2,1)S(1)}, u32[]{:S(2)}, u32[]{:S(2)}) collective-permute-start(bf16[1,3,3072]{2,0,1:T(2,128)(2,1)S(1)} %add_convert_fusion), channel_id=1, source_target_pairs={{0,128},{1,129},{2,130},{3,131},{4,132},{5,133},{6,134},{7,135},{8... | collective-permute-start | bytes 55304 | tf_op jit(solution)/shard_map/ppermute | solution.py:316

commit v14 on v13

--- a/solution.py
+++ b/solution.py
@@ -236,9 +236,10 @@
     use_fresh = (fresh_own == 1)[:, None, None]
     keys = jnp.where(use_fresh, new_keys, old_keys)
     values = jnp.where(use_fresh, new_values, old_values)
-    kv_all = gather_rows(jnp.concatenate([keys, values], axis=2), 1, active)
-    key_all = kv_all[:, :width]
-    value_all = kv_all[:, width:]
+    kv_all = gather_tokens(jnp.concatenate([keys, values], axis=2), 3)
+    chunks = width // 128
+    key_all = kv_all[:, :chunks]
+    value_all = kv_all[:, chunks:]
     nz = n // PLANE
     live_zxy = live[0].reshape(nz, NX, NY)
     live_by_slot = jnp.concatenate([
@@ -250,14 +251,15 @@
     head_of_col = jnp.arange(width) // 64
     in_head = head_of_col[None, :] == jnp.arange(num_heads)[:, None]
     q_diag = jnp.where(in_head[None], queries[:, None, :], jnp.zeros((), queries.dtype))
-    scores = jnp.einsum("qhc,kc->qhk", q_diag, key_all, preferred_element_type=jnp.float32) * 0.125
+    q_diag = q_diag.reshape(num_rows, num_heads, chunks, 128)
+    scores = jnp.einsum("qhal,kal->qhk", q_diag, key_all, preferred_element_type=jnp.float32) * 0.125
     scores = jnp.where(usable, scores, -1e30)
     top = jnp.max(scores, axis=-1, keepdims=True)
     weights = jnp.where(usable, jnp.exp(scores - top), 0.0)
     total = jnp.sum(weights, axis=-1)
     mixed_all = jnp.einsum(
-        "qhk,kc->qhc", weights, value_all.astype(jnp.float32), precision=lax.Precision.HIGHEST
-    )
+        "qhk,kal->qhal", weights, value_all.astype(jnp.float32), precision=lax.Precision.HIGHEST
+    ).reshape(num_rows, num_heads, width)
     own_head = jnp.sum(jnp.where(in_head[None], mixed_all, 0.0), axis=1)
     total_col = jnp.broadcast_to(total[:, :, None], (num_rows, num_heads, 64)).reshape(num_rows, width)
     attn = (own_head / total_col).astype(jnp.bfloat16)[None]

time: 363 us -> 357 us (0.983)
  local copies, waits for them, and re-layouts: 37.5 us -> 30.9 us
    another operation x4 -> x0, local copies, waits for them, and re-layouts: 16.8 us -> none  [the longest x2 15.4 us: gather_rows(): return out.reshape(n * rows, width)]
    slice x0 -> x2, local copies, waits for them, and re-layouts: none -> 9.37 us  [attend(): key_all = kv_all[:, :chunks]]
    sub x0 -> x2, matrix products: none -> 6.01 us  [attend(): weights = jnp.where(usable, jnp.exp(scores - top), 0.0)]
    dot_general x4 -> x2, matrix products: 8.88 us -> 4.16 us  [attend(): jnp.einsum('qhk,kal->qhal', weights, value_all.astype(jnp.float32), preci...]
where the time goes in v14:
time: 357 us
  Pallas kernels  188 us (53%)
  starting transfers between devices  59.8 us (17%)
  waiting for transfers between devices  34.1 us (10%)
  local copies, waits for them, and re-layouts  30.9 us (9%)
  blocking collectives  20.4 us (6%)
  matrix products  15.7 us (4%)
  other arithmetic  4.15 us (1%)
  between operations  3.92 us (1%)
    pallas_call x6, Pallas kernels, gather_blk(): pl.pallas_call(functools.partial(gather_kernel, n), out_shape=jax.ShapeDt...  188 us
    ppermute x1, starting transfers between devices, per_device(): first_req1 = lax.ppermute(outs[0], 'section', [(1, 0)])  29.1 us
    all_to_all x2, waiting for transfers between devices, attend(): lax.all_to_all(to_blk_order(columns, n), 'blk', split_axis=1, concat_axis...  22.4 us
    all_to_all x1, blocking collectives, attend(): lax.all_to_all(to_blk_order(out_part, n), 'blk', split_axis=1, concat_axi...  20.4 us
    all_to_all x2, starting transfers between devices, attend(): lax.all_to_all(to_blk_order(columns, n), 'blk', split_axis=1, concat_axis...  17.1 us
    ppermute x1, waiting for transfers between devices, per_device(): second_req0 = lax.ppermute(outs[1], 'section', [(0, 1)])  11.7 us
    slice x2, local copies, waits for them, and re-layouts, attend(): key_all = kv_all[:, :chunks]  9.37 us
    slice x4, local copies, waits for them, and re-layouts, gather_tokens(): return out.reshape(n * rows, per_token, 128)[:, :chunks]  8.35 us
  transfers between devices with their start and end apart: 10, of which 3 were waited for; matrix products, arithmetic and copies ran while one was open for 3% of the time, Pallas kernels for 9%

profile of v14, /device:TPU:1, one launch (start us, length us, event | category | flops | bytes accessed | tf_op | source)
XLA Modules:
  0.0 356.6 jit_solution(2297486114366906430)
XLA Ops:
  0.7 2.4 fusion.14
  3.1 3.3 collective-permute-start
  13.8 33.3 %shard_map.91 = bf16[2,4,4,4,96,128]{5,4,3,2,1,0:T(8,128)(2,1)} custom-call(bf16[96,128]{1,0:T(8,128)(2,1)} %bitcast.238), custom_call_target="tpu_custom_call" | custom-call | tf_op jit(solution)/shard_map/pallas_call | solution.py:151
  47.2 2.1 slice.149
  51.6 10.4 %all-to-all-start = ((bf16[1,384,72]{2,0,1:T(2,128)(2,1)}), bf16[1,384,72]{2,0,1:T(2,128)(2,1)S(1)}, u32[]{:S(2)}, u32[]{:S(2)}) async-start(bf16[1,384,72]{2,0,1:T(2,128)(2,1)} %reshape.445), calls=%async_computation | async-start | bytes 393216 | tf_op jit(solution)/shard_map/all_to_all | solution.py:231
  62.1 11.7 %all-to-all-done = bf16[1,384,72]{2,0,1:T(2,128)(2,1)S(1)} async-done(((bf16[1,384,72]{2,0,1:T(2,128)(2,1)}), bf16[1,384,72]{2,0,1:T(2,128)(2,1)S(1)}, u32[]{:S(2)}, u32[]{:S(2)}) %all-to-all-start) | async-done | bytes 55328 | tf_op jit(solution)/shard_map/all_to_all | solution.py:231
  75.5 36.8 %shard_map.92 = bf16[2,4,4,4,144,128]{5,4,3,2,1,0:T(8,128)(2,1)} custom-call(bf16[144,128]{1,0:T(8,128)(2,1)} %reshape.407.x_ref), custom_call_target="tpu_custom_call" | custom-call | tf_op jit(solution)/shard_map/pallas_call | solution.py:151
  112.3 4.7 %fusion.82 = (bf16[384,24,128]{2,1,0:T(8,128)(2,1)}, bf16[384,24,128]{2,1,0:T(8,128)(2,1)S(1)}) fusion(bf16[384,48,128]{2,1,0:T(8,128)(2,1)} %bitcast.217), kind=kLoop, calls=%fused_computation.144 | loop fusion | bytes 9437184 | tf_op jit(solution)/shard_map/slice | solution.py:241
  117.0 3.3 fusion.89
  120.4 2.5 select_reduce_fusion.1
  123.6 26.8 %shard_map.93 = bf16[2,4,4,4,96,128]{5,4,3,2,1,0:T(8,128)(2,1)} custom-call(bf16[96,128]{1,0:T(8,128)(2,1)} %bitcast.239), custom_call_target="tpu_custom_call" | custom-call | tf_op jit(solution)/shard_map/pallas_call | solution.py:151
  150.4 2.1 slice.159
  153.9 20.4 %all_to_all.54 = bf16[1,384,24]{2,0,1:T(2,128)(2,1)S(1)} all-to-all(bf16[1,384,24]{2,0,1:T(2,128)(2,1)S(1)} %reshape.446), channel_id=1, replica_groups=mesh['section'=2,'blk'=128] {'blk'}, dimensions={1} | all-to-all | bytes 36864 | tf_op jit(solution)/shard_map/all_to_all | solution.py:267
  176.0 29.9 %shard_map.94 = bf16[2,4,4,4,96,128]{5,4,3,2,1,0:T(8,128)(2,1)} custom-call(bf16[96,128]{1,0:T(8,128)(2,1)} %bitcast.240), custom_call_target="tpu_custom_call" | custom-call | tf_op jit(solution)/shard_map/pallas_call | solution.py:151
  205.9 2.1 slice.165
  210.2 6.7 %all-to-all-start.2 = ((bf16[1,384,72]{2,0,1:T(2,128)(2,1)}), bf16[1,384,72]{2,0,1:T(2,128)(2,1)S(1)}, u32[]{:S(2)}, u32[]{:S(2)}) async-start(bf16[1,384,72]{2,0,1:T(2,128)(2,1)} %reshape.447), calls=%async_computation.2 | async-start | bytes 393216 | tf_op jit(solution)/shard_map/all_to_all | solution.py:231
  218.1 10.7 %all-to-all-done.2 = bf16[1,384,72]{2,0,1:T(2,128)(2,1)S(1)} async-done(((bf16[1,384,72]{2,0,1:T(2,128)(2,1)}), bf16[1,384,72]{2,0,1:T(2,128)(2,1)S(1)}, u32[]{:S(2)}, u32[]{:S(2)}) %all-to-all-start.2) | async-done | bytes 55328 | tf_op jit(solution)/shard_map/all_to_all | solution.py:231
  230.5 33.2 %shard_map.95 = bf16[2,4,4,4,144,128]{5,4,3,2,1,0:T(8,128)(2,1)} custom-call(bf16[144,128]{1,0:T(8,128)(2,1)} %reshape.420.x_ref), custom_call_target="tpu_custom_call" | custom-call | tf_op jit(solution)/shard_map/pallas_call | solution.py:151
  263.7 4.7 %fusion.81 = (bf16[384,24,128]{2,1,0:T(8,128)(2,1)}, bf16[384,24,128]{2,1,0:T(8,128)(2,1)S(1)}) fusion(bf16[384,48,128]{2,1,0:T(8,128)(2,1)} %bitcast.218), kind=kLoop, calls=%fused_computation.143 | loop fusion | bytes 9437184 | tf_op jit(solution)/shard_map/slice | solution.py:241
  268.4 2.7 fusion.90
  273.5 27.6 %shard_map.96 = bf16[2,4,4,4,96,128]{5,4,3,2,1,0:T(8,128)(2,1)} custom-call(bf16[96,128]{1,0:T(8,128)(2,1)} %bitcast.237), custom_call_target="tpu_custom_call" | custom-call | tf_op jit(solution)/shard_map/pallas_call | solution.py:151
  305.3 7.8 %all-to-all-start.3 = ((bf16[1,384,24]{2,0,1:T(2,128)(2,1)}), bf16[1,384,24]{2,0,1:T(2,128)(2,1)S(1)}, u32[]{:S(2)}, u32[]{:S(2)}) async-start(bf16[1,384,24]{2,0,1:T(2,128)(2,1)} %reshape.448), calls=%async_computation.3 | async-start | bytes 393216 | tf_op jit(solution)/shard_map/all_to_all | solution.py:267
  313.1 29.1 %collective-permute-start.5 = (bf16[1,3,3072]{2,0,1:T(2,128)(2,1)S(1)}, bf16[1,3,3072]{2,0,1:T(2,128)(2,1)S(1)}, u32[]{:S(2)}, u32[]{:S(2)}) collective-permute-start(bf16[1,3,3072]{2,0,1:T(2,128)(2,1)S(1)} %get-tuple-element.8), channel_id=1, source_target_pairs={{128,0},{129,1},{130,2},{131,3},{132,4},{133,5},{134,6},{135,7},{1... | collective-permute-start | bytes 55304 | tf_op jit(solution)/shard_map/ppermute | solution.py:317
  344.1 11.7 %collective-permute-done.6 = bf16[1,3,3072]{2,0,1:T(2,128)(2,1)S(1)} collective-permute-done((bf16[1,3,3072]{2,0,1:T(2,128)(2,1)S(1)}, bf16[1,3,3072]{2,0,1:T(2,128)(2,1)S(1)}, u32[]{:S(2)}, u32[]{:S(2)}) %collective-permute-start.6) | collective-permute-done | bytes 18464 | tf_op jit(solution)/shard_map/ppermute | solution.py:318
  (140 shorter events, 26.6 us)
Async XLA Ops:
  0.0 9.1 %copy-start = (s32[2,128]{1,0:T(2,128)S(1)}, s32[2,128]{1,0:T(2,128)}, u32[]{:S(2)}) copy-start(s32[2,128]{1,0:T(2,128)} %param.15) | copy-start | bytes 3076
  0.0 7.9 %copy-start.4 = (s32[1,2,128]{2,1,0:T(2,128)S(1)}, s32[1,2,128]{2,1,0:T(2,128)}, u32[]{:S(2)}) copy-start(s32[1,2,128]{2,1,0:T(2,128)} %param.14) | copy-start | bytes 3076
  0.0 8.2 %copy-start.3 = (bf16[1,3072,24]{1,2,0:T(8,128)(2,1)S(1)}, bf16[1,3072,24]{1,2,0:T(8,128)(2,1)}, u32[]{:S(2)}) copy-start(bf16[1,3072,24]{1,2,0:T(8,128)(2,1)} %param.11) | copy-start | bytes 442372
  0.0 8.7 %copy-start.1 = (bf16[2,3,3072]{2,0,1:T(2,128)(2,1)S(1)}, bf16[2,3,3072]{2,0,1:T(2,128)(2,1)}, u32[]{:S(2)}) copy-start(bf16[2,3,3072]{2,0,1:T(2,128)(2,1)} %param.9) | copy-start | bytes 110596
  3.1 9.7 %collective-permute-start = (f32[3,3072]{1,0:T(4,128)S(1)}, f32[3,3072]{1,0:T(4,128)S(1)}, u32[]{:S(2)}, u32[]{:S(2)}) collective-permute-start(f32[3,3072]{1,0:T(4,128)S(1)} %bitcast.249), channel_id=1, source_target_pairs={{0,128},{128,0},{1,129},{129,1},{2,130},{130,2},{3,131},{131,3},{4... | collective-permute-start | bytes 110600 | tf_op jit(solution)/shard_map/ppermute | solution.py:272
  6.5 42.8 %collective-permute-start.1 = (bf16[3072,72]{0,1:T(8,128)(2,1)}, bf16[3072,72]{0,1:T(8,128)(2,1)S(1)}, u32[]{:S(2)}, u32[]{:S(2)}) collective-permute-start(bf16[3072,72]{0,1:T(8,128)(2,1)} %bitcast.227), channel_id=1, source_target_pairs={{0,128},{128,0},{1,129},{129,1},{2,130},{130,2},{3,131},{131,3},{4... | collective-permute-start | bytes 1327112 | tf_op jit(solution)/shard_map/ppermute | solution.py:272
  7.4 5.4 %collective-permute-start.3 = (bf16[1,3,6144]{2,1,0:T(4,128)(2,1)S(1)}, bf16[1,3,6144]{2,1,0:T(4,128)(2,1)S(1)}, u32[]{:S(2)}, u32[]{:S(2)}) collective-permute-start(bf16[1,3,6144]{2,1,0:T(4,128)(2,1)S(1)} %fusion.71), channel_id=1, source_target_pairs={{0,128},{128,0},{1,129},{129,1},{2,130},{130,2},{3,131},{131,3},{4... | collective-permute-start | bytes 110600 | tf_op jit(solution)/shard_map/ppermute | solution.py:272
  8.1 2.8 collective-permute-start.2
  8.2 53.8 %collective-permute-start.4 = (bf16[3072,24]{0,1:T(8,128)(2,1)S(1)}, bf16[3072,24]{0,1:T(8,128)(2,1)S(1)}, u32[]{:S(2)}, u32[]{:S(2)}) collective-permute-start(bf16[3072,24]{0,1:T(8,128)(2,1)S(1)} %bitcast.236), channel_id=1, source_target_pairs={{0,128},{128,0},{1,129},{129,1},{2,130},{130,2},{3,131},{131,3},{4... | collective-permute-start | bytes 442376 | tf_op jit(solution)/shard_map/ppermute | solution.py:272
  47.1 2.2 copy-start.2
  51.6 22.2 %all-to-all-start = ((bf16[1,384,72]{2,0,1:T(2,128)(2,1)}), bf16[1,384,72]{2,0,1:T(2,128)(2,1)S(1)}, u32[]{:S(2)}, u32[]{:S(2)}) async-start(bf16[1,384,72]{2,0,1:T(2,128)(2,1)} %reshape.445), calls=%async_computation | async-start | bytes 393216 | tf_op jit(solution)/shard_map/all_to_all | solution.py:231
  210.2 18.6 %all-to-all-start.2 = ((bf16[1,384,72]{2,0,1:T(2,128)(2,1)}), bf16[1,384,72]{2,0,1:T(2,128)(2,1)S(1)}, u32[]{:S(2)}, u32[]{:S(2)}) async-start(bf16[1,384,72]{2,0,1:T(2,128)(2,1)} %reshape.447), calls=%async_computation.2 | async-start | bytes 393216 | tf_op jit(solution)/shard_map/all_to_all | solution.py:231
  305.3 36.9 %all-to-all-start.3 = ((bf16[1,384,24]{2,0,1:T(2,128)(2,1)}), bf16[1,384,24]{2,0,1:T(2,128)(2,1)S(1)}, u32[]{:S(2)}, u32[]{:S(2)}) async-start(bf16[1,384,24]{2,0,1:T(2,128)(2,1)} %reshape.448), calls=%async_computation.3 | async-start | bytes 393216 | tf_op jit(solution)/shard_map/all_to_all | solution.py:267
  313.1 30.9 %collective-permute-start.5 = (bf16[1,3,3072]{2,0,1:T(2,128)(2,1)S(1)}, bf16[1,3,3072]{2,0,1:T(2,128)(2,1)S(1)}, u32[]{:S(2)}, u32[]{:S(2)}) collective-permute-start(bf16[1,3,3072]{2,0,1:T(2,128)(2,1)S(1)} %get-tuple-element.8), channel_id=1, source_target_pairs={{128,0},{129,1},{130,2},{131,3},{132,4},{133,5},{134,6},{135,7},{1... | collective-permute-start | bytes 55304 | tf_op jit(solution)/shard_map/ppermute | solution.py:317
  342.7 13.1 %collective-permute-start.6 = (bf16[1,3,3072]{2,0,1:T(2,128)(2,1)S(1)}, bf16[1,3,3072]{2,0,1:T(2,128)(2,1)S(1)}, u32[]{:S(2)}, u32[]{:S(2)}) collective-permute-start(bf16[1,3,3072]{2,0,1:T(2,128)(2,1)S(1)} %add_convert_fusion), channel_id=1, source_target_pairs={{0,128},{1,129},{2,130},{3,131},{4,132},{5,133},{6,134},{7,135},{8... | collective-permute-start | bytes 55304 | tf_op jit(solution)/shard_map/ppermute | solution.py:318

commit v15 on v14

--- a/solution.py
+++ b/solution.py
@@ -276,8 +276,7 @@
     sec = lax.axis_index("section")
     block_idx = lax.axis_index("blk")
     steps_all = modulation.shape[1]
-    pick_row = (jnp.arange(steps_all) == timestep[0]).astype(jnp.float32)
-    modulate_own = jnp.einsum("t,tcd->cd", pick_row, modulation[0], precision=lax.Precision.HIGHEST)
+    modulate_own = lax.dynamic_index_in_dim(modulation[0], jnp.clip(timestep[0], 0, steps_all - 1), 0, keepdims=False)
     num_blocks = fresh.shape[2]
     own_column = (jnp.arange(num_blocks) == block_idx).astype(jnp.int32)
     fresh_own = jnp.sum(fresh[0] * own_column[None, :], axis=1)

time: 357 us -> 363 us (1.017)
  transfers between devices with their start and end apart: 10 -> 10, of which waited for: 3 -> 3; matrix products, arithmetic and copies ran while one was open for 3% -> 4% of each run, Pallas kernels for 9% -> 9%
where the time goes in v15:
time: 363 us; the launch traced here: 362 us
  Pallas kernels  187 us (52%)
  starting transfers between devices  60.1 us (17%)
  waiting for transfers between devices  34 us (9%)
  local copies, waits for them, and re-layouts  33.8 us (9%)
  blocking collectives  20.4 us (6%)
  matrix products  15.1 us (4%)
  other arithmetic  7.13 us (2%)
  between operations  4.14 us (1%)
    pallas_call x6, Pallas kernels, gather_blk(): pl.pallas_call(functools.partial(gather_kernel, n), out_shape=jax.ShapeDt...  187 us
    ppermute x1, starting transfers between devices, per_device(): first_req1 = lax.ppermute(outs[0], 'section', [(1, 0)])  28.8 us
    all_to_all x2, waiting for transfers between devices, attend(): lax.all_to_all(to_blk_order(columns, n), 'blk', split_axis=1, concat_axis...  22.3 us
    all_to_all x1, blocking collectives, attend(): lax.all_to_all(to_blk_order(out_part, n), 'blk', split_axis=1, concat_axi...  20.4 us
    all_to_all x2, starting transfers between devices, attend(): lax.all_to_all(to_blk_order(columns, n), 'blk', split_axis=1, concat_axis...  17.1 us
    ppermute x1, waiting for transfers between devices, per_device(): second_req0 = lax.ppermute(outs[1], 'section', [(0, 1)])  11.7 us
    slice x2, local copies, waits for them, and re-layouts, attend(): key_all = kv_all[:, :chunks]  10.8 us
    all_to_all x1, starting transfers between devices, attend(): lax.all_to_all(to_blk_order(out_part, n), 'blk', split_axis=1, concat_axi...  8.37 us
  transfers between devices with their start and end apart: 10, of which 3 were waited for; matrix products, arithmetic and copies ran while one was open for 4% of the time, Pallas kernels for 9%

profile of v15, /device:TPU:1, one launch (start us, length us, event | category | flops | bytes accessed | tf_op | source)
XLA Modules:
  0.0 361.7 jit_solution(16671143083377013062)
XLA Ops:
  1.5 3.3 collective-permute-start
  16.0 33.3 %shard_map.91 = bf16[2,4,4,4,96,128]{5,4,3,2,1,0:T(8,128)(2,1)} custom-call(bf16[96,128]{1,0:T(8,128)(2,1)} %bitcast.231), custom_call_target="tpu_custom_call" | custom-call | tf_op jit(solution)/shard_map/pallas_call | solution.py:151
  49.3 2.1 slice.149
  53.7 10.4 %all-to-all-start = ((bf16[1,384,72]{2,0,1:T(2,128)(2,1)}), bf16[1,384,72]{2,0,1:T(2,128)(2,1)S(1)}, u32[]{:S(2)}, u32[]{:S(2)}) async-start(bf16[1,384,72]{2,0,1:T(2,128)(2,1)} %reshape.449), calls=%async_computation | async-start | bytes 393216 | tf_op jit(solution)/shard_map/all_to_all | solution.py:231
  64.2 11.7 %all-to-all-done = bf16[1,384,72]{2,0,1:T(2,128)(2,1)S(1)} async-done(((bf16[1,384,72]{2,0,1:T(2,128)(2,1)}), bf16[1,384,72]{2,0,1:T(2,128)(2,1)S(1)}, u32[]{:S(2)}, u32[]{:S(2)}) %all-to-all-start) | async-done | bytes 55328 | tf_op jit(solution)/shard_map/all_to_all | solution.py:231
  77.6 36.8 %shard_map.92 = bf16[2,4,4,4,144,128]{5,4,3,2,1,0:T(8,128)(2,1)} custom-call(bf16[144,128]{1,0:T(8,128)(2,1)} %reshape.413.x_ref), custom_call_target="tpu_custom_call" | custom-call | tf_op jit(solution)/shard_map/pallas_call | solution.py:151
  114.4 5.4 %fusion.75 = (bf16[384,24,128]{2,1,0:T(8,128)(2,1)}, bf16[384,24,128]{2,1,0:T(8,128)(2,1)}) fusion(bf16[384,48,128]{2,1,0:T(8,128)(2,1)} %bitcast.210), kind=kLoop, calls=%fused_computation.138 | loop fusion | bytes 9437184 | tf_op jit(solution)/shard_map/slice | solution.py:241
  119.8 2.7 fusion.82
  122.7 3.3 select_reduce_fusion.1
  126.6 26.8 %shard_map.93 = bf16[2,4,4,4,96,128]{5,4,3,2,1,0:T(8,128)(2,1)} custom-call(bf16[96,128]{1,0:T(8,128)(2,1)} %bitcast.232), custom_call_target="tpu_custom_call" | custom-call | tf_op jit(solution)/shard_map/pallas_call | solution.py:151
  153.4 2.1 slice.159
  156.9 20.4 %all_to_all.54 = bf16[1,384,24]{2,0,1:T(2,128)(2,1)S(1)} all-to-all(bf16[1,384,24]{2,0,1:T(2,128)(2,1)S(1)} %reshape.450), channel_id=1, replica_groups=mesh['section'=2,'blk'=128] {'blk'}, dimensions={1} | all-to-all | bytes 36864 | tf_op jit(solution)/shard_map/all_to_all | solution.py:267
  179.0 29.9 %shard_map.94 = bf16[2,4,4,4,96,128]{5,4,3,2,1,0:T(8,128)(2,1)} custom-call(bf16[96,128]{1,0:T(8,128)(2,1)} %bitcast.233), custom_call_target="tpu_custom_call" | custom-call | tf_op jit(solution)/shard_map/pallas_call | solution.py:151
  208.9 2.1 slice.165
  213.2 6.7 %all-to-all-start.2 = ((bf16[1,384,72]{2,0,1:T(2,128)(2,1)}), bf16[1,384,72]{2,0,1:T(2,128)(2,1)S(1)}, u32[]{:S(2)}, u32[]{:S(2)}) async-start(bf16[1,384,72]{2,0,1:T(2,128)(2,1)} %reshape.451), calls=%async_computation.2 | async-start | bytes 393216 | tf_op jit(solution)/shard_map/all_to_all | solution.py:231
  221.2 10.6 %all-to-all-done.2 = bf16[1,384,72]{2,0,1:T(2,128)(2,1)S(1)} async-done(((bf16[1,384,72]{2,0,1:T(2,128)(2,1)}), bf16[1,384,72]{2,0,1:T(2,128)(2,1)S(1)}, u32[]{:S(2)}, u32[]{:S(2)}) %all-to-all-start.2) | async-done | bytes 55328 | tf_op jit(solution)/shard_map/all_to_all | solution.py:231
  233.5 33.2 %shard_map.95 = bf16[2,4,4,4,144,128]{5,4,3,2,1,0:T(8,128)(2,1)} custom-call(bf16[144,128]{1,0:T(8,128)(2,1)} %reshape.426.x_ref), custom_call_target="tpu_custom_call" | custom-call | tf_op jit(solution)/shard_map/pallas_call | solution.py:151
  266.7 5.4 %fusion.74 = (bf16[384,24,128]{2,1,0:T(8,128)(2,1)}, bf16[384,24,128]{2,1,0:T(8,128)(2,1)}) fusion(bf16[384,48,128]{2,1,0:T(8,128)(2,1)} %bitcast.211), kind=kLoop, calls=%fused_computation.137 | loop fusion | bytes 9437184 | tf_op jit(solution)/shard_map/slice | solution.py:241
  272.1 2.7 fusion.83
  275.0 3.3 select_reduce_fusion
  278.9 27.0 %shard_map.96 = bf16[2,4,4,4,96,128]{5,4,3,2,1,0:T(8,128)(2,1)} custom-call(bf16[96,128]{1,0:T(8,128)(2,1)} %bitcast.230), custom_call_target="tpu_custom_call" | custom-call | tf_op jit(solution)/shard_map/pallas_call | solution.py:151
  310.1 8.4 %all-to-all-start.3 = ((bf16[1,384,24]{2,0,1:T(2,128)(2,1)}), bf16[1,384,24]{2,0,1:T(2,128)(2,1)S(1)}, u32[]{:S(2)}, u32[]{:S(2)}) async-start(bf16[1,384,24]{2,0,1:T(2,128)(2,1)} %reshape.452), calls=%async_computation.3 | async-start | bytes 393216 | tf_op jit(solution)/shard_map/all_to_all | solution.py:267
  318.5 28.8 %collective-permute-start.5 = (bf16[1,3,3072]{2,0,1:T(2,128)(2,1)S(1)}, bf16[1,3,3072]{2,0,1:T(2,128)(2,1)S(1)}, u32[]{:S(2)}, u32[]{:S(2)}) collective-permute-start(bf16[1,3,3072]{2,0,1:T(2,128)(2,1)S(1)} %get-tuple-element.8), channel_id=1, source_target_pairs={{128,0},{129,1},{130,2},{131,3},{132,4},{133,5},{134,6},{135,7},{1... | collective-permute-start | bytes 55304 | tf_op jit(solution)/shard_map/ppermute | solution.py:316
  349.2 11.7 %collective-permute-done.6 = bf16[1,3,3072]{2,0,1:T(2,128)(2,1)S(1)} collective-permute-done((bf16[1,3,3072]{2,0,1:T(2,128)(2,1)S(1)}, bf16[1,3,3072]{2,0,1:T(2,128)(2,1)S(1)}, u32[]{:S(2)}, u32[]{:S(2)}) %collective-permute-start.6) | collective-permute-done | bytes 18464 | tf_op jit(solution)/shard_map/ppermute | solution.py:317
  (138 shorter events, 29.4 us)
Async XLA Ops:
  0.0 1.5 copy-start
  1.5 12.6 %collective-permute-start = (f32[3,3072]{1,0:T(4,128)S(1)}, f32[3,3072]{1,0:T(4,128)S(1)}, u32[]{:S(2)}, u32[]{:S(2)}) collective-permute-start(f32[3,3072]{1,0:T(4,128)S(1)} %bitcast.242), channel_id=1, source_target_pairs={{0,128},{128,0},{1,129},{129,1},{2,130},{130,2},{3,131},{131,3},{4... | collective-permute-start | bytes 110600 | tf_op jit(solution)/shard_map/ppermute | solution.py:272
  4.9 46.5 %collective-permute-start.1 = (bf16[3072,72]{0,1:T(8,128)(2,1)}, bf16[3072,72]{0,1:T(8,128)(2,1)S(1)}, u32[]{:S(2)}, u32[]{:S(2)}) collective-permute-start(bf16[3072,72]{0,1:T(8,128)(2,1)} %bitcast.220), channel_id=1, source_target_pairs={{0,128},{128,0},{1,129},{129,1},{2,130},{130,2},{3,131},{131,3},{4... | collective-permute-start | bytes 1327112 | tf_op jit(solution)/shard_map/ppermute | solution.py:272
  5.8 8.4 %collective-permute-start.3 = (bf16[1,3,6144]{2,1,0:T(4,128)(2,1)S(1)}, bf16[1,3,6144]{2,1,0:T(4,128)(2,1)S(1)}, u32[]{:S(2)}, u32[]{:S(2)}) collective-permute-start(bf16[1,3,6144]{2,1,0:T(4,128)(2,1)S(1)} %fusion.68), channel_id=1, source_target_pairs={{0,128},{128,0},{1,129},{129,1},{2,130},{130,2},{3,131},{131,3},{4... | collective-permute-start | bytes 110600 | tf_op jit(solution)/shard_map/ppermute | solution.py:272
  7.1 5.0 %collective-permute-start.2 = (s32[2]{0:T(128)S(1)}, s32[2]{0:T(128)S(1)}, u32[]{:S(2)}, u32[]{:S(2)}) collective-permute-start(s32[2]{0:T(128)S(1)} %fusion.71), channel_id=1, source_target_pairs={{0,128},{128,0},{1,129},{129,1},{2,130},{130,2},{3,131},{131,3},{4... | collective-permute-start | bytes 32 | tf_op jit(solution)/shard_map/ppermute | solution.py:272
  7.3 56.9 %collective-permute-start.4 = (bf16[3072,24]{0,1:T(8,128)(2,1)}, bf16[3072,24]{0,1:T(8,128)(2,1)S(1)}, u32[]{:S(2)}, u32[]{:S(2)}) collective-permute-start(bf16[3072,24]{0,1:T(8,128)(2,1)} %bitcast.229), channel_id=1, source_target_pairs={{0,128},{128,0},{1,129},{129,1},{2,130},{130,2},{3,131},{131,3},{4... | collective-permute-start | bytes 442376 | tf_op jit(solution)/shard_map/ppermute | solution.py:272
  49.3 2.2 copy-start.2
  51.5 12.7 %copy-start.3 = (bf16[1,3072,24]{1,2,0:T(8,128)(2,1)S(1)}, bf16[1,3072,24]{1,2,0:T(8,128)(2,1)}, u32[]{:S(2)}) copy-start(bf16[1,3072,24]{1,2,0:T(8,128)(2,1)} %param.11) | copy-start | bytes 442372
  53.7 22.2 %all-to-all-start = ((bf16[1,384,72]{2,0,1:T(2,128)(2,1)}), bf16[1,384,72]{2,0,1:T(2,128)(2,1)S(1)}, u32[]{:S(2)}, u32[]{:S(2)}) async-start(bf16[1,384,72]{2,0,1:T(2,128)(2,1)} %reshape.449), calls=%async_computation | async-start | bytes 393216 | tf_op jit(solution)/shard_map/all_to_all | solution.py:231
  155.5 22.2 %copy-start.1 = (bf16[2,3,3072]{2,0,1:T(2,128)(2,1)S(1)}, bf16[2,3,3072]{2,0,1:T(2,128)(2,1)}, u32[]{:S(2)}) copy-start(bf16[2,3,3072]{2,0,1:T(2,128)(2,1)} %param.9) | copy-start | bytes 110596
  213.2 18.6 %all-to-all-start.2 = ((bf16[1,384,72]{2,0,1:T(2,128)(2,1)}), bf16[1,384,72]{2,0,1:T(2,128)(2,1)S(1)}, u32[]{:S(2)}, u32[]{:S(2)}) async-start(bf16[1,384,72]{2,0,1:T(2,128)(2,1)} %reshape.451), calls=%async_computation.2 | async-start | bytes 393216 | tf_op jit(solution)/shard_map/all_to_all | solution.py:231
  310.1 37.2 %all-to-all-start.3 = ((bf16[1,384,24]{2,0,1:T(2,128)(2,1)}), bf16[1,384,24]{2,0,1:T(2,128)(2,1)S(1)}, u32[]{:S(2)}, u32[]{:S(2)}) async-start(bf16[1,384,24]{2,0,1:T(2,128)(2,1)} %reshape.452), calls=%async_computation.3 | async-start | bytes 393216 | tf_op jit(solution)/shard_map/all_to_all | solution.py:267
  318.5 30.6 %collective-permute-start.5 = (bf16[1,3,3072]{2,0,1:T(2,128)(2,1)S(1)}, bf16[1,3,3072]{2,0,1:T(2,128)(2,1)S(1)}, u32[]{:S(2)}, u32[]{:S(2)}) collective-permute-start(bf16[1,3,3072]{2,0,1:T(2,128)(2,1)S(1)} %get-tuple-element.8), channel_id=1, source_target_pairs={{128,0},{129,1},{130,2},{131,3},{132,4},{133,5},{134,6},{135,7},{1... | collective-permute-start | bytes 55304 | tf_op jit(solution)/shard_map/ppermute | solution.py:316
  347.8 13.1 %collective-permute-start.6 = (bf16[1,3,3072]{2,0,1:T(2,128)(2,1)S(1)}, bf16[1,3,3072]{2,0,1:T(2,128)(2,1)S(1)}, u32[]{:S(2)}, u32[]{:S(2)}) collective-permute-start(bf16[1,3,3072]{2,0,1:T(2,128)(2,1)S(1)} %add_convert_fusion), channel_id=1, source_target_pairs={{0,128},{1,129},{2,130},{3,131},{4,132},{5,133},{6,134},{7,135},{8... | collective-permute-start | bytes 55304 | tf_op jit(solution)/shard_map/ppermute | solution.py:317
